TPU v7x, 256 devices: a whole 4x4x8 slice. The times are simulated.
256 devices in a mesh: gx: 64 (over x, z, core), gy: 4 (over y).
Axes of the slice: x: 4, y: 4, z: 8, core: 2. Of those that a mesh axis runs over, the one named last changes fastest.
Arguments:
- velocity: float32 [2048, 512, 256], P('gx', 'gy'), may hold values from -6 to 6
- threshold_table: float32 [16], replicated, may hold values from 0.05 to 1.5
- band_index: int32 [3, 7], replicated, may hold values from 0 to 15
Outputs:
- updated: float32 [2048, 512, 256], P('gx', 'gy')
All inputs are finite; a program needn't handle non-finite values.
Results may differ from a plain program's by a relative error of at most 0.0003.
Values sent between devices are 32-bit elements; how exact they have to be, the bound alone decides.
A program may use at most 128 MiB of HBM per device.

v0:
```python
import functools

import jax
import jax.numpy as jnp
import numpy as np
from jax import lax
from jax.experimental import pallas as pl
from jax.experimental.pallas import tpu as pltpu
from jax.sharding import PartitionSpec as P

LEVELS = 3
PREC = lax.Precision.HIGH

filt_low = [
    0.23037781330885523,
    0.7148465705525415,
    0.6308807679295904,
    -0.02798376941698385,
    -0.18703481171888114,
    0.030841381835986965,
    0.032883011666982945,
    -0.010597401784997278,
]
filt_high = [(-1.0) ** j * filt_low[7 - j] for j in range(8)]


def split_analysis(length):
    matrix = np.zeros((length + 6, length), np.float32)
    for k in range(length // 2):
        for j in range(8):
            matrix[2 * k + j, k] = filt_low[j]
            matrix[2 * k + j, length // 2 + k] = filt_high[j]
    return matrix


def periodic_analysis(length):
    matrix = np.zeros((length, length), np.float32)
    for k in range(length // 2):
        for j in range(8):
            matrix[(2 * k + j - 3) % length, k] += filt_low[j]
            matrix[(2 * k + j - 3) % length, length // 2 + k] += filt_high[j]
    return matrix


def split_synthesis(length):
    half_len = length // 2
    matrix = np.zeros((2, half_len + 4, length), np.float32)
    for position in range(half_len + 4):
        k = position - 2
        for m in range(length):
            j = m + 3 - 2 * k
            if 0 <= j < 8:
                matrix[0, position, m] = filt_low[j]
                matrix[1, position, m] = filt_high[j]
    return matrix


OFFSETS = ((1, 0), (-1, 0), (0, 1), (0, -1), (1, 1), (1, -1), (-1, 1), (-1, -1))
EXCHANGE_IDS = [0]


def exchange_kernel(size_x, size_y, *refs):
    count = len(OFFSETS)
    sources, targets = refs[:count], refs[count : 2 * count]
    send_sem, recv_sem = refs[2 * count], refs[2 * count + 1]
    me_x = lax.axis_index("gx")
    me_y = lax.axis_index("gy")
    peers = [
        (lax.rem(me_x + np.int32(dx + size_x), np.int32(size_x)), lax.rem(me_y + np.int32(dy + size_y), np.int32(size_y)))
        for dx, dy in OFFSETS
    ]
    barrier = pltpu.get_barrier_semaphore()
    for peer in peers:
        pl.semaphore_signal(barrier, inc=1, device_id=peer, device_id_type=pl.DeviceIdType.MESH)
    pl.semaphore_wait(barrier, count)
    copies = []
    for slot, peer in enumerate(peers):
        copy = pltpu.make_async_remote_copy(
            src_ref=sources[slot],
            dst_ref=targets[slot],
            send_sem=send_sem.at[slot],
            recv_sem=recv_sem.at[slot],
            device_id=peer,
            device_id_type=pl.DeviceIdType.MESH,
        )
        copy.start()
        copies.append(copy)
    for copy in copies:
        copy.wait()


def exchange(pieces):
    cid = EXCHANGE_IDS[0]
    EXCHANGE_IDS[0] += 1
    count = len(OFFSETS)
    return pl.pallas_call(
        functools.partial(exchange_kernel, lax.axis_size("gx"), lax.axis_size("gy")),
        out_shape=[jax.ShapeDtypeStruct(p.shape, p.dtype) for p in pieces],
        in_specs=[pl.BlockSpec(memory_space=pl.ANY)] * count,
        out_specs=[pl.BlockSpec(memory_space=pl.ANY)] * count,
        scratch_shapes=[pltpu.SemaphoreType.DMA((count,)), pltpu.SemaphoreType.DMA((count,))],
        compiler_params=pltpu.CompilerParams(collective_id=cid, has_side_effects=True),
    )(*pieces)


def halo(array, dx, hx, dy, hy):
    size_x, size_y = array.shape[dx], array.shape[dy]
    cut = lax.slice_in_dim
    last_x = cut(array, size_x - hx, size_x, axis=dx)
    first_x = cut(array, 0, hx, axis=dx)
    pieces = [
        last_x,
        first_x,
        cut(array, size_y - hy, size_y, axis=dy),
        cut(array, 0, hy, axis=dy),
        cut(last_x, size_y - hy, size_y, axis=dy),
        cut(last_x, 0, hy, axis=dy),
        cut(first_x, size_y - hy, size_y, axis=dy),
        cut(first_x, 0, hy, axis=dy),
    ]
    before_x, after_x, before_y, after_y, corner_bb, corner_ba, corner_ab, corner_aa = exchange(pieces)
    top = jnp.concatenate([corner_bb, before_x, corner_ba], axis=dy)
    mid = jnp.concatenate([before_y, array, after_y], axis=dy)
    bottom = jnp.concatenate([corner_ab, after_x, corner_aa], axis=dy)
    return jnp.concatenate([top, mid, bottom], axis=dx)


def contract(left, right, dims, batch):
    return lax.dot_general(
        left, right, (dims, batch), precision=PREC, preferred_element_type=jnp.float32
    )


def batched_left(matrix, data):
    spread = jnp.broadcast_to(jnp.asarray(matrix), (data.shape[0],) + matrix.shape)
    return contract(spread, data, ((1,), (1,)), ((0,), (0,)))


def analyse_lead(extended):
    count = extended.shape[0] - 6
    low = 0.0
    high = 0.0
    for j in range(8):
        taken = lax.slice_in_dim(extended, j, j + count - 1, 2, 0)
        low = low + filt_low[j] * taken
        high = high + filt_high[j] * taken
    return jnp.concatenate([low, high], axis=0)


def synthesise_lead(low_ext, high_ext):
    half = low_ext.shape[0] - 4
    even = 0.0
    odd = 0.0
    for j in range(8):
        if j % 2 == 1:
            start = (3 - j) // 2 + 2
        else:
            start = (4 - j) // 2 + 2
        term = filt_low[j] * low_ext[start : start + half] + filt_high[j] * high_ext[start : start + half]
        if j % 2 == 1:
            even = even + term
        else:
            odd = odd + term
    joined = jnp.stack([even, odd], axis=1)
    return joined.reshape((2 * half,) + even.shape[1:])


def analysis_level(approx):
    size_x, size_y, size_z = approx.shape
    extended = halo(approx, 0, 3, 1, 3)
    x_part = analyse_lead(extended)
    y_part = batched_left(split_analysis(size_y), x_part)
    return contract(y_part, jnp.asarray(periodic_analysis(size_z)), ((2,), (0,)), ((), ()))


def shrink_field(coeffs, thr_table, indices):
    size_x, size_y, size_z = coeffs.shape
    matched = indices[:, None] == jnp.arange(thr_table.shape[0], dtype=jnp.int32)[None, :]
    seven = jnp.sum(jnp.where(matched, thr_table[None, :], 0.0), axis=1)
    eight = jnp.concatenate([jnp.zeros((1,), jnp.float32), seven])
    high_x = (jnp.arange(size_x, dtype=jnp.int32) >= size_x // 2).astype(jnp.int32)
    high_y = (jnp.arange(size_y, dtype=jnp.int32) >= size_y // 2).astype(jnp.int32)
    high_z = (jnp.arange(size_z, dtype=jnp.int32) >= size_z // 2).astype(jnp.int32)
    band_ids = 4 * high_x[:, None, None] + 2 * high_y[None, :, None] + high_z[None, None, :]
    thresh = jnp.zeros(coeffs.shape, jnp.float32)
    for band_no in range(1, 8):
        thresh = jnp.where(band_ids == band_no, eight[band_no], thresh)
    return jnp.sign(coeffs) * jnp.maximum(jnp.abs(coeffs) - thresh, 0.0)


def synthesis_level(shrunk, recon):
    size_x, size_y, size_z = shrunk.shape
    full = lax.dynamic_update_slice(shrunk, recon, (0, 0, 0))
    blocked = full.reshape(2, size_x // 2, 2, size_y // 2, size_z)
    extended = halo(blocked, 1, 2, 3, 2)
    hx4 = size_x // 2 + 4
    z_part = contract(extended, jnp.asarray(periodic_analysis(size_z)), ((4,), (1,)), ((), ()))
    z_part = z_part.reshape(2 * hx4, 2, size_y // 2 + 4, size_z)
    matrix = split_synthesis(size_y)
    y_part = batched_left(matrix[0], z_part[:, 0]) + batched_left(matrix[1], z_part[:, 1])
    y_part = y_part.reshape(2, hx4, size_y, size_z)
    return synthesise_lead(y_part[0], y_part[1])


def local(velocity, threshold_table, band_index):
    EXCHANGE_IDS[0] = 0
    approx = velocity
    detail_list = []
    for level_no in range(LEVELS):
        coeffs = analysis_level(approx)
        detail_list.append(shrink_field(coeffs, threshold_table, band_index[level_no]))
        size_x, size_y, size_z = coeffs.shape
        approx = coeffs[: size_x // 2, : size_y // 2, : size_z // 2]
    rebuilt = approx
    for level_no in range(LEVELS - 1, -1, -1):
        rebuilt = synthesis_level(detail_list[level_no], rebuilt)
    return rebuilt


def solution(mesh):
    return jax.shard_map(
        local,
        mesh=mesh,
        in_specs=(P("gx", "gy", None), P(), P()),
        out_specs=P("gx", "gy", None),
        check_vma=False,
    )
```

profile of v0, /device:TPU:8, one launch (start us, length us, event | category | flops | bytes accessed | tf_op | source)
XLA Modules:
  0.0 163.0 jit_solution(17532686782708722199)
XLA Ops:
  0.0 1.4 fusion.117
  1.4 2.1 %fusion.119 = (f32[3,128,256]{2,1,0:T(8,128)}, f32[3,128,256]{2,1,0:T(8,128)}) fusion(f32[32,128,256]{2,1,0:T(8,128)} %param.18), kind=kLoop, calls=%fused_computation.201 | loop fusion | bytes 1572864 | tf_op jit(solution)/shard_map/slice | solution.py:110
  3.5 1.8 %fusion.118 = (f32[32,3,256]{2,1,0:T(4,128)}, f32[32,3,256]{2,1,0:T(4,128)}) fusion(f32[32,128,256]{2,1,0:T(8,128)} %param.18), kind=kLoop, calls=%fused_computation.200 | loop fusion | bytes 393216 | tf_op jit(solution)/shard_map/slice | solution.py:115
  5.3 16.8 %shard_map.172 = (f32[3,128,256]{2,1,0:T(8,128)}, f32[3,128,256]{2,1,0:T(8,128)}, f32[32,3,256]{2,1,0:T(4,128)}, f32[32,3,256]{2,1,0:T(4,128)}, f32[3,3,256]{2,1...) custom-call(f32[3,128,256]{2,1,0:T(8,128)} %get-tuple-element.131.refs_0_, ...), custom_call_target="tpu_custom_call" | custom-call | tf_op jit(solution)/shard_map/pallas_call | solution.py:96
  22.1 3.2 %maximum_maximum_fusion = f32[38,134,256]{2,1,0:T(8,128)S(1)} fusion(f32[3,3,256]{2,1,0:T(4,128)} %get-tuple-element.60, f32[3,128,256]{2,1,0:T(8,128)} %get-tuple-element.59, f32[3,3,256]{2,1,0:T(4,128)} %get-tuple-element.58, f32[32,3,256]{2,1,0:T(4,128)} %get-tuple-element.57, f32[32,128,256]{2,1,0:T(8,128)} %param.18, ...), kind=kLoop, calls=%fused_computation.25 | loop fusion | flops 10428416 | bytes 10428416 | tf_op jit(solution)/shard_map/concatenate | solution.py:125
  25.3 0.7 copy-done
  26.0 0.5 pad_maximum_fusion
  26.5 2.5 %multiply_add_fusion.1 = (f32[16,134,256]{2,1,0:T(8,128)S(1)}, f32[16,134,256]{2,1,0:T(8,128)S(1)}) fusion(f32[38,134,256]{2,1,0:T(8,128)S(1)} %maximum_maximum_fusion, f32[32,134,256]{2,1,0:T(8,128)S(1)} %pad_maximum_fusion), kind=kLoop, calls=%fused_computation.39 | loop fusion | flops 16465920 | bytes 21954560 | tf_op jit(solution)/shard_map/add | solution.py:145
  29.1 3.8 %fusion.18 = f32[32,128,256]{2,1,0:T(8,128)S(1)} fusion(f32[16,134,256]{2,1,0:T(8,128)S(1)} %get-tuple-element.105, f32[16,134,256]{2,1,0:T(8,128)S(1)} %get-tuple-element.104, f32[134,128]{1,0:T(8,128)S(1)} %copy-done.4), kind=kOutput, calls=%fused_computation.28 | convolution fusion | flops 844152832 | bytes 8653824 | tf_op jit(solution)/shard_map/dot_general | solution.py:129
  32.9 0.2 select_reduce_fusion
  33.1 0.7 fusion.131
  33.8 0.1 broadcast_add_fusion
  33.9 10.4 %maximum_multiply_fusion = (f32[32,128,256]{2,1,0:T(8,128)}, f32[32,128,256]{2,1,0:T(8,128)S(1)}) fusion(f32[]{:T(128)} %bitcast.8, f32[]{:T(128)} %bitcast.7, f32[]{:T(128)} %bitcast.6, f32[]{:T(128)} %bitcast.5, f32[]{:T(128)} %bitcast.4, f32[]{:T(128)} %bitcast.3, f32[]{:T(128)} %bitcast.2, s32[256]{0:T(256)S(1)} %compare_convert_fusion, ...), kind=kOutput, calls=%fused_computation.33 | convolution fusion | flops 1631584256 | bytes 12862492 | tf_op jit(solution)/shard_map/dot_general | solution.py:129
  44.2 0.7 fusion.116
  44.9 1.1 fusion.115
  46.1 0.2 copy-done.3
  46.3 0.6 fusion.114
  46.9 10.1 %shard_map.173 = (f32[3,64,128]{2,1,0:T(8,128)}, f32[3,64,128]{2,1,0:T(8,128)}, f32[16,3,128]{2,1,0:T(4,128)}, f32[16,3,128]{2,1,0:T(4,128)}, f32[3,3,128]{2,1,0...) custom-call(f32[3,64,128]{2,1,0:T(8,128)} %get-tuple-element.123.refs_0_, ...), custom_call_target="tpu_custom_call" | custom-call | tf_op jit(solution)/shard_map/pallas_call | solution.py:96
  57.0 1.1 slice.646
  58.1 0.8 pad_maximum_fusion.2
  59.0 1.1 maximum_maximum_fusion.1
  60.1 0.3 multiply_add_fusion.3
  60.4 0.4 fusion.55
  60.8 0.7 fusion.129
  61.6 0.1 broadcast_add_fusion.1
  61.6 5.0 %maximum_multiply_fusion.1 = (f32[16,64,128]{2,1,0:T(8,128)S(1)}, f32[16,64,128]{2,1,0:T(8,128)S(1)}) fusion(f32[]{:T(128)} %bitcast.17, f32[]{:T(128)} %bitcast.16, f32[]{:T(128)} %bitcast.15, f32[]{:T(128)} %bitcast.14, f32[]{:T(128)} %bitcast.13, f32[]{:T(128)} %bitcast.12, f32[]{:T(128)} %bitcast.11, s32[128]{0:T(128)S(1)} %compare_convert_fusion.2, ...), kind=kOutput, calls=%fused_computation.91 | convolution fusion | flops 103284736 | bytes 1643036 | tf_op jit(solution)/shard_map/dot_general | solution.py:129
  66.7 0.6 fusion.125
  67.3 0.6 fusion.124
  67.9 0.6 fusion.123
  68.6 9.5 %shard_map.174 = (f32[3,32,64]{2,1,0:T(8,128)}, f32[3,32,64]{2,1,0:T(8,128)}, f32[8,3,64]{2,1,0:T(4,128)}, f32[8,3,64]{2,1,0:T(4,128)}, f32[3,3,64]{2,1,0:T(4,12...) custom-call(f32[3,32,64]{2,1,0:T(8,128)} %get-tuple-element.151.refs_0_, ...), custom_call_target="tpu_custom_call" | custom-call | tf_op jit(solution)/shard_map/pallas_call | solution.py:96
  78.1 0.8 pad_maximum_fusion.4
  78.9 1.0 maximum_maximum_fusion.2
  79.8 0.1 multiply_add_fusion.5
  79.9 0.2 fusion.90
  80.3 4.6 %maximum_multiply_fusion.2 = (f32[8,32,64]{2,1,0:T(8,128)S(1)}, f32[8,32,64]{2,1,0:T(8,128)S(1)}) fusion(f32[]{:T(128)} %bitcast.26, f32[]{:T(128)} %bitcast.25, f32[]{:T(128)} %bitcast.24, f32[]{:T(128)} %bitcast.23, f32[]{:T(128)} %bitcast.22, f32[]{:T(128)} %bitcast.21, f32[]{:T(128)} %bitcast.20, s32[64]{0:T(128)S(1)} %compare_convert_fusion.1, ...), kind=kOutput, calls=%fused_computation.147 | convolution fusion | flops 6619136 | bytes 214300 | tf_op jit(solution)/shard_map/dot_general | solution.py:129
  84.9 0.8 dynamic_update_slice.9
  85.7 0.7 fusion.128
  86.3 0.6 fusion.126
  86.9 0.6 fusion.127
  87.6 9.7 %shard_map.175 = (f32[2,2,2,16,64]{4,3,2,1,0:T(8,128)}, f32[2,2,2,16,64]{4,3,2,1,0:T(8,128)}, f32[2,4,2,2,64]{4,3,2,1,0:T(2,128)}, f32[2,4,2,2,64]{4,3,2,1,0:T(2...) custom-call(f32[2,2,2,16,64]{4,3,2,1,0:T(8,128)} %get-tuple-element., ...), custom_call_target="tpu_custom_call" | custom-call | tf_op jit(solution)/shard_map/pallas_call | solution.py:96
  97.3 1.3 fusion.60
  98.6 0.4 fusion.89
  99.0 0.4 fusion.33
  99.5 0.1 fusion.103
  99.6 0.8 dynamic_update_slice.10
  100.4 0.7 fusion.122
  101.1 0.6 fusion.121
  101.8 0.6 fusion.120
  102.4 10.5 %shard_map.176 = (f32[2,2,2,32,128]{4,3,2,1,0:T(8,128)}, f32[2,2,2,32,128]{4,3,2,1,0:T(8,128)}, f32[2,8,2,2,128]{4,3,2,1,0:T(2,128)}, f32[2,8,2,2,128]{4,3,2,1,0...) custom-call(f32[2,2,2,32,128]{4,3,2,1,0:T(8,128)} %get-tuple-element, ...), custom_call_target="tpu_custom_call" | custom-call | tf_op jit(solution)/shard_map/pallas_call | solution.py:96
  112.9 1.6 %fusion.35 = f32[2,12,2,36,128]{4,3,2,1,0:T(8,128)S(1)} fusion(f32[128,128,1,1,1]{1,0,4,3,2:T(8,128)S(1)} %copy-done.17, f32[2,2,2,2,128]{4,3,2,1,0:T(2,128)} %get-tuple-element.92, f32[2,2,2,32,128]{4,3,2,1,0:T(8,128)} %get-tuple-element.91, f32[2,2,2,2,128]{4,3,2,1,0:T(2,128)} %get-tuple-element.90, f32[2,8,2,2,128]{4,3,2,1,0:T(2,128)} %get-tuple-element.89, ...), kind=kOutput, calls=%fused_computation.64 | convolution fusion | flops 171638784 | bytes 1835008 | tf_op jit(solution)/shard_map/dot_general | solution.py:129
  114.5 0.8 fusion.59
  115.4 0.8 fusion.32
  116.2 0.3 fusion.85
  116.6 0.8 constant_dynamic-update-slice_fusion
  117.4 2.3 %fusion.113 = (f32[2,2,2,64,256]{4,3,2,1,0:T(8,128)}, f32[2,2,2,64,256]{4,3,2,1,0:T(8,128)}) fusion(f32[2,16,2,64,256]{4,3,2,1,0:T(8,128)} %bitcast.113), kind=kLoop, calls=%fused_computation.195 | loop fusion | bytes 2097152 | tf_op jit(solution)/shard_map/slice | solution.py:110
  119.7 2.0 %fusion.112 = (f32[2,16,2,2,256]{4,3,2,1,0:T(2,128)}, f32[2,16,2,2,256]{4,3,2,1,0:T(2,128)}) fusion(f32[2,16,2,64,256]{4,3,2,1,0:T(8,128)} %bitcast.114), kind=kLoop, calls=%fused_computation.194 | loop fusion | bytes 524288 | tf_op jit(solution)/shard_map/slice | solution.py:115
  121.8 1.6 fusion.111
  123.4 14.8 %shard_map.177 = (f32[2,2,2,64,256]{4,3,2,1,0:T(8,128)}, f32[2,2,2,64,256]{4,3,2,1,0:T(8,128)}, f32[2,16,2,2,256]{4,3,2,1,0:T(2,128)}, f32[2,16,2,2,256]{4,3,2,1...) custom-call(f32[2,2,2,64,256]{4,3,2,1,0:T(8,128)} %get-tuple-element, ...), custom_call_target="tpu_custom_call" | custom-call | tf_op jit(solution)/shard_map/pallas_call | solution.py:96
  138.1 5.3 %fusion = f32[2,20,2,68,256]{4,3,2,1,0:T(8,128)S(1)} fusion(f32[256,256,1,1,1]{1,0,4,3,2:T(8,128)S(1)} %copy-done.15, f32[2,2,2,2,256]{4,3,2,1,0:T(2,128)} %get-tuple-element.100, f32[2,2,2,64,256]{4,3,2,1,0:T(8,128)} %get-tuple-element.99, f32[2,2,2,2,256]{4,3,2,1,0:T(2,128)} %get-tuple-element.98, f32[2,16,2,2,256]{4,3,2,1,0:T(2,128)} %get-tuple-element.97, ...), kind=kOutput, calls=%fused_computation.7 | convolution fusion | flops 2150236160 | bytes 11403264 | tf_op jit(solution)/shard_map/dot_general | solution.py:129
  143.5 4.7 %fusion.22 = f32[40,256,128]{2,1,0:T(8,128)S(1)} fusion(f32[40,2,68,256]{3,2,1,0:T(8,128)S(1)} %bitcast.107, f32[68,128]{1,0:T(8,128)S(1)} %copy-done.5), kind=kOutput, calls=%fused_computation.35 | convolution fusion | flops 534773760 | bytes 8228864 | tf_op jit(solution)/shard_map/dot_general | solution.py:129
  148.2 4.7 %add_bitcast_fusion = f32[40,128,256]{1,2,0:T(8,128)S(1)} fusion(f32[40,256,128]{2,1,0:T(8,128)S(1)} %fusion.22, f32[40,2,68,256]{3,2,1,0:T(8,128)S(1)} %bitcast.108, f32[68,128]{1,0:T(8,128)S(1)} %copy-done.6), kind=kOutput, calls=%fused_computation.26 | convolution fusion | flops 536084480 | bytes 13471744 | tf_op jit(solution)/shard_map/dot_general | solution.py:129
  152.9 2.5 %fusion.31 = (f32[16,1,128,256]{2,3,0,1:T(8,128)S(1)}, f32[16,1,128,256]{2,3,0,1:T(8,128)S(1)}) fusion(f32[40,128,256]{1,2,0:T(8,128)S(1)} %add_bitcast_fusion), kind=kLoop, calls=%fused_computation.50 | loop fusion | flops 15728640 | bytes 25165824 | tf_op jit(solution)/shard_map/stack | solution.py:164
  155.4 2.3 %pad_maximum_fusion.1 = f32[16,2,128,256]{2,3,0,1:T(8,128)} fusion(f32[16,1,128,256]{2,3,0,1:T(8,128)S(1)} %get-tuple-element.107, f32[16,1,128,256]{2,3,0,1:T(8,128)S(1)} %get-tuple-element.106), kind=kLoop, calls=%fused_computation.32 | loop fusion | flops 1048576 | bytes 8388608 | tf_op jit(solution)/shard_map/stack | solution.py:164
  157.6 5.3 %copy.44 = f32[16,2,128,256]{3,2,1,0:T(8,128)} copy(f32[16,2,128,256]{2,3,0,1:T(8,128)} %pad_maximum_fusion.1) | data formatting | bytes 8388608 | tf_op jit(solution)/shard_map/stack | solution.py:164
  (57 shorter events, 0.4 us)
Async XLA Ops:
  22.1 3.9 %copy-start = (f32[32,128,256]{2,1,0:T(8,128)S(1)}, f32[32,128,256]{2,1,0:T(8,128)}, u32[]{:S(2)}) copy-start(f32[32,128,256]{2,1,0:T(8,128)} %param.18) | copy-start | bytes 12582916
  22.1 3.9 %copy-start.1 = (f32[32,3,256]{2,1,0:T(4,128)S(1)}, f32[32,3,256]{2,1,0:T(4,128)}, u32[]{:S(2)}) copy-start(f32[32,3,256]{2,1,0:T(4,128)} %get-tuple-element.56) | copy-start | bytes 294916
  22.1 3.9 %copy-start.2 = (f32[32,3,256]{2,1,0:T(4,128)S(1)}, f32[32,3,256]{2,1,0:T(4,128)}, u32[]{:S(2)}) copy-start(f32[32,3,256]{2,1,0:T(4,128)} %get-tuple-element.57) | copy-start | bytes 294916
  26.5 2.5 %copy-start.4 = (f32[134,128]{1,0:T(8,128)S(1)}, f32[134,128]{1,0:T(8,128)}, u32[]{:S(2)}) copy-start(f32[134,128]{1,0:T(8,128)} %constant.64.clone) | copy-start | bytes 205828
  29.0 3.8 %copy-start.13 = (s32[3,7]{1,0:T(4,128)S(1)}, s32[3,7]{1,0:T(4,128)}, u32[]{:S(2)}) copy-start(s32[3,7]{1,0:T(4,128)} %param.20) | copy-start | bytes 256
  29.0 3.8 %copy-start.14 = (f32[16]{0:T(128)S(1)}, f32[16]{0:T(128)}, u32[]{:S(2)}) copy-start(f32[16]{0:T(128)} %param.19) | copy-start | bytes 196
  29.1 4.8 %copy-start.16 = (f32[256,256,1]{1,0,2:T(8,128)S(1)}, f32[256,256,1]{1,0,2:T(8,128)}, u32[]{:S(2)}) copy-start(f32[256,256,1]{1,0,2:T(8,128)} %constant.19) | copy-start | bytes 786436
  44.2 2.0 %copy-start.3 = (f32[32,128,256]{2,1,0:T(8,128)}, f32[32,128,256]{2,1,0:T(8,128)S(1)}, u32[]{:S(2)}) copy-start(f32[32,128,256]{2,1,0:T(8,128)S(1)} %get-tuple-element.189) | copy-start | bytes 12582916
  58.1 2.3 %copy-start.7 = (f32[70,64]{0,1:T(8,128)S(1)}, f32[70,64]{0,1:T(8,128)}, u32[]{:S(2)}) copy-start(f32[70,64]{0,1:T(8,128)} %constant.66.clone) | copy-start | bytes 53764
  59.0 2.7 %copy-start.18 = (f32[128,128,1]{1,0,2:T(8,128)S(1)}, f32[128,128,1]{1,0,2:T(8,128)}, u32[]{:S(2)}) copy-start(f32[128,128,1]{1,0,2:T(8,128)} %constant.20) | copy-start | bytes 196612
  61.5 18.4 %copy-start.10 = (f32[38,32]{0,1:T(8,128)S(1)}, f32[38,32]{0,1:T(8,128)}, u32[]{:S(2)}) copy-start(f32[38,32]{0,1:T(8,128)} %constant.68.clone) | copy-start | bytes 14596
  61.6 18.6 %copy-start.20 = (f32[64,64,1]{1,0,2:T(8,128)S(1)}, f32[64,64,1]{1,0,2:T(8,128)}, u32[]{:S(2)}) copy-start(f32[64,64,1]{1,0,2:T(8,128)} %constant.21) | copy-start | bytes 49156
  66.7 30.6 %copy-start.19 = (f32[64,64,1,1,1]{1,0,4,3,2:T(8,128)S(1)}, f32[64,64,1,1,1]{1,0,4,3,2:T(8,128)}, u32[]{:S(2)}) copy-start(f32[64,64,1,1,1]{1,0,4,3,2:T(8,128)} %constant.22) | copy-start | bytes 49156
  67.3 31.3 %copy-start.12 = (f32[20,32]{1,0:T(8,128)S(1)}, f32[20,32]{1,0:T(8,128)}, u32[]{:S(2)}) copy-start(f32[20,32]{1,0:T(8,128)} %constant.70.clone) | copy-start | bytes 7684
  78.1 21.0 %copy-start.11 = (f32[20,32]{1,0:T(8,128)S(1)}, f32[20,32]{1,0:T(8,128)}, u32[]{:S(2)}) copy-start(f32[20,32]{1,0:T(8,128)} %constant.71.clone) | copy-start | bytes 7684
  86.3 26.5 %copy-start.17 = (f32[128,128,1,1,1]{1,0,4,3,2:T(8,128)S(1)}, f32[128,128,1,1,1]{1,0,4,3,2:T(8,128)}, u32[]{:S(2)}) copy-start(f32[128,128,1,1,1]{1,0,4,3,2:T(8,128)} %constant.23) | copy-start | bytes 196612
  99.5 15.0 %copy-start.9 = (f32[36,64]{1,0:T(8,128)S(1)}, f32[36,64]{1,0:T(8,128)}, u32[]{:S(2)}) copy-start(f32[36,64]{1,0:T(8,128)} %constant.72.clone) | copy-start | bytes 27652
  101.1 14.2 %copy-start.8 = (f32[36,64]{1,0:T(8,128)S(1)}, f32[36,64]{1,0:T(8,128)}, u32[]{:S(2)}) copy-start(f32[36,64]{1,0:T(8,128)} %constant.73.clone) | copy-start | bytes 27652
  116.5 21.6 %copy-start.15 = (f32[256,256,1,1,1]{1,0,4,3,2:T(8,128)S(1)}, f32[256,256,1,1,1]{1,0,4,3,2:T(8,128)}, u32[]{:S(2)}) copy-start(f32[256,256,1,1,1]{1,0,4,3,2:T(8,128)} %constant.24) | copy-start | bytes 786436
  138.1 5.3 %copy-start.5 = (f32[68,128]{1,0:T(8,128)S(1)}, f32[68,128]{1,0:T(8,128)}, u32[]{:S(2)}) copy-start(f32[68,128]{1,0:T(8,128)} %constant.75.clone) | copy-start | bytes 104452
  143.4 4.7 %copy-start.6 = (f32[68,128]{1,0:T(8,128)S(1)}, f32[68,128]{1,0:T(8,128)}, u32[]{:S(2)}) copy-start(f32[68,128]{1,0:T(8,128)} %constant.74.clone) | copy-start | bytes 104452
where the time goes:
time: 164 us; the launch traced here: 163 us
  Pallas kernels  71.3 us (43%)
  matrix products  44.4 us (27%)
  local copies, waits for them, and re-layouts  30.7 us (19%)
  other arithmetic  15.9 us (10%)
    pallas_call x6, Pallas kernels, exchange(): pl.pallas_call(functools.partial(exchange_kernel, lax.axis_size('gx'), la...  71.3 us
    dot_general x15, matrix products, contract(): lax.dot_general(left, right, (dims, batch), precision=PREC, preferred_ele...  44.4 us
    slice x6, local copies, waits for them, and re-layouts, halo(): first_x = cut(array, 0, hx, axis=dx)  7.11 us
    slice x6, local copies, waits for them, and re-layouts, halo(): cut(array, 0, hy, axis=dy)  6.81 us
    slice x6, local copies, waits for them, and re-layouts, halo(): cut(first_x, 0, hy, axis=dy)  5.48 us
    another operation x3, local copies, waits for them, and re-layouts, synthesise_lead(): joined = jnp.stack([even, odd], axis=1)  5.39 us
    concatenate x3, other arithmetic, halo(): return jnp.concatenate([top, mid, bottom], axis=dx)  5.27 us
    another operation x6, other arithmetic, synthesise_lead(): joined = jnp.stack([even, odd], axis=1)  5.17 us

commit v1 on v0

--- a/solution.py
+++ b/solution.py
@@ -165,11 +165,10 @@
     return joined.reshape((2 * half,) + even.shape[1:])
 
 
-def analysis_level(approx):
-    size_x, size_y, size_z = approx.shape
-    extended = halo(approx, 0, 3, 1, 3)
+def analysis_ext(extended):
     x_part = analyse_lead(extended)
-    y_part = batched_left(split_analysis(size_y), x_part)
+    y_part = batched_left(split_analysis(x_part.shape[1] - 6), x_part)
+    size_z = y_part.shape[2]
     return contract(y_part, jnp.asarray(periodic_analysis(size_z)), ((2,), (0,)), ((), ()))
 
 
@@ -188,33 +187,44 @@
     return jnp.sign(coeffs) * jnp.maximum(jnp.abs(coeffs) - thresh, 0.0)
 
 
-def synthesis_level(shrunk, recon):
-    size_x, size_y, size_z = shrunk.shape
-    full = lax.dynamic_update_slice(shrunk, recon, (0, 0, 0))
-    blocked = full.reshape(2, size_x // 2, 2, size_y // 2, size_z)
-    extended = halo(blocked, 1, 2, 3, 2)
-    hx4 = size_x // 2 + 4
+def synthesis_ext(extended):
+    two, hx4, _, hy4, size_z = extended.shape
     z_part = contract(extended, jnp.asarray(periodic_analysis(size_z)), ((4,), (1,)), ((), ()))
-    z_part = z_part.reshape(2 * hx4, 2, size_y // 2 + 4, size_z)
+    z_part = z_part.reshape(2 * hx4, 2, hy4, size_z)
+    size_y = 2 * (hy4 - 4)
     matrix = split_synthesis(size_y)
     y_part = batched_left(matrix[0], z_part[:, 0]) + batched_left(matrix[1], z_part[:, 1])
     y_part = y_part.reshape(2, hx4, size_y, size_z)
     return synthesise_lead(y_part[0], y_part[1])
 
 
+def blocked(cube):
+    size_x, size_y, size_z = cube.shape
+    return cube.reshape(2, size_x // 2, 2, size_y // 2, size_z)
+
+
+def low_corner(cube):
+    size_x, size_y, size_z = cube.shape
+    return cube[: size_x // 2, : size_y // 2, : size_z // 2]
+
+
 def local(velocity, threshold_table, band_index):
     EXCHANGE_IDS[0] = 0
-    approx = velocity
-    detail_list = []
-    for level_no in range(LEVELS):
-        coeffs = analysis_level(approx)
-        detail_list.append(shrink_field(coeffs, threshold_table, band_index[level_no]))
-        size_x, size_y, size_z = coeffs.shape
-        approx = coeffs[: size_x // 2, : size_y // 2, : size_z // 2]
-    rebuilt = approx
-    for level_no in range(LEVELS - 1, -1, -1):
-        rebuilt = synthesis_level(detail_list[level_no], rebuilt)
-    return rebuilt
+    cube0 = analysis_ext(halo(velocity, 0, 3, 1, 3))
+    shrunk0 = shrink_field(cube0, threshold_table, band_index[0])
+    cube1 = analysis_ext(halo(low_corner(cube0), 0, 9, 1, 9))
+    shrunk1 = blocked(shrink_field(cube1, threshold_table, band_index[1]))
+    cube2 = analysis_ext(low_corner(cube1))
+    shrunk2 = shrink_field(cube2, threshold_table, band_index[2])
+    full2 = lax.dynamic_update_slice(shrunk2, low_corner(cube2), (0, 0, 0))
+    recon2 = synthesis_ext(halo(blocked(full2), 1, 3, 3, 3))
+    hx, hy = shrunk1.shape[1], shrunk1.shape[3]
+    full1 = shrunk1[:, 1 : hx - 1, :, 1 : hy - 1, :]
+    half_z = full1.shape[4] // 2
+    full1 = full1.at[0, :, 0, :, :half_z].set(recon2)
+    recon1 = synthesis_ext(full1)
+    full0 = lax.dynamic_update_slice(shrunk0, recon1, (0, 0, 0))
+    return synthesis_ext(halo(blocked(full0), 1, 2, 3, 2))
 
 
 def solution(mesh):

time: 164 us -> 143 us (0.87)
  Pallas kernels: 71.3 us -> 54.8 us
  local copies, waits for them, and re-layouts: 30.7 us -> 27.5 us
  other arithmetic: 15.9 us -> 14.1 us
    pallas_call x6 -> x4, Pallas kernels: 71.3 us -> 54.8 us  [exchange(): pl.pallas_call(functools.partial(exchange_kernel, lax.axis_size('gx'), la...]
    slice x6 -> x4, local copies, waits for them, and re-layouts: 6.81 us -> 5.17 us  [halo(): cut(array, 0, hy, axis=dy)]
    slice x6 -> x4, local copies, waits for them, and re-layouts: 7.11 us -> 6.07 us  [halo(): first_x = cut(array, 0, hx, axis=dx)]
    concatenate x3 -> x2, other arithmetic: 5.27 us -> 4.58 us  [halo(): return jnp.concatenate([top, mid, bottom], axis=dx)]
    slice x6 -> x4, local copies, waits for them, and re-layouts: 5.48 us -> 4.88 us  [halo(): cut(first_x, 0, hy, axis=dy)]
where the time goes in v1:
time: 143 us; the launch traced here: 142 us
  Pallas kernels  54.8 us (38%)
  matrix products  45 us (31%)
  local copies, waits for them, and re-layouts  27.5 us (19%)
  other arithmetic  14.1 us (10%)
    pallas_call x4, Pallas kernels, exchange(): pl.pallas_call(functools.partial(exchange_kernel, lax.axis_size('gx'), la...  54.8 us
    dot_general x15, matrix products, contract(): lax.dot_general(left, right, (dims, batch), precision=PREC, preferred_ele...  45 us
    slice x4, local copies, waits for them, and re-layouts, halo(): first_x = cut(array, 0, hx, axis=dx)  6.07 us
    another operation x3, local copies, waits for them, and re-layouts, synthesise_lead(): joined = jnp.stack([even, odd], axis=1)  5.4 us
    another operation x6, other arithmetic, synthesise_lead(): joined = jnp.stack([even, odd], axis=1)  5.25 us
    slice x4, local copies, waits for them, and re-layouts, halo(): cut(array, 0, hy, axis=dy)  5.17 us
    slice x4, local copies, waits for them, and re-layouts, halo(): cut(first_x, 0, hy, axis=dy)  4.88 us
    concatenate x2, other arithmetic, halo(): return jnp.concatenate([top, mid, bottom], axis=dx)  4.58 us

profile of v1, /device:TPU:8, one launch (start us, length us, event | category | flops | bytes accessed | tf_op | source)
XLA Modules:
  0.0 141.9 jit_solution(9066146852145794274)
XLA Ops:
  0.0 1.4 %fusion.98 = (f32[3,3,256]{2,1,0:T(4,128)}, f32[3,3,256]{2,1,0:T(4,128)}, f32[3,3,256]{2,1,0:T(4,128)}, f32[3,3,256]{2,1,0:T(4,128)}) fusion(f32[32,128,256]{2,1,0:T(8,128)} %param.20), kind=kLoop, calls=%fused_computation.177 | loop fusion | bytes 73728 | tf_op jit(solution)/shard_map/slice | solution.py:119
  1.4 2.1 %fusion.100 = (f32[3,128,256]{2,1,0:T(8,128)}, f32[3,128,256]{2,1,0:T(8,128)}) fusion(f32[32,128,256]{2,1,0:T(8,128)} %param.20), kind=kLoop, calls=%fused_computation.179 | loop fusion | bytes 1572864 | tf_op jit(solution)/shard_map/slice | solution.py:110
  3.5 1.8 %fusion.99 = (f32[32,3,256]{2,1,0:T(4,128)}, f32[32,3,256]{2,1,0:T(4,128)}) fusion(f32[32,128,256]{2,1,0:T(8,128)} %param.20), kind=kLoop, calls=%fused_computation.178 | loop fusion | bytes 393216 | tf_op jit(solution)/shard_map/slice | solution.py:115
  5.3 16.8 %shard_map.172 = (f32[3,128,256]{2,1,0:T(8,128)}, f32[3,128,256]{2,1,0:T(8,128)}, f32[32,3,256]{2,1,0:T(4,128)}, f32[32,3,256]{2,1,0:T(4,128)}, f32[3,3,256]{2,1...) custom-call(f32[3,128,256]{2,1,0:T(8,128)} %get-tuple-element.111.refs_0_, ...), custom_call_target="tpu_custom_call" | custom-call | tf_op jit(solution)/shard_map/pallas_call | solution.py:96
  22.1 3.2 %maximum_maximum_fusion = f32[38,134,256]{2,1,0:T(8,128)S(1)} fusion(f32[3,3,256]{2,1,0:T(4,128)} %get-tuple-element.56, f32[3,128,256]{2,1,0:T(8,128)} %get-tuple-element.55, f32[3,3,256]{2,1,0:T(4,128)} %get-tuple-element.54, f32[32,3,256]{2,1,0:T(4,128)} %get-tuple-element.53, f32[32,128,256]{2,1,0:T(8,128)} %param.20, ...), kind=kLoop, calls=%fused_computation.25 | loop fusion | flops 10428416 | bytes 10428416 | tf_op jit(solution)/shard_map/concatenate | solution.py:125
  25.3 0.7 copy-done
  26.0 0.0 copy-done.3
  26.0 0.5 pad_maximum_fusion
  26.5 0.0 copy-start.4
  26.5 2.5 %multiply_add_fusion.1 = (f32[16,134,256]{2,1,0:T(8,128)S(1)}, f32[16,134,256]{2,1,0:T(8,128)S(1)}) fusion(f32[38,134,256]{2,1,0:T(8,128)S(1)} %maximum_maximum_fusion, f32[32,134,256]{2,1,0:T(8,128)S(1)} %pad_maximum_fusion), kind=kLoop, calls=%fused_computation.46 | loop fusion | flops 16465920 | bytes 21954560 | tf_op jit(solution)/shard_map/add | solution.py:145
  29.1 3.8 %fusion.18 = f32[32,128,256]{2,1,0:T(8,128)S(1)} fusion(f32[16,134,256]{2,1,0:T(8,128)S(1)} %get-tuple-element.85, f32[16,134,256]{2,1,0:T(8,128)S(1)} %get-tuple-element.84, f32[134,128]{1,0:T(8,128)S(1)} %copy-done.4), kind=kOutput, calls=%fused_computation.28 | convolution fusion | flops 844152832 | bytes 8653824 | tf_op jit(solution)/shard_map/dot_general | solution.py:129
  32.9 0.2 select_reduce_fusion
  33.1 0.7 fusion.106
  33.8 0.1 broadcast_add_fusion.1
  33.9 10.3 %maximum_multiply_fusion = (f32[32,128,256]{2,1,0:T(8,128)}, f32[32,128,256]{2,1,0:T(8,128)S(1)}) fusion(f32[]{:T(128)} %bitcast.8, f32[]{:T(128)} %bitcast.7, f32[]{:T(128)} %bitcast.6, f32[]{:T(128)} %bitcast.5, f32[]{:T(128)} %bitcast.4, f32[]{:T(128)} %bitcast.3, f32[]{:T(128)} %bitcast.2, s32[256]{0:T(256)S(1)} %compare_convert_fusion.1, ...), kind=kOutput, calls=%fused_computation.33 | convolution fusion | flops 1631584256 | bytes 12862492 | tf_op jit(solution)/shard_map/dot_general | solution.py:129
  44.2 1.0 fusion.97
  45.2 1.2 fusion.95
  46.4 0.0 copy-done.1
  46.4 0.7 fusion.96
  47.2 12.6 %shard_map.173 = (f32[9,64,128]{2,1,0:T(8,128)}, f32[9,64,128]{2,1,0:T(8,128)}, f32[16,9,128]{2,1,0:T(8,128)}, f32[16,9,128]{2,1,0:T(8,128)}, f32[9,9,128]{2,1,0...) custom-call(f32[9,64,128]{2,1,0:T(8,128)} %get-tuple-element.103.refs_0_, ...), custom_call_target="tpu_custom_call" | custom-call | tf_op jit(solution)/shard_map/pallas_call | solution.py:96
  59.8 1.1 slice.609
  60.9 1.4 maximum_maximum_fusion.1
  62.3 0.0 copy-start.6
  62.3 0.7 multiply_add_fusion.3
  63.0 0.0 copy-start.18
  63.0 0.1 copy-done.6
  63.1 0.7 fusion.33
  63.8 0.7 fusion.104
  64.5 0.1 broadcast_add_fusion
  64.6 0.0 copy-start.20
  64.6 6.0 %maximum_multiply_fusion.1 = (f32[28,76,128]{2,1,0:T(8,128)S(1)}, f32[28,76,128]{2,1,0:T(8,128)S(1)}) fusion(f32[]{:T(128)} %bitcast.17, f32[]{:T(128)} %bitcast.16, f32[]{:T(128)} %bitcast.15, f32[]{:T(128)} %bitcast.14, f32[]{:T(128)} %bitcast.13, f32[]{:T(128)} %bitcast.12, f32[]{:T(128)} %bitcast.11, s32[128]{0:T(128)S(1)} %compare_convert_fusion.2, ...), kind=kOutput, calls=%fused_computation.68 | convolution fusion | flops 214638592 | bytes 3343196 | tf_op jit(solution)/shard_map/dot_general | solution.py:129
  70.6 0.0 copy-start.19
  70.7 0.1 multiply_add_fusion.5
  70.8 0.2 fusion.72
  71.0 0.1 broadcast_add_fusion.2
  71.1 4.5 %maximum_multiply_fusion.2 = (f32[8,32,64]{2,1,0:T(8,128)S(1)}, f32[8,32,64]{2,1,0:T(8,128)S(1)}) fusion(f32[]{:T(128)} %bitcast.26, f32[]{:T(128)} %bitcast.25, f32[]{:T(128)} %bitcast.24, f32[]{:T(128)} %bitcast.23, f32[]{:T(128)} %bitcast.22, f32[]{:T(128)} %bitcast.21, f32[]{:T(128)} %bitcast.20, s32[64]{0:T(128)S(1)} %compare_convert_fusion, ...), kind=kOutput, calls=%fused_computation.126 | convolution fusion | flops 6619136 | bytes 214300 | tf_op jit(solution)/shard_map/dot_general | solution.py:129
  75.7 0.8 dynamic_update_slice.6
  76.5 0.7 fusion.103
  77.2 0.7 fusion.101
  77.8 0.6 fusion.102
  78.5 10.5 %shard_map.174 = (f32[2,3,2,16,64]{4,3,2,1,0:T(8,128)}, f32[2,3,2,16,64]{4,3,2,1,0:T(8,128)}, f32[2,4,2,3,64]{4,3,2,1,0:T(4,128)}, f32[2,4,2,3,64]{4,3,2,1,0:T(4...) custom-call(f32[2,3,2,16,64]{4,3,2,1,0:T(8,128)} %get-tuple-element., ...), custom_call_target="tpu_custom_call" | custom-call | tf_op jit(solution)/shard_map/pallas_call | solution.py:96
  89.0 1.4 %fusion.43 = f32[2,10,2,22,64]{4,3,2,1,0:T(8,128)S(1)} fusion(f32[64,64,1,1,1]{1,0,4,3,2:T(8,128)S(1)} %copy-done.19, f32[2,3,2,3,64]{4,3,2,1,0:T(4,128)} %get-tuple-element.72, f32[2,3,2,16,64]{4,3,2,1,0:T(8,128)} %get-tuple-element.71, f32[2,3,2,3,64]{4,3,2,1,0:T(4,128)} %get-tuple-element.70, f32[2,4,2,3,64]{4,3,2,1,0:T(4,128)} %get-tuple-element.69, ...), kind=kOutput, calls=%fused_computation.79 | convolution fusion | flops 22077440 | bytes 466944 | tf_op jit(solution)/shard_map/dot_general | solution.py:129
  90.5 0.5 fusion.69
  91.0 0.5 fusion.37
  91.6 0.1 fusion.83
  91.8 0.1 reshape.243
  91.9 0.1 slice.610
  92.0 0.4 scatter.4
  92.4 0.3 copy-done.5
  92.7 0.6 fusion.107
  93.3 0.8 fusion.42
  94.1 0.8 fusion.32
  95.0 0.3 fusion.68
  95.4 0.8 constant_dynamic-update-slice_fusion
  96.2 2.3 %fusion.94 = (f32[2,2,2,64,256]{4,3,2,1,0:T(8,128)}, f32[2,2,2,64,256]{4,3,2,1,0:T(8,128)}) fusion(f32[2,16,2,64,256]{4,3,2,1,0:T(8,128)} %bitcast.121), kind=kLoop, calls=%fused_computation.173 | loop fusion | bytes 2097152 | tf_op jit(solution)/shard_map/slice | solution.py:110
  98.5 2.0 %fusion.93 = (f32[2,16,2,2,256]{4,3,2,1,0:T(2,128)}, f32[2,16,2,2,256]{4,3,2,1,0:T(2,128)}) fusion(f32[2,16,2,64,256]{4,3,2,1,0:T(8,128)} %bitcast.122), kind=kLoop, calls=%fused_computation.172 | loop fusion | bytes 524288 | tf_op jit(solution)/shard_map/slice | solution.py:115
  100.6 1.6 %fusion.92 = (f32[2,2,2,2,256]{4,3,2,1,0:T(2,128)}, f32[2,2,2,2,256]{4,3,2,1,0:T(2,128)}, f32[2,2,2,2,256]{4,3,2,1,0:T(2,128)}, f32[2,2,2,2,256]{4,3,2,1,0:T(2,128)}) fusion(f32[2,16,2,64,256]{4,3,2,1,0:T(8,128)} %bitcast.123), kind=kLoop, calls=%fused_computation.171 | loop fusion | bytes 131072 | tf_op jit(solution)/shard_map/slice | solution.py:119
  102.1 14.9 %shard_map.175 = (f32[2,2,2,64,256]{4,3,2,1,0:T(8,128)}, f32[2,2,2,64,256]{4,3,2,1,0:T(8,128)}, f32[2,16,2,2,256]{4,3,2,1,0:T(2,128)}, f32[2,16,2,2,256]{4,3,2,1...) custom-call(f32[2,2,2,64,256]{4,3,2,1,0:T(8,128)} %get-tuple-element, ...), custom_call_target="tpu_custom_call" | custom-call | tf_op jit(solution)/shard_map/pallas_call | solution.py:96
  117.0 5.3 %fusion = f32[2,20,2,68,256]{4,3,2,1,0:T(8,128)S(1)} fusion(f32[256,256,1,1,1]{1,0,4,3,2:T(8,128)S(1)} %copy-done.16, f32[2,2,2,2,256]{4,3,2,1,0:T(2,128)} %get-tuple-element.80, f32[2,2,2,64,256]{4,3,2,1,0:T(8,128)} %get-tuple-element.79, f32[2,2,2,2,256]{4,3,2,1,0:T(2,128)} %get-tuple-element.78, f32[2,16,2,2,256]{4,3,2,1,0:T(2,128)} %get-tuple-element.77, ...), kind=kOutput, calls=%fused_computation.7 | convolution fusion | flops 2150236160 | bytes 11403264 | tf_op jit(solution)/shard_map/dot_general | solution.py:129
  122.3 4.7 %fusion.22 = f32[40,256,128]{2,1,0:T(8,128)S(1)} fusion(f32[40,2,68,256]{3,2,1,0:T(8,128)S(1)} %bitcast.109, f32[68,128]{1,0:T(8,128)S(1)} %copy-done.7), kind=kOutput, calls=%fused_computation.42 | convolution fusion | flops 534773760 | bytes 8228864 | tf_op jit(solution)/shard_map/dot_general | solution.py:129
  127.0 4.7 %add_bitcast_fusion = f32[40,128,256]{1,2,0:T(8,128)S(1)} fusion(f32[40,256,128]{2,1,0:T(8,128)S(1)} %fusion.22, f32[40,2,68,256]{3,2,1,0:T(8,128)S(1)} %bitcast.110, f32[68,128]{1,0:T(8,128)S(1)} %copy-done.8), kind=kOutput, calls=%fused_computation.26 | convolution fusion | flops 536084480 | bytes 13471744 | tf_op jit(solution)/shard_map/dot_general | solution.py:129
  131.8 2.5 %fusion.31 = (f32[16,1,128,256]{2,3,0,1:T(8,128)S(1)}, f32[16,1,128,256]{2,3,0,1:T(8,128)S(1)}) fusion(f32[40,128,256]{1,2,0:T(8,128)S(1)} %add_bitcast_fusion), kind=kLoop, calls=%fused_computation.57 | loop fusion | flops 15728640 | bytes 25165824 | tf_op jit(solution)/shard_map/stack | solution.py:164
  134.3 2.3 %pad_maximum_fusion.1 = f32[16,2,128,256]{2,3,0,1:T(8,128)} fusion(f32[16,1,128,256]{2,3,0,1:T(8,128)S(1)} %get-tuple-element.87, f32[16,1,128,256]{2,3,0,1:T(8,128)S(1)} %get-tuple-element.86), kind=kLoop, calls=%fused_computation.32 | loop fusion | flops 1048576 | bytes 8388608 | tf_op jit(solution)/shard_map/stack | solution.py:164
  136.5 5.3 %copy.45 = f32[16,2,128,256]{3,2,1,0:T(8,128)} copy(f32[16,2,128,256]{2,3,0,1:T(8,128)} %pad_maximum_fusion.1) | data formatting | bytes 8388608 | tf_op jit(solution)/shard_map/stack | solution.py:164
  (48 shorter events, 0.3 us)
Async XLA Ops:
  22.1 3.9 %copy-start = (f32[32,128,256]{2,1,0:T(8,128)S(1)}, f32[32,128,256]{2,1,0:T(8,128)}, u32[]{:S(2)}) copy-start(f32[32,128,256]{2,1,0:T(8,128)} %param.20) | copy-start | bytes 12582916
  22.1 3.9 %copy-start.2 = (f32[32,3,256]{2,1,0:T(4,128)S(1)}, f32[32,3,256]{2,1,0:T(4,128)}, u32[]{:S(2)}) copy-start(f32[32,3,256]{2,1,0:T(4,128)} %get-tuple-element.52) | copy-start | bytes 294916
  22.1 3.9 %copy-start.3 = (f32[32,3,256]{2,1,0:T(4,128)S(1)}, f32[32,3,256]{2,1,0:T(4,128)}, u32[]{:S(2)}) copy-start(f32[32,3,256]{2,1,0:T(4,128)} %get-tuple-element.53) | copy-start | bytes 294916
  26.5 2.5 %copy-start.4 = (f32[134,128]{1,0:T(8,128)S(1)}, f32[134,128]{1,0:T(8,128)}, u32[]{:S(2)}) copy-start(f32[134,128]{1,0:T(8,128)} %constant.74.clone) | copy-start | bytes 205828
  29.0 3.8 %copy-start.14 = (s32[3,7]{1,0:T(4,128)S(1)}, s32[3,7]{1,0:T(4,128)}, u32[]{:S(2)}) copy-start(s32[3,7]{1,0:T(4,128)} %param.22) | copy-start | bytes 256
  29.0 3.8 %copy-start.15 = (f32[16]{0:T(128)S(1)}, f32[16]{0:T(128)}, u32[]{:S(2)}) copy-start(f32[16]{0:T(128)} %param.21) | copy-start | bytes 196
  29.1 4.8 %copy-start.17 = (f32[256,256,1]{1,0,2:T(8,128)S(1)}, f32[256,256,1]{1,0,2:T(8,128)}, u32[]{:S(2)}) copy-start(f32[256,256,1]{1,0,2:T(8,128)} %constant.87) | copy-start | bytes 786436
  44.2 2.2 %copy-start.1 = (f32[32,128,256]{2,1,0:T(8,128)}, f32[32,128,256]{2,1,0:T(8,128)S(1)}, u32[]{:S(2)}) copy-start(f32[32,128,256]{2,1,0:T(8,128)S(1)} %get-tuple-element.153) | copy-start | bytes 12582916
  62.3 0.8 copy-start.6
  63.0 1.6 %copy-start.18 = (f32[128,128,1]{1,0,2:T(8,128)S(1)}, f32[128,128,1]{1,0,2:T(8,128)}, u32[]{:S(2)}) copy-start(f32[128,128,1]{1,0,2:T(8,128)} %constant.88) | copy-start | bytes 196612
  64.6 6.2 %copy-start.11 = (f32[38,32]{0,1:T(8,128)S(1)}, f32[38,32]{0,1:T(8,128)}, u32[]{:S(2)}) copy-start(f32[38,32]{0,1:T(8,128)} %constant.78.clone) | copy-start | bytes 14596
  64.6 6.5 %copy-start.20 = (f32[64,64,1]{1,0,2:T(8,128)S(1)}, f32[64,64,1]{1,0,2:T(8,128)}, u32[]{:S(2)}) copy-start(f32[64,64,1]{1,0,2:T(8,128)} %constant.89) | copy-start | bytes 49156
  70.6 18.4 %copy-start.19 = (f32[64,64,1,1,1]{1,0,4,3,2:T(8,128)S(1)}, f32[64,64,1,1,1]{1,0,4,3,2:T(8,128)}, u32[]{:S(2)}) copy-start(f32[64,64,1,1,1]{1,0,4,3,2:T(8,128)} %constant.90) | copy-start | bytes 49156
  70.8 19.7 %copy-start.13 = (f32[22,36]{1,0:T(8,128)S(1)}, f32[22,36]{1,0:T(8,128)}, u32[]{:S(2)}) copy-start(f32[22,36]{1,0:T(8,128)} %constant.80.clone) | copy-start | bytes 9508
  71.1 19.9 %copy-start.12 = (f32[22,36]{1,0:T(8,128)S(1)}, f32[22,36]{1,0:T(8,128)}, u32[]{:S(2)}) copy-start(f32[22,36]{1,0:T(8,128)} %constant.81.clone) | copy-start | bytes 9508
  91.9 0.8 copy-start.5
  91.9 1.4 copy-start.10
  92.0 2.2 %copy-start.9 = (f32[36,64]{1,0:T(8,128)S(1)}, f32[36,64]{1,0:T(8,128)}, u32[]{:S(2)}) copy-start(f32[36,64]{1,0:T(8,128)} %constant.83.clone) | copy-start | bytes 27652
  96.2 20.8 %copy-start.16 = (f32[256,256,1,1,1]{1,0,4,3,2:T(8,128)S(1)}, f32[256,256,1,1,1]{1,0,4,3,2:T(8,128)}, u32[]{:S(2)}) copy-start(f32[256,256,1,1,1]{1,0,4,3,2:T(8,128)} %constant.92) | copy-start | bytes 786436
  117.0 5.3 %copy-start.7 = (f32[68,128]{1,0:T(8,128)S(1)}, f32[68,128]{1,0:T(8,128)}, u32[]{:S(2)}) copy-start(f32[68,128]{1,0:T(8,128)} %constant.85.clone) | copy-start | bytes 104452
  122.3 4.7 %copy-start.8 = (f32[68,128]{1,0:T(8,128)S(1)}, f32[68,128]{1,0:T(8,128)}, u32[]{:S(2)}) copy-start(f32[68,128]{1,0:T(8,128)} %constant.84.clone) | copy-start | bytes 104452

commit v2 on v1

--- a/solution.py
+++ b/solution.py
@@ -59,25 +59,37 @@
 EXCHANGE_IDS = [0]
 
 
-def exchange_kernel(size_x, size_y, *refs):
-    count = len(OFFSETS)
-    sources, targets = refs[:count], refs[count : 2 * count]
-    send_sem, recv_sem = refs[2 * count], refs[2 * count + 1]
+def spans(offset, halo_len, size):
+    if offset == 1:
+        return halo_len + size - halo_len, 0, halo_len
+    if offset == -1:
+        return halo_len, halo_len + size, halo_len
+    return halo_len, halo_len, size
+
+
+def fill_kernel(layout, in_ref, out_ref, send_sem, recv_sem):
+    ndim, dim_x, dim_y, hx, hy, size_x, size_y, mesh_x, mesh_y = layout
     me_x = lax.axis_index("gx")
     me_y = lax.axis_index("gy")
     peers = [
-        (lax.rem(me_x + np.int32(dx + size_x), np.int32(size_x)), lax.rem(me_y + np.int32(dy + size_y), np.int32(size_y)))
-        for dx, dy in OFFSETS
+        (lax.rem(me_x + np.int32(ox + mesh_x), np.int32(mesh_x)), lax.rem(me_y + np.int32(oy + mesh_y), np.int32(mesh_y)))
+        for ox, oy in OFFSETS
     ]
     barrier = pltpu.get_barrier_semaphore()
     for peer in peers:
         pl.semaphore_signal(barrier, inc=1, device_id=peer, device_id_type=pl.DeviceIdType.MESH)
-    pl.semaphore_wait(barrier, count)
+    pl.semaphore_wait(barrier, len(OFFSETS))
     copies = []
-    for slot, peer in enumerate(peers):
+    for slot, ((ox, oy), peer) in enumerate(zip(OFFSETS, peers)):
+        source = [slice(None)] * ndim
+        target = [slice(None)] * ndim
+        sx, tx, lx = spans(ox, hx, size_x)
+        sy, ty, ly = spans(oy, hy, size_y)
+        source[dim_x], target[dim_x] = pl.ds(sx, lx), pl.ds(tx, lx)
+        source[dim_y], target[dim_y] = pl.ds(sy, ly), pl.ds(ty, ly)
         copy = pltpu.make_async_remote_copy(
-            src_ref=sources[slot],
-            dst_ref=targets[slot],
+            src_ref=in_ref.at[tuple(source)],
+            dst_ref=out_ref.at[tuple(target)],
             send_sem=send_sem.at[slot],
             recv_sem=recv_sem.at[slot],
             device_id=peer,
@@ -89,40 +101,52 @@
         copy.wait()
 
 
-def exchange(pieces):
+def fill_halo(padded, dim_x, hx, dim_y, hy):
     cid = EXCHANGE_IDS[0]
     EXCHANGE_IDS[0] += 1
     count = len(OFFSETS)
+    size_x = padded.shape[dim_x] - 2 * hx
+    size_y = padded.shape[dim_y] - 2 * hy
+    layout = (padded.ndim, dim_x, dim_y, hx, hy, size_x, size_y, lax.axis_size("gx"), lax.axis_size("gy"))
     return pl.pallas_call(
-        functools.partial(exchange_kernel, lax.axis_size("gx"), lax.axis_size("gy")),
-        out_shape=[jax.ShapeDtypeStruct(p.shape, p.dtype) for p in pieces],
-        in_specs=[pl.BlockSpec(memory_space=pl.ANY)] * count,
-        out_specs=[pl.BlockSpec(memory_space=pl.ANY)] * count,
+        functools.partial(fill_kernel, layout),
+        out_shape=jax.ShapeDtypeStruct(padded.shape, padded.dtype),
+        in_specs=[pl.BlockSpec(memory_space=pl.ANY)],
+        out_specs=pl.BlockSpec(memory_space=pl.ANY),
         scratch_shapes=[pltpu.SemaphoreType.DMA((count,)), pltpu.SemaphoreType.DMA((count,))],
+        input_output_aliases={0: 0},
         compiler_params=pltpu.CompilerParams(collective_id=cid, has_side_effects=True),
-    )(*pieces)
-
-
-def halo(array, dx, hx, dy, hy):
-    size_x, size_y = array.shape[dx], array.shape[dy]
-    cut = lax.slice_in_dim
-    last_x = cut(array, size_x - hx, size_x, axis=dx)
-    first_x = cut(array, 0, hx, axis=dx)
-    pieces = [
-        last_x,
-        first_x,
-        cut(array, size_y - hy, size_y, axis=dy),
-        cut(array, 0, hy, axis=dy),
-        cut(last_x, size_y - hy, size_y, axis=dy),
-        cut(last_x, 0, hy, axis=dy),
-        cut(first_x, size_y - hy, size_y, axis=dy),
-        cut(first_x, 0, hy, axis=dy),
-    ]
-    before_x, after_x, before_y, after_y, corner_bb, corner_ba, corner_ab, corner_aa = exchange(pieces)
-    top = jnp.concatenate([corner_bb, before_x, corner_ba], axis=dy)
-    mid = jnp.concatenate([before_y, array, after_y], axis=dy)
-    bottom = jnp.concatenate([corner_ab, after_x, corner_aa], axis=dy)
-    return jnp.concatenate([top, mid, bottom], axis=dx)
+    )(padded)
+
+
+def pad_dims(array, dim_x, hx, dim_y, hy):
+    widths = [(0, 0)] * array.ndim
+    widths[dim_x] = (hx, hx)
+    widths[dim_y] = (hy, hy)
+    return jnp.pad(array, widths)
+
+
+def analysis_matrix(size, pad, out_halo):
+    half = size // 2 + 2 * out_halo
+    matrix = np.zeros((size + 2 * pad, 2 * half), np.float32)
+    for col in range(half):
+        k = col - out_halo
+        for j in range(8):
+            matrix[2 * k + j - 3 + pad, col] = filt_low[j]
+            matrix[2 * k + j - 3 + pad, half + col] = filt_high[j]
+    return matrix
+
+
+def synthesis_matrix(size, pad, out_halo):
+    matrix = np.zeros((2, size // 2 + 2 * pad, size + 2 * out_halo), np.float32)
+    for row in range(size // 2 + 2 * pad):
+        k = row - pad
+        for col in range(size + 2 * out_halo):
+            j = col - out_halo + 3 - 2 * k
+            if 0 <= j < 8:
+                matrix[0, row, col] = filt_low[j]
+                matrix[1, row, col] = filt_high[j]
+    return matrix
 
 
 def contract(left, right, dims, batch):
@@ -165,9 +189,9 @@
     return joined.reshape((2 * half,) + even.shape[1:])
 
 
-def analysis_ext(extended):
+def analysis_ext(extended, size_y, pad_y, out_halo):
     x_part = analyse_lead(extended)
-    y_part = batched_left(split_analysis(x_part.shape[1] - 6), x_part)
+    y_part = batched_left(analysis_matrix(size_y, pad_y, out_halo), x_part)
     size_z = y_part.shape[2]
     return contract(y_part, jnp.asarray(periodic_analysis(size_z)), ((2,), (0,)), ((), ()))
 
@@ -187,14 +211,13 @@
     return jnp.sign(coeffs) * jnp.maximum(jnp.abs(coeffs) - thresh, 0.0)
 
 
-def synthesis_ext(extended):
+def synthesis_ext(extended, size_y, pad_y, out_halo):
     two, hx4, _, hy4, size_z = extended.shape
     z_part = contract(extended, jnp.asarray(periodic_analysis(size_z)), ((4,), (1,)), ((), ()))
     z_part = z_part.reshape(2 * hx4, 2, hy4, size_z)
-    size_y = 2 * (hy4 - 4)
-    matrix = split_synthesis(size_y)
+    matrix = synthesis_matrix(size_y, pad_y, out_halo)
     y_part = batched_left(matrix[0], z_part[:, 0]) + batched_left(matrix[1], z_part[:, 1])
-    y_part = y_part.reshape(2, hx4, size_y, size_z)
+    y_part = y_part.reshape(2, hx4, matrix.shape[2], size_z)
     return synthesise_lead(y_part[0], y_part[1])
 
 
@@ -210,21 +233,25 @@
 
 def local(velocity, threshold_table, band_index):
     EXCHANGE_IDS[0] = 0
-    cube0 = analysis_ext(halo(velocity, 0, 3, 1, 3))
+    size_x, size_y, size_z = velocity.shape
+    ext0 = fill_halo(pad_dims(velocity, 0, 3, 1, 8), 0, 3, 1, 8)
+    cube0 = analysis_ext(ext0, size_y, 8, 0)
     shrunk0 = shrink_field(cube0, threshold_table, band_index[0])
-    cube1 = analysis_ext(halo(low_corner(cube0), 0, 9, 1, 9))
+    ext1 = fill_halo(pad_dims(low_corner(cube0), 0, 9, 1, 16), 0, 9, 1, 16)
+    cube1 = analysis_ext(ext1, size_y // 2, 16, 3)
     shrunk1 = blocked(shrink_field(cube1, threshold_table, band_index[1]))
-    cube2 = analysis_ext(low_corner(cube1))
+    cube2 = analysis_ext(low_corner(cube1), size_y // 4, 3, 0)
     shrunk2 = shrink_field(cube2, threshold_table, band_index[2])
     full2 = lax.dynamic_update_slice(shrunk2, low_corner(cube2), (0, 0, 0))
-    recon2 = synthesis_ext(halo(blocked(full2), 1, 3, 3, 3))
-    hx, hy = shrunk1.shape[1], shrunk1.shape[3]
-    full1 = shrunk1[:, 1 : hx - 1, :, 1 : hy - 1, :]
-    half_z = full1.shape[4] // 2
-    full1 = full1.at[0, :, 0, :, :half_z].set(recon2)
-    recon1 = synthesis_ext(full1)
-    full0 = lax.dynamic_update_slice(shrunk0, recon1, (0, 0, 0))
-    return synthesis_ext(halo(blocked(full0), 1, 2, 3, 2))
+    ext2 = fill_halo(pad_dims(blocked(full2), 1, 3, 3, 8), 1, 3, 3, 8)
+    recon2 = synthesis_ext(ext2, size_y // 4, 8, 3)
+    full1 = shrunk1[:, 1 : shrunk1.shape[1] - 1]
+    full1 = full1.at[0, :, 0, :, : full1.shape[4] // 2].set(recon2)
+    recon1 = synthesis_ext(full1, size_y // 2, 3, 0)
+    padded0 = pad_dims(blocked(shrunk0), 1, 2, 3, 8)
+    padded0 = padded0.at[0, 2 : 2 + size_x // 2, 0, 8 : 8 + size_y // 2, : size_z // 2].set(recon1)
+    ext0 = fill_halo(padded0, 1, 2, 3, 8)
+    return synthesis_ext(ext0, size_y, 8, 0)
 
 
 def solution(mesh):

time: 143 us -> 149 us (1.042)
  Pallas kernels: 54.8 us -> 59.8 us
  other arithmetic: 14.1 us -> 18.2 us
  local copies, waits for them, and re-layouts: 27.5 us -> 23.6 us
    slice x13 -> x2, local copies, waits for them, and re-layouts: 16.2 us -> 0.01 us  [local(): full1 = shrunk1[:, 1:shrunk1.shape[1] - 1]]
    pad x0 -> x4, local copies, waits for them, and re-layouts: none -> 11.3 us  [pad_dims(): return jnp.pad(array, widths)]
    add x3, other arithmetic: 3.26 us -> 11.9 us  [analyse_lead(): low = low + filt_low[j] * taken]
    concatenate x3 -> x0, other arithmetic: 5.09 us -> none  [the longest x2 4.58 us: halo(): return jnp.concatenate([top, mid, bottom], axis=dx)]
    pallas_call x4, Pallas kernels: 54.8 us -> 59.8 us  [fill_halo(): pl.pallas_call(functools.partial(fill_kernel, layout), out_shape=jax.Shap...]
where the time goes in v2:
time: 149 us; the launch traced here: 147 us
  Pallas kernels  59.8 us (40%)
  matrix products  44.8 us (30%)
  local copies, waits for them, and re-layouts  23.6 us (16%)
  other arithmetic  18.2 us (12%)
    pallas_call x4, Pallas kernels, fill_halo(): pl.pallas_call(functools.partial(fill_kernel, layout), out_shape=jax.Shap...  59.8 us
    dot_general x15, matrix products, contract(): lax.dot_general(left, right, (dims, batch), precision=PREC, preferred_ele...  44.8 us
    add x3, other arithmetic, analyse_lead(): low = low + filt_low[j] * taken  11.9 us
    pad x4, local copies, waits for them, and re-layouts, pad_dims(): return jnp.pad(array, widths)  11.3 us
    another operation x3, local copies, waits for them, and re-layouts, synthesise_lead(): joined = jnp.stack([even, odd], axis=1)  5.4 us
    another operation x6, other arithmetic, synthesise_lead(): joined = jnp.stack([even, odd], axis=1)  5.21 us

profile of v2, /device:TPU:8, one launch (start us, length us, event | category | flops | bytes accessed | tf_op | source)
XLA Modules:
  0.0 147.0 jit_solution(11444003105138263779)
XLA Ops:
  0.1 0.8 slice_bitcast_fusion.16
  0.9 0.9 select_reduce_fusion
  1.8 0.1 broadcast_add_fusion.2
  1.8 0.7 fusion.56
  2.5 0.7 fusion.54
  3.2 0.1 broadcast_add_fusion
  3.3 0.1 broadcast_add_fusion.1
  3.4 5.3 %pad.24.in_ref = f32[38,144,256]{2,1,0:T(8,128)} pad(f32[32,128,256]{2,1,0:T(8,128)} %param.22, f32[]{:T(128)} %constant.80.clone.1), padding=3_3x8_8x0_0 | pad | bytes 9797636 | tf_op jit(solution)/shard_map/jit(_pad)/pad | solution.py:126
  8.7 16.9 %shard_map.172 = f32[38,144,256]{2,1,0:T(8,128)} custom-call(f32[38,144,256]{2,1,0:T(8,128)} %pad.24.in_ref), custom_call_target="tpu_custom_call", output_to_operand_aliasing={{}: (0, {})} | custom-call | tf_op jit(solution)/shard_map/pallas_call | solution.py:111
  25.6 0.0 copy-start.3
  25.6 8.1 %multiply_add_fusion.1 = (f32[16,144,256]{2,1,0:T(8,128)S(1)}, f32[16,144,256]{2,1,0:T(8,128)S(1)}) fusion(f32[38,144,256]{2,1,0:T(8,128)} %shard_map.172), kind=kLoop, calls=%fused_computation.26 | loop fusion | flops 17694720 | bytes 23592960 | tf_op jit(solution)/shard_map/add | solution.py:169
  33.7 0.0 copy-start.14
  33.7 3.6 %fusion = f32[32,128,256]{2,1,0:T(8,128)S(1)} fusion(f32[16,144,256]{2,1,0:T(8,128)S(1)} %get-tuple-element.33, f32[16,144,256]{2,1,0:T(8,128)S(1)} %get-tuple-element.32, f32[144,128]{1,0:T(8,128)S(1)} %copy-done.3), kind=kOutput, calls=%fused_computation.8 | convolution fusion | flops 907149312 | bytes 8986624 | tf_op jit(solution)/shard_map/dot_general | solution.py:153
  37.4 10.4 %maximum_multiply_fusion = (f32[32,128,256]{2,1,0:T(8,128)}, f32[32,128,256]{2,1,0:T(8,128)S(1)}) fusion(f32[]{:T(128)} %bitcast.8, f32[]{:T(128)} %bitcast.7, f32[]{:T(128)} %bitcast.6, f32[]{:T(128)} %bitcast.5, f32[]{:T(128)} %bitcast.4, f32[]{:T(128)} %bitcast.3, f32[]{:T(128)} %bitcast.2, s32[256]{0:T(256)S(1)} %compare_convert_fusion.1, ...), kind=kOutput, calls=%fused_computation.13 | convolution fusion | flops 1631584256 | bytes 12862492 | tf_op jit(solution)/shard_map/dot_general | solution.py:153
  47.8 1.4 pad.26.in_ref
  49.2 13.3 %shard_map.173 = f32[34,96,128]{2,1,0:T(8,128)} custom-call(f32[34,96,128]{2,1,0:T(8,128)} %pad.26.in_ref), custom_call_target="tpu_custom_call", output_to_operand_aliasing={{}: (0, {})} | custom-call | tf_op jit(solution)/shard_map/pallas_call | solution.py:111
  62.4 0.0 copy-start.7
  62.5 3.7 %multiply_add_fusion.3 = (f32[14,96,128]{2,1,0:T(8,128)S(1)}, f32[14,96,128]{2,1,0:T(8,128)S(1)}) fusion(f32[34,96,128]{2,1,0:T(8,128)} %shard_map.173), kind=kLoop, calls=%fused_computation.52 | loop fusion | flops 5160960 | bytes 6881280 | tf_op jit(solution)/shard_map/add | solution.py:169
  66.2 0.0 copy-start.15
  66.2 0.0 copy-done.7
  66.2 0.7 fusion.14
  67.0 0.1 copy-done.15
  67.1 6.0 %maximum_multiply_fusion.1 = (f32[28,76,128]{2,1,0:T(8,128)S(1)}, f32[28,76,128]{2,1,0:T(8,128)S(1)}) fusion(f32[]{:T(128)} %bitcast.18, f32[]{:T(128)} %bitcast.17, f32[]{:T(128)} %bitcast.16, f32[]{:T(128)} %bitcast.15, f32[]{:T(128)} %bitcast.14, f32[]{:T(128)} %bitcast.13, f32[]{:T(128)} %bitcast.12, s32[128]{0:T(128)S(1)} %compare_convert_fusion.2, ...), kind=kOutput, calls=%fused_computation.48 | convolution fusion | flops 214638592 | bytes 3343196 | tf_op jit(solution)/shard_map/dot_general | solution.py:153
  73.1 0.0 copy-start.13
  73.1 0.1 reshape.285
  73.2 0.0 copy-start.16
  73.2 0.0 copy-start.8
  73.3 0.1 multiply_add_fusion.5
  73.4 0.5 copy-done.13
  73.8 0.2 fusion.36
  74.0 4.6 %maximum_multiply_fusion.2 = (f32[8,32,64]{2,1,0:T(8,128)S(1)}, f32[8,32,64]{2,1,0:T(8,128)S(1)}) fusion(f32[]{:T(128)} %bitcast.27, f32[]{:T(128)} %bitcast.26, f32[]{:T(128)} %bitcast.25, f32[]{:T(128)} %bitcast.24, f32[]{:T(128)} %bitcast.23, f32[]{:T(128)} %bitcast.22, f32[]{:T(128)} %bitcast.21, s32[64]{0:T(128)S(1)} %compare_convert_fusion, ...), kind=kOutput, calls=%fused_computation.89 | convolution fusion | flops 6619136 | bytes 214300 | tf_op jit(solution)/shard_map/dot_general | solution.py:153
  78.6 0.0 copy-start.11
  78.6 0.6 dynamic_update_slice.3
  79.3 0.9 pad.27.in_ref
  80.2 11.1 %shard_map.174 = f32[2,10,2,32,64]{4,3,2,1,0:T(8,128)} custom-call(f32[2,10,2,32,64]{4,3,2,1,0:T(8,128)} %pad.27.in_ref), custom_call_target="tpu_custom_call", output_to_operand_aliasing={{}: (0, {})} | custom-call | tf_op jit(solution)/shard_map/pallas_call | solution.py:111
  91.3 1.5 %fusion.57 = f32[2,10,2,32,64]{4,3,2,1,0:T(8,128)S(1)} fusion(f32[2,10,2,32,64]{4,3,2,1,0:T(8,128)} %shard_map.174, f32[64,64,1,1,1]{1,0,4,3,2:T(8,128)S(1)} %copy-done.8), kind=kOutput, calls=%fused_computation.133 | convolution fusion | flops 31457280 | bytes 671744 | tf_op jit(solution)/shard_map/dot_general | solution.py:153
  92.9 0.0 slice-start
  92.9 0.0 copy-done.12
  92.9 0.0 copy-start.4
  92.9 0.6 fusion.25
  93.5 0.6 fusion.19
  94.0 0.0 copy-start.10
  94.0 0.1 fusion.49
  94.2 0.0 copy-start.9
  94.3 0.6 scatter.6
  94.9 0.6 fusion.58
  95.5 0.8 fusion.24
  96.3 0.8 fusion.18
  97.1 0.0 copy-start
  97.2 0.3 fusion.33
  97.5 1.8 %copy-done = f32[32,128,256]{2,1,0:T(8,128)S(1)} copy-done((f32[32,128,256]{2,1,0:T(8,128)S(1)}, f32[32,128,256]{2,1,0:T(8,128)}, u32[]{:S(2)}) %copy-start) | copy-done | bytes 4194328
  99.3 3.6 %pad.25 = f32[2,20,2,80,256]{4,3,2,1,0:T(8,128)} pad(f32[2,16,2,64,256]{4,3,2,1,0:T(8,128)S(1)} %bitcast.113, f32[]{:T(128)} %constant.80.clone.1), padding=0_0x2_2x0_0x8_8x0_0 | pad | bytes 10747908 | tf_op jit(solution)/shard_map/jit(_pad)/pad | solution.py:126
  103.0 0.9 constant_dynamic-update-slice_fusion.in_ref
  103.8 18.5 %shard_map.175 = f32[2,20,2,80,256]{4,3,2,1,0:T(8,128)} custom-call(f32[2,20,2,80,256]{4,3,2,1,0:T(8,128)} %constant_dynamic-update-slice_fusion.in_ref), custom_call_target="tpu_custom_call", output_to_operand_aliasing={{}: (0, {})} | custom-call | tf_op jit(solution)/shard_map/pallas_call | solution.py:111
  122.3 0.0 copy-done.2
  122.4 0.0 copy-start.6
  122.4 5.1 %fusion.59 = f32[2,20,2,80,256]{4,3,2,1,0:T(8,128)S(1)} fusion(f32[2,20,2,80,256]{4,3,2,1,0:T(8,128)} %shard_map.175, f32[256,256,1,1,1]{1,0,4,3,2:T(8,128)S(1)} %copy-done.2), kind=kOutput, calls=%fused_computation.135 | convolution fusion | flops 2516582400 | bytes 13369344 | tf_op jit(solution)/shard_map/dot_general | solution.py:153
  127.5 0.0 copy-start.5
  127.5 4.7 %fusion.4 = f32[40,256,128]{2,1,0:T(8,128)S(1)} fusion(f32[40,2,80,256]{3,2,1,0:T(8,128)S(1)} %bitcast.111, f32[80,128]{1,0:T(8,128)S(1)} %copy-done.6), kind=kOutput, calls=%fused_computation.22 | convolution fusion | flops 629145600 | bytes 8560640 | tf_op jit(solution)/shard_map/dot_general | solution.py:153
  132.2 0.0 copy-done.5
  132.2 4.7 %add_bitcast_fusion = f32[40,128,256]{1,2,0:T(8,128)S(1)} fusion(f32[40,256,128]{2,1,0:T(8,128)S(1)} %fusion.4, f32[40,2,80,256]{3,2,1,0:T(8,128)S(1)} %bitcast.112, f32[80,128]{1,0:T(8,128)S(1)} %copy-done.5), kind=kOutput, calls=%fused_computation.7 | convolution fusion | flops 630456320 | bytes 13803520 | tf_op jit(solution)/shard_map/dot_general | solution.py:153
  136.9 2.5 %fusion.13 = (f32[16,1,128,256]{2,3,0,1:T(8,128)S(1)}, f32[16,1,128,256]{2,3,0,1:T(8,128)S(1)}) fusion(f32[40,128,256]{1,2,0:T(8,128)S(1)} %add_bitcast_fusion), kind=kLoop, calls=%fused_computation.37 | loop fusion | flops 15728640 | bytes 25165824 | tf_op jit(solution)/shard_map/stack | solution.py:188
  139.4 2.2 %pad_maximum_fusion = f32[16,2,128,256]{2,3,0,1:T(8,128)} fusion(f32[16,1,128,256]{2,3,0,1:T(8,128)S(1)} %get-tuple-element.35, f32[16,1,128,256]{2,3,0,1:T(8,128)S(1)} %get-tuple-element.34), kind=kLoop, calls=%fused_computation.12 | loop fusion | flops 1048576 | bytes 8388608 | tf_op jit(solution)/shard_map/stack | solution.py:188
  141.6 5.3 %copy.49 = f32[16,2,128,256]{3,2,1,0:T(8,128)} copy(f32[16,2,128,256]{2,3,0,1:T(8,128)} %pad_maximum_fusion) | data formatting | bytes 8388608 | tf_op jit(solution)/shard_map/stack | solution.py:188
  (30 shorter events, 0.2 us)
Async XLA Ops:
  25.6 8.1 %copy-start.3 = (f32[144,128]{1,0:T(8,128)S(1)}, f32[144,128]{1,0:T(8,128)}, u32[]{:S(2)}) copy-start(f32[144,128]{1,0:T(8,128)} %constant.108.clone) | copy-start | bytes 221188
  33.7 3.7 %copy-start.14 = (f32[256,256,1]{1,0,2:T(8,128)S(1)}, f32[256,256,1]{1,0,2:T(8,128)}, u32[]{:S(2)}) copy-start(f32[256,256,1]{1,0,2:T(8,128)} %constant.254) | copy-start | bytes 786436
  62.4 3.8 %copy-start.7 = (f32[96,76]{0,1:T(8,128)S(1)}, f32[96,76]{0,1:T(8,128)}, u32[]{:S(2)}) copy-start(f32[96,76]{0,1:T(8,128)} %constant.110.clone) | copy-start | bytes 87556
  66.2 0.8 copy-start.15
  73.1 0.7 copy-start.13
  73.2 7.0 %copy-start.1 = (f32[2,14,2,38,128]{4,3,2,1,0:T(8,128)}, f32[2,14,2,38,128]{4,3,2,1,0:T(8,128)S(1)}, u32[]{:S(2)}) copy-start(f32[2,14,2,38,128]{4,3,2,1,0:T(8,128)S(1)} %reshape.285) | copy-start | bytes 3268612
  73.2 0.8 copy-start.16
  73.2 18.1 %copy-start.8 = (f32[64,64,1,1,1]{1,0,4,3,2:T(8,128)S(1)}, f32[64,64,1,1,1]{1,0,4,3,2:T(8,128)}, u32[]{:S(2)}) copy-start(f32[64,64,1,1,1]{1,0,4,3,2:T(8,128)} %constant.257) | copy-start | bytes 49156
  73.8 19.1 %copy-start.12 = (f32[32,38]{1,0:T(8,128)S(1)}, f32[32,38]{1,0:T(8,128)}, u32[]{:S(2)}) copy-start(f32[32,38]{1,0:T(8,128)} %constant.114.clone) | copy-start | bytes 14596
  78.6 14.8 %copy-start.11 = (f32[32,38]{1,0:T(8,128)S(1)}, f32[32,38]{1,0:T(8,128)}, u32[]{:S(2)}) copy-start(f32[32,38]{1,0:T(8,128)} %constant.115.clone) | copy-start | bytes 14596
  92.9 1.4 slice-start
  92.9 2.0 %copy-start.4 = (f32[128,128,1,1,1]{1,0,4,3,2:T(8,128)S(1)}, f32[128,128,1,1,1]{1,0,4,3,2:T(8,128)}, u32[]{:S(2)}) copy-start(f32[128,128,1,1,1]{1,0,4,3,2:T(8,128)} %constant.258) | copy-start | bytes 196612
  94.0 1.4 copy-start.10
  94.2 2.1 %copy-start.9 = (f32[38,64]{1,0:T(8,128)S(1)}, f32[38,64]{1,0:T(8,128)}, u32[]{:S(2)}) copy-start(f32[38,64]{1,0:T(8,128)} %constant.117.clone) | copy-start | bytes 29188
  97.1 2.2 %copy-start = (f32[32,128,256]{2,1,0:T(8,128)S(1)}, f32[32,128,256]{2,1,0:T(8,128)}, u32[]{:S(2)}) copy-start(f32[32,128,256]{2,1,0:T(8,128)} %get-tuple-element.68) | copy-start | bytes 12582916
  103.8 18.5 %copy-start.2 = (f32[256,256,1,1,1]{1,0,4,3,2:T(8,128)S(1)}, f32[256,256,1,1,1]{1,0,4,3,2:T(8,128)}, u32[]{:S(2)}) copy-start(f32[256,256,1,1,1]{1,0,4,3,2:T(8,128)} %constant.259) | copy-start | bytes 786436
  122.4 5.1 %copy-start.6 = (f32[80,128]{1,0:T(8,128)S(1)}, f32[80,128]{1,0:T(8,128)}, u32[]{:S(2)}) copy-start(f32[80,128]{1,0:T(8,128)} %constant.119.clone) | copy-start | bytes 122884
  127.5 4.7 %copy-start.5 = (f32[80,128]{1,0:T(8,128)S(1)}, f32[80,128]{1,0:T(8,128)}, u32[]{:S(2)}) copy-start(f32[80,128]{1,0:T(8,128)} %constant.118.clone) | copy-start | bytes 122884

commit v3 on v1

--- a/solution.py
+++ b/solution.py
@@ -61,8 +61,9 @@
 
 def exchange_kernel(size_x, size_y, *refs):
     count = len(OFFSETS)
-    sources, targets = refs[:count], refs[count : 2 * count]
-    send_sem, recv_sem = refs[2 * count], refs[2 * count + 1]
+    total = (len(refs) - 2) // 2
+    sources, targets = refs[:total], refs[total : 2 * total]
+    send_sem, recv_sem = refs[2 * total], refs[2 * total + 1]
     me_x = lax.axis_index("gx")
     me_y = lax.axis_index("gy")
     peers = [
@@ -74,7 +75,8 @@
         pl.semaphore_signal(barrier, inc=1, device_id=peer, device_id_type=pl.DeviceIdType.MESH)
     pl.semaphore_wait(barrier, count)
     copies = []
-    for slot, peer in enumerate(peers):
+    for slot in range(len(sources)):
+        peer = peers[slot % count]
         copy = pltpu.make_async_remote_copy(
             src_ref=sources[slot],
             dst_ref=targets[slot],
@@ -92,7 +94,7 @@
 def exchange(pieces):
     cid = EXCHANGE_IDS[0]
     EXCHANGE_IDS[0] += 1
-    count = len(OFFSETS)
+    count = len(pieces)
     return pl.pallas_call(
         functools.partial(exchange_kernel, lax.axis_size("gx"), lax.axis_size("gy")),
         out_shape=[jax.ShapeDtypeStruct(p.shape, p.dtype) for p in pieces],
@@ -103,12 +105,12 @@
     )(*pieces)
 
 
-def halo(array, dx, hx, dy, hy):
+def halo_pieces(array, dx, hx, dy, hy):
     size_x, size_y = array.shape[dx], array.shape[dy]
     cut = lax.slice_in_dim
     last_x = cut(array, size_x - hx, size_x, axis=dx)
     first_x = cut(array, 0, hx, axis=dx)
-    pieces = [
+    return [
         last_x,
         first_x,
         cut(array, size_y - hy, size_y, axis=dy),
@@ -118,11 +120,30 @@
         cut(first_x, size_y - hy, size_y, axis=dy),
         cut(first_x, 0, hy, axis=dy),
     ]
-    before_x, after_x, before_y, after_y, corner_bb, corner_ba, corner_ab, corner_aa = exchange(pieces)
+
+
+def assemble(array, dx, dy, received):
+    before_x, after_x, before_y, after_y, corner_bb, corner_ba, corner_ab, corner_aa = received
     top = jnp.concatenate([corner_bb, before_x, corner_ba], axis=dy)
     mid = jnp.concatenate([before_y, array, after_y], axis=dy)
     bottom = jnp.concatenate([corner_ab, after_x, corner_aa], axis=dy)
     return jnp.concatenate([top, mid, bottom], axis=dx)
+
+
+def halos(requests):
+    pieces = []
+    for array, dx, hx, dy, hy in requests:
+        pieces += halo_pieces(array, dx, hx, dy, hy)
+    received = exchange(pieces)
+    count = len(OFFSETS)
+    return [
+        assemble(array, dx, dy, received[n * count : (n + 1) * count])
+        for n, (array, dx, hx, dy, hy) in enumerate(requests)
+    ]
+
+
+def halo(array, dx, hx, dy, hy):
+    return halos([(array, dx, hx, dy, hy)])[0]
 
 
 def contract(left, right, dims, batch):
@@ -211,20 +232,19 @@
 def local(velocity, threshold_table, band_index):
     EXCHANGE_IDS[0] = 0
     cube0 = analysis_ext(halo(velocity, 0, 3, 1, 3))
-    shrunk0 = shrink_field(cube0, threshold_table, band_index[0])
-    cube1 = analysis_ext(halo(low_corner(cube0), 0, 9, 1, 9))
+    shrunk0 = blocked(shrink_field(cube0, threshold_table, band_index[0]))
+    ext1, ext0 = halos([(low_corner(cube0), 0, 9, 1, 9), (shrunk0, 1, 2, 3, 2)])
+    cube1 = analysis_ext(ext1)
     shrunk1 = blocked(shrink_field(cube1, threshold_table, band_index[1]))
     cube2 = analysis_ext(low_corner(cube1))
     shrunk2 = shrink_field(cube2, threshold_table, band_index[2])
     full2 = lax.dynamic_update_slice(shrunk2, low_corner(cube2), (0, 0, 0))
-    recon2 = synthesis_ext(halo(blocked(full2), 1, 3, 3, 3))
-    hx, hy = shrunk1.shape[1], shrunk1.shape[3]
-    full1 = shrunk1[:, 1 : hx - 1, :, 1 : hy - 1, :]
-    half_z = full1.shape[4] // 2
-    full1 = full1.at[0, :, 0, :, :half_z].set(recon2)
-    recon1 = synthesis_ext(full1)
-    full0 = lax.dynamic_update_slice(shrunk0, recon1, (0, 0, 0))
-    return synthesis_ext(halo(blocked(full0), 1, 2, 3, 2))
+    recon2 = synthesis_ext(halo(blocked(full2), 1, 4, 3, 4))
+    recon2 = recon2[1 : recon2.shape[0] - 1, 1 : recon2.shape[1] - 1]
+    half_z = shrunk1.shape[4] // 2
+    recon1 = synthesis_ext(shrunk1.at[0, :, 0, :, :half_z].set(recon2))
+    half_z = ext0.shape[4] // 2
+    return synthesis_ext(ext0.at[0, :, 0, :, :half_z].set(recon1))
 
 
 def solution(mesh):

time: 143 us -> 133 us (0.930)
  Pallas kernels: 54.8 us -> 46.6 us
  matrix products: 45 us -> 42 us
  other arithmetic: 14.1 us -> 15.7 us
    pallas_call x4 -> x3, Pallas kernels: 54.8 us -> 46.6 us  [exchange(): pl.pallas_call(functools.partial(exchange_kernel, lax.axis_size('gx'), la...]
    slice x13 -> x10, local copies, waits for them, and re-layouts: 16.2 us -> 12 us  [the longest x3 4.73 us: halo_pieces(): first_x = cut(array, 0, hx, axis=dx)]
    scatter x1 -> x2, local copies, waits for them, and re-layouts: 0.43 us -> 3.54 us  [the longest x1 3.46 us: local(): recon1 = synthesis_ext(shrunk1.at[0, :, 0, :, :half_z].set(recon2))]
    dot_general x15, matrix products: 45 us -> 42 us  [contract(): lax.dot_general(left, right, (dims, batch), precision=PREC, preferred_ele...]
    unnamed x42 -> x64, local copies, waits for them, and re-layouts: 1.24 us -> 2.97 us
    concatenate x3 -> x4, other arithmetic: 5.09 us -> 6.43 us  [the longest x3 5.92 us: assemble(): return jnp.concatenate([top, mid, bottom], axis=dx)]
where the time goes in v3:
time: 133 us; the launch traced here: 132 us
  Pallas kernels  46.6 us (35%)
  matrix products  42 us (32%)
  local copies, waits for them, and re-layouts  27.1 us (20%)
  other arithmetic  15.7 us (12%)
    pallas_call x3, Pallas kernels, exchange(): pl.pallas_call(functools.partial(exchange_kernel, lax.axis_size('gx'), la...  46.6 us
    dot_general x15, matrix products, contract(): lax.dot_general(left, right, (dims, batch), precision=PREC, preferred_ele...  42 us
    concatenate x3, other arithmetic, assemble(): return jnp.concatenate([top, mid, bottom], axis=dx)  5.92 us
    another operation x3, local copies, waits for them, and re-layouts, synthesise_lead(): joined = jnp.stack([even, odd], axis=1)  5.42 us
    another operation x6, other arithmetic, synthesise_lead(): joined = jnp.stack([even, odd], axis=1)  5.4 us
    slice x3, local copies, waits for them, and re-layouts, halo_pieces(): first_x = cut(array, 0, hx, axis=dx)  4.73 us
    slice x4, local copies, waits for them, and re-layouts, halo_pieces(): cut(array, 0, hy, axis=dy)  4.03 us
    scatter x1, local copies, waits for them, and re-layouts, local(): recon1 = synthesis_ext(shrunk1.at[0, :, 0, :, :half_z].set(recon2))  3.46 us

profile of v3, /device:TPU:8, one launch (start us, length us, event | category | flops | bytes accessed | tf_op | source)
XLA Modules:
  0.0 132.1 jit_solution(16182192324414099228)
XLA Ops:
  0.0 1.4 %fusion.79 = (f32[3,3,256]{2,1,0:T(4,128)}, f32[3,3,256]{2,1,0:T(4,128)}, f32[3,3,256]{2,1,0:T(4,128)}, f32[3,3,256]{2,1,0:T(4,128)}) fusion(f32[32,128,256]{2,1,0:T(8,128)} %param.22), kind=kLoop, calls=%fused_computation.160 | loop fusion | bytes 73728 | tf_op jit(solution)/shard_map/slice | solution.py:121
  1.4 2.1 %fusion.81 = (f32[3,128,256]{2,1,0:T(8,128)}, f32[3,128,256]{2,1,0:T(8,128)}) fusion(f32[32,128,256]{2,1,0:T(8,128)} %param.22), kind=kLoop, calls=%fused_computation.162 | loop fusion | bytes 1572864 | tf_op jit(solution)/shard_map/slice | solution.py:112
  3.5 1.8 %fusion.80 = (f32[32,3,256]{2,1,0:T(4,128)}, f32[32,3,256]{2,1,0:T(4,128)}) fusion(f32[32,128,256]{2,1,0:T(8,128)} %param.22), kind=kLoop, calls=%fused_computation.161 | loop fusion | bytes 393216 | tf_op jit(solution)/shard_map/slice | solution.py:117
  5.3 16.8 %shard_map.172 = (f32[3,128,256]{2,1,0:T(8,128)}, f32[3,128,256]{2,1,0:T(8,128)}, f32[32,3,256]{2,1,0:T(4,128)}, f32[32,3,256]{2,1,0:T(4,128)}, f32[3,3,256]{2,1...) custom-call(f32[3,128,256]{2,1,0:T(8,128)} %get-tuple-element.123.refs_0_, ...), custom_call_target="tpu_custom_call" | custom-call | tf_op jit(solution)/shard_map/pallas_call | solution.py:98
  22.1 3.2 %maximum_maximum_fusion.1 = f32[38,134,256]{2,1,0:T(8,128)S(1)} fusion(f32[3,3,256]{2,1,0:T(4,128)} %get-tuple-element.68, f32[3,128,256]{2,1,0:T(8,128)} %get-tuple-element.67, f32[3,3,256]{2,1,0:T(4,128)} %get-tuple-element.66, f32[32,3,256]{2,1,0:T(4,128)} %get-tuple-element.65, f32[32,128,256]{2,1,0:T(8,128)} %param.22, ...), kind=kLoop, calls=%fused_computation.8 | loop fusion | flops 10428416 | bytes 10428416 | tf_op jit(solution)/shard_map/concatenate | solution.py:130
  25.2 0.7 copy-done
  25.9 0.0 copy-done.6
  26.0 0.5 pad_maximum_fusion
  26.5 0.0 copy-start.12
  26.5 2.7 %multiply_add_fusion.1 = (f32[16,134,256]{2,1,0:T(8,128)S(1)}, f32[16,134,256]{2,1,0:T(8,128)S(1)}) fusion(f32[38,134,256]{2,1,0:T(8,128)S(1)} %maximum_maximum_fusion.1, f32[32,134,256]{2,1,0:T(8,128)S(1)} %pad_maximum_fusion), kind=kLoop, calls=%fused_computation.29 | loop fusion | flops 16465920 | bytes 21954560 | tf_op jit(solution)/shard_map/add | solution.py:166
  29.2 0.0 copy-start.28
  29.2 3.8 %fusion = f32[32,128,256]{2,1,0:T(8,128)S(1)} fusion(f32[16,134,256]{2,1,0:T(8,128)S(1)} %get-tuple-element.97, f32[16,134,256]{2,1,0:T(8,128)S(1)} %get-tuple-element.96, f32[134,128]{1,0:T(8,128)S(1)} %copy-done.12), kind=kOutput, calls=%fused_computation.11 | convolution fusion | flops 844152832 | bytes 8653824 | tf_op jit(solution)/shard_map/dot_general | solution.py:150
  33.0 0.2 select_reduce_fusion
  33.3 0.7 fusion.85
  33.9 0.1 broadcast_add_fusion.1
  34.0 9.1 %maximum_multiply_fusion = (f32[32,128,256]{2,1,0:T(8,128)S(1)}, f32[32,128,256]{2,1,0:T(8,128)S(1)}) fusion(f32[]{:T(128)} %bitcast.8, f32[]{:T(128)} %bitcast.7, f32[]{:T(128)} %bitcast.6, f32[]{:T(128)} %bitcast.5, f32[]{:T(128)} %bitcast.4, f32[]{:T(128)} %bitcast.3, f32[]{:T(128)} %bitcast.2, s32[256]{0:T(256)S(1)} %compare_convert_fusion.1, ...), kind=kOutput, calls=%fused_computation.16 | convolution fusion | flops 1631584256 | bytes 12862492 | tf_op jit(solution)/shard_map/dot_general | solution.py:150
  43.1 1.2 fusion.75
  44.3 1.5 %fusion.78 = (f32[9,64,128]{2,1,0:T(8,128)}, f32[9,64,128]{2,1,0:T(8,128)}) fusion(f32[32,128,256]{2,1,0:T(8,128)S(1)} %get-tuple-element.159), kind=kLoop, calls=%fused_computation.159 | loop fusion | bytes 1179648 | tf_op jit(solution)/shard_map/slice | solution.py:112
  45.8 1.1 fusion.76
  46.9 0.8 fusion.74
  47.7 0.7 fusion.77
  48.5 0.6 fusion.73
  49.1 19.0 %shard_map.173 = (f32[9,64,128]{2,1,0:T(8,128)}, f32[9,64,128]{2,1,0:T(8,128)}, f32[16,9,128]{2,1,0:T(8,128)}, f32[16,9,128]{2,1,0:T(8,128)}, f32[9,9,128]{2,1,0...) custom-call(f32[9,64,128]{2,1,0:T(8,128)} %get-tuple-element.115.ref, ...), custom_call_target="tpu_custom_call" | custom-call | tf_op jit(solution)/shard_map/pallas_call | solution.py:98
  68.1 1.1 slice.626
  69.2 1.4 %maximum_maximum_fusion.2 = f32[34,82,128]{2,1,0:T(8,128)S(1)} fusion(f32[9,9,128]{2,1,0:T(8,128)} %get-tuple-element.84, f32[9,64,128]{2,1,0:T(8,128)} %get-tuple-element.83, f32[9,9,128]{2,1,0:T(8,128)} %get-tuple-element.82, f32[16,9,128]{2,1,0:T(8,128)} %get-tuple-element.81, f32[16,64,128]{2,1,0:T(8,128)S(1)} %slice.626, ...), kind=kLoop, calls=%fused_computation.42 | loop fusion | flops 2854912 | bytes 2854912 | tf_op jit(solution)/shard_map/concatenate | solution.py:130
  70.7 0.0 copy-start.14
  70.7 0.7 multiply_add_fusion.3
  71.3 0.0 copy-start.29
  71.3 0.1 copy-done.14
  71.4 0.7 fusion.15
  72.1 0.7 fusion.83
  72.8 0.1 broadcast_add_fusion
  72.9 6.2 %maximum_multiply_fusion.1 = (f32[28,76,128]{2,1,0:T(8,128)S(1)}, f32[28,76,128]{2,1,0:T(8,128)S(1)}) fusion(f32[]{:T(128)} %bitcast.18, f32[]{:T(128)} %bitcast.17, f32[]{:T(128)} %bitcast.16, f32[]{:T(128)} %bitcast.15, f32[]{:T(128)} %bitcast.14, f32[]{:T(128)} %bitcast.13, f32[]{:T(128)} %bitcast.12, s32[128]{0:T(128)S(1)} %compare_convert_fusion.2, ...), kind=kOutput, calls=%fused_computation.51 | convolution fusion | flops 214638592 | bytes 3343196 | tf_op jit(solution)/shard_map/dot_general | solution.py:150
  79.2 0.1 multiply_add_fusion.5
  79.3 0.2 fusion.62
  79.5 0.1 broadcast_add_fusion.2
  79.6 4.6 %maximum_multiply_fusion.2 = (f32[8,32,64]{2,1,0:T(8,128)S(1)}, f32[8,32,64]{2,1,0:T(8,128)S(1)}) fusion(f32[]{:T(128)} %bitcast.27, f32[]{:T(128)} %bitcast.26, f32[]{:T(128)} %bitcast.25, f32[]{:T(128)} %bitcast.24, f32[]{:T(128)} %bitcast.23, f32[]{:T(128)} %bitcast.22, f32[]{:T(128)} %bitcast.21, s32[64]{0:T(128)S(1)} %compare_convert_fusion, ...), kind=kOutput, calls=%fused_computation.124 | convolution fusion | flops 6619136 | bytes 214300 | tf_op jit(solution)/shard_map/dot_general | solution.py:150
  84.2 0.6 dynamic_update_slice.3
  84.8 0.7 fusion.82
  85.5 10.8 %shard_map.174 = (f32[2,4,2,16,64]{4,3,2,1,0:T(8,128)}, f32[2,4,2,16,64]{4,3,2,1,0:T(8,128)}, f32[2,4,2,4,64]{4,3,2,1,0:T(4,128)}, f32[2,4,2,4,64]{4,3,2,1,0:T(4...) custom-call(f32[2,4,2,16,64]{4,3,2,1,0:T(8,128)} %bitcast.121, ...), custom_call_target="tpu_custom_call" | custom-call | tf_op jit(solution)/shard_map/pallas_call | solution.py:98
  96.3 1.6 %fusion.23 = f32[2,12,2,24,64]{4,3,2,1,0:T(8,128)S(1)} fusion(f32[64,64,1,1,1]{1,0,4,3,2:T(8,128)S(1)} %copy-done.30, f32[2,4,2,4,64]{4,3,2,1,0:T(4,128)} %get-tuple-element.92, f32[2,4,2,16,64]{4,3,2,1,0:T(8,128)} %get-tuple-element.91, f32[2,4,2,4,64]{4,3,2,1,0:T(4,128)} %get-tuple-element.90, f32[2,4,2,4,64]{4,3,2,1,0:T(4,128)} %get-tuple-element.89, ...), kind=kOutput, calls=%fused_computation.58 | convolution fusion | flops 28901376 | bytes 606208 | tf_op jit(solution)/shard_map/dot_general | solution.py:150
  97.9 0.6 fusion.51
  98.6 0.6 fusion.19
  99.2 0.2 fusion.61
  99.5 0.1 reshape.284
  99.6 3.5 %scatter.6 = f32[2,14,2,38,128]{4,3,2,1,0:T(8,128)S(1)} dynamic-update-slice(f32[2,14,2,38,128]{4,3,2,1,0:T(8,128)S(1)} %reshape.284, f32[1,14,1,38,64]{4,3,2,1,0:T(8,128)S(1)} %slice_bitcast_fusion.14, s32[]{:T(128)} %constant.85.clone.1, s32[]{:T(128)} %constant.85.clone.1, s32[]{:T(128)} %constant.85.clone.1, s32[]{:T(128)} %constant.85.clone.1, s32[]{:T(128)} %constant.85.clone.1) | dynamic-update-slice | bytes 272388 | tf_op jit(solution)/shard_map/scatter | solution.py:245
  103.1 0.6 fusion.86
  103.7 1.1 fusion.41
  104.8 1.1 fusion.14
  105.8 0.4 fusion.50
  106.3 0.1 pad_maximum_fusion.2
  106.4 1.6 %copy-done.2 = f32[32,128,256]{2,1,0:T(8,128)S(1)} copy-done((f32[32,128,256]{2,1,0:T(8,128)S(1)}, f32[32,128,256]{2,1,0:T(8,128)}, u32[]{:S(2)}) %copy-start.2) | copy-done | bytes 4194328
  108.0 0.2 copy-done.7
  108.2 0.2 copy-done.8
  108.4 0.0 copy-done.10
  108.4 0.0 copy-done.11
  108.5 1.3 maximum_maximum_fusion
  109.8 0.1 constant_dynamic-update-slice_fusion
  109.9 2.6 %fusion.87 = f32[2,20,2,68,256]{4,3,2,1,0:T(8,128)S(1)} fusion(f32[2,20,2,68,256]{4,3,2,1,0:T(8,128)S(1)} %constant_dynamic-update-slice_fusion, f32[256,256,1,1,1]{1,0,4,3,2:T(8,128)S(1)} %copy-done.9), kind=kOutput, calls=%fused_computation.168 | convolution fusion | flops 2139095040 | bytes 11403264 | tf_op jit(solution)/shard_map/dot_general | solution.py:150
  112.6 4.7 %fusion.4 = f32[40,256,128]{2,1,0:T(8,128)S(1)} fusion(f32[40,2,68,256]{3,2,1,0:T(8,128)S(1)} %bitcast.110, f32[68,128]{1,0:T(8,128)S(1)} %copy-done.15), kind=kOutput, calls=%fused_computation.25 | convolution fusion | flops 534773760 | bytes 8228864 | tf_op jit(solution)/shard_map/dot_general | solution.py:150
  117.3 4.7 %add_bitcast_fusion = f32[40,128,256]{1,2,0:T(8,128)S(1)} fusion(f32[40,256,128]{2,1,0:T(8,128)S(1)} %fusion.4, f32[40,2,68,256]{3,2,1,0:T(8,128)S(1)} %bitcast.111, f32[68,128]{1,0:T(8,128)S(1)} %copy-done.16), kind=kOutput, calls=%fused_computation.9 | convolution fusion | flops 536084480 | bytes 13471744 | tf_op jit(solution)/shard_map/dot_general | solution.py:150
  122.0 2.5 %fusion.13 = (f32[16,1,128,256]{2,3,0,1:T(8,128)S(1)}, f32[16,1,128,256]{2,3,0,1:T(8,128)S(1)}) fusion(f32[40,128,256]{1,2,0:T(8,128)S(1)} %add_bitcast_fusion), kind=kLoop, calls=%fused_computation.40 | loop fusion | flops 15728640 | bytes 25165824 | tf_op jit(solution)/shard_map/stack | solution.py:185
  124.5 2.3 %pad_maximum_fusion.1 = f32[16,2,128,256]{2,3,0,1:T(8,128)} fusion(f32[16,1,128,256]{2,3,0,1:T(8,128)S(1)} %get-tuple-element.99, f32[16,1,128,256]{2,3,0,1:T(8,128)S(1)} %get-tuple-element.98), kind=kLoop, calls=%fused_computation.15 | loop fusion | flops 1048576 | bytes 8388608 | tf_op jit(solution)/shard_map/stack | solution.py:185
  126.7 5.3 %copy.43 = f32[16,2,128,256]{3,2,1,0:T(8,128)} copy(f32[16,2,128,256]{2,3,0,1:T(8,128)} %pad_maximum_fusion.1) | data formatting | bytes 8388608 | tf_op jit(solution)/shard_map/stack | solution.py:185
  (68 shorter events, 0.3 us)
Async XLA Ops:
  22.0 3.9 %copy-start = (f32[32,128,256]{2,1,0:T(8,128)S(1)}, f32[32,128,256]{2,1,0:T(8,128)}, u32[]{:S(2)}) copy-start(f32[32,128,256]{2,1,0:T(8,128)} %param.22) | copy-start | bytes 12582916
  22.0 3.9 %copy-start.5 = (f32[32,3,256]{2,1,0:T(4,128)S(1)}, f32[32,3,256]{2,1,0:T(4,128)}, u32[]{:S(2)}) copy-start(f32[32,3,256]{2,1,0:T(4,128)} %get-tuple-element.64) | copy-start | bytes 294916
  22.1 3.9 %copy-start.6 = (f32[32,3,256]{2,1,0:T(4,128)S(1)}, f32[32,3,256]{2,1,0:T(4,128)}, u32[]{:S(2)}) copy-start(f32[32,3,256]{2,1,0:T(4,128)} %get-tuple-element.65) | copy-start | bytes 294916
  26.5 2.7 %copy-start.12 = (f32[134,128]{1,0:T(8,128)S(1)}, f32[134,128]{1,0:T(8,128)}, u32[]{:S(2)}) copy-start(f32[134,128]{1,0:T(8,128)} %constant.98.clone) | copy-start | bytes 205828
  29.2 3.8 %copy-start.26 = (s32[3,7]{1,0:T(4,128)S(1)}, s32[3,7]{1,0:T(4,128)}, u32[]{:S(2)}) copy-start(s32[3,7]{1,0:T(4,128)} %param.24) | copy-start | bytes 256
  29.2 3.8 %copy-start.27 = (f32[16]{0:T(128)S(1)}, f32[16]{0:T(128)}, u32[]{:S(2)}) copy-start(f32[16]{0:T(128)} %param.23) | copy-start | bytes 196
  29.2 4.8 %copy-start.28 = (f32[256,256,1]{1,0,2:T(8,128)S(1)}, f32[256,256,1]{1,0,2:T(8,128)}, u32[]{:S(2)}) copy-start(f32[256,256,1]{1,0,2:T(8,128)} %constant.111) | copy-start | bytes 786436
  43.1 5.4 %copy-start.1 = (f32[32,128,256]{2,1,0:T(8,128)}, f32[32,128,256]{2,1,0:T(8,128)S(1)}, u32[]{:S(2)}) copy-start(f32[32,128,256]{2,1,0:T(8,128)S(1)} %get-tuple-element.158) | copy-start | bytes 12582916
  43.1 6.0 %copy-start.4 = (f32[32,128,256]{2,1,0:T(8,128)}, f32[32,128,256]{2,1,0:T(8,128)S(1)}, u32[]{:S(2)}) copy-start(f32[32,128,256]{2,1,0:T(8,128)S(1)} %get-tuple-element.159) | copy-start | bytes 12582916
  70.7 0.8 copy-start.14
  71.3 1.6 %copy-start.29 = (f32[128,128,1]{1,0,2:T(8,128)S(1)}, f32[128,128,1]{1,0,2:T(8,128)}, u32[]{:S(2)}) copy-start(f32[128,128,1]{1,0,2:T(8,128)} %constant.112) | copy-start | bytes 196612
  72.9 6.4 %copy-start.23 = (f32[38,32]{0,1:T(8,128)S(1)}, f32[38,32]{0,1:T(8,128)}, u32[]{:S(2)}) copy-start(f32[38,32]{0,1:T(8,128)} %constant.102.clone) | copy-start | bytes 14596
  72.9 6.7 %copy-start.31 = (f32[64,64,1]{1,0,2:T(8,128)S(1)}, f32[64,64,1]{1,0,2:T(8,128)}, u32[]{:S(2)}) copy-start(f32[64,64,1]{1,0,2:T(8,128)} %constant.113) | copy-start | bytes 49156
  79.1 17.2 %copy-start.30 = (f32[64,64,1,1,1]{1,0,4,3,2:T(8,128)S(1)}, f32[64,64,1,1,1]{1,0,4,3,2:T(8,128)}, u32[]{:S(2)}) copy-start(f32[64,64,1,1,1]{1,0,4,3,2:T(8,128)} %constant.114) | copy-start | bytes 49156
  79.3 18.7 %copy-start.25 = (f32[24,40]{1,0:T(8,128)S(1)}, f32[24,40]{1,0:T(8,128)}, u32[]{:S(2)}) copy-start(f32[24,40]{1,0:T(8,128)} %constant.104.clone) | copy-start | bytes 11524
  79.6 19.0 %copy-start.24 = (f32[24,40]{1,0:T(8,128)S(1)}, f32[24,40]{1,0:T(8,128)}, u32[]{:S(2)}) copy-start(f32[24,40]{1,0:T(8,128)} %constant.105.clone) | copy-start | bytes 11524
  84.8 0.7 copy-start.3
  99.4 3.7 %copy-start.13 = (f32[128,128,1,1,1]{1,0,4,3,2:T(8,128)S(1)}, f32[128,128,1,1,1]{1,0,4,3,2:T(8,128)}, u32[]{:S(2)}) copy-start(f32[128,128,1,1,1]{1,0,4,3,2:T(8,128)} %constant.115) | copy-start | bytes 196612
  99.5 4.2 %copy-start.17 = (f32[38,68]{1,0:T(8,128)S(1)}, f32[38,68]{1,0:T(8,128)}, u32[]{:S(2)}) copy-start(f32[38,68]{1,0:T(8,128)} %constant.106.clone) | copy-start | bytes 31012
  99.6 5.2 %copy-start.18 = (f32[38,68]{1,0:T(8,128)S(1)}, f32[38,68]{1,0:T(8,128)}, u32[]{:S(2)}) copy-start(f32[38,68]{1,0:T(8,128)} %constant.107.clone) | copy-start | bytes 31012
  105.8 2.2 %copy-start.2 = (f32[32,128,256]{2,1,0:T(8,128)S(1)}, f32[32,128,256]{2,1,0:T(8,128)}, u32[]{:S(2)}) copy-start(f32[32,128,256]{2,1,0:T(8,128)} %copy-done.1) | copy-start | bytes 12582916
  106.2 2.0 %copy-start.7 = (f32[2,2,2,64,256]{4,3,2,1,0:T(8,128)S(1)}, f32[2,2,2,64,256]{4,3,2,1,0:T(8,128)}, u32[]{:S(2)}) copy-start(f32[2,2,2,64,256]{4,3,2,1,0:T(8,128)} %get-tuple-element.70) | copy-start | bytes 1572868
  106.3 2.1 %copy-start.8 = (f32[2,2,2,64,256]{4,3,2,1,0:T(8,128)S(1)}, f32[2,2,2,64,256]{4,3,2,1,0:T(8,128)}, u32[]{:S(2)}) copy-start(f32[2,2,2,64,256]{4,3,2,1,0:T(8,128)} %get-tuple-element.75) | copy-start | bytes 1572868
  106.3 2.1 %copy-start.10 = (f32[2,16,2,2,256]{4,3,2,1,0:T(2,128)S(1)}, f32[2,16,2,2,256]{4,3,2,1,0:T(2,128)}, u32[]{:S(2)}) copy-start(f32[2,16,2,2,256]{4,3,2,1,0:T(2,128)} %get-tuple-element.72) | copy-start | bytes 393220
  106.3 2.2 %copy-start.11 = (f32[2,16,2,2,256]{4,3,2,1,0:T(2,128)S(1)}, f32[2,16,2,2,256]{4,3,2,1,0:T(2,128)}, u32[]{:S(2)}) copy-start(f32[2,16,2,2,256]{4,3,2,1,0:T(2,128)} %get-tuple-element.73) | copy-start | bytes 393220
  106.3 2.2 %copy-start.19 = (f32[2,2,2,2,256]{4,3,2,1,0:T(2,128)S(1)}, f32[2,2,2,2,256]{4,3,2,1,0:T(2,128)}, u32[]{:S(2)}) copy-start(f32[2,2,2,2,256]{4,3,2,1,0:T(2,128)} %get-tuple-element.69) | copy-start | bytes 49156
  106.3 2.2 %copy-start.20 = (f32[2,2,2,2,256]{4,3,2,1,0:T(2,128)S(1)}, f32[2,2,2,2,256]{4,3,2,1,0:T(2,128)}, u32[]{:S(2)}) copy-start(f32[2,2,2,2,256]{4,3,2,1,0:T(2,128)} %get-tuple-element.71) | copy-start | bytes 49156
  106.3 2.2 %copy-start.21 = (f32[2,2,2,2,256]{4,3,2,1,0:T(2,128)S(1)}, f32[2,2,2,2,256]{4,3,2,1,0:T(2,128)}, u32[]{:S(2)}) copy-start(f32[2,2,2,2,256]{4,3,2,1,0:T(2,128)} %get-tuple-element.74) | copy-start | bytes 49156
  106.3 2.1 %copy-start.22 = (f32[2,2,2,2,256]{4,3,2,1,0:T(2,128)S(1)}, f32[2,2,2,2,256]{4,3,2,1,0:T(2,128)}, u32[]{:S(2)}) copy-start(f32[2,2,2,2,256]{4,3,2,1,0:T(2,128)} %get-tuple-element.76) | copy-start | bytes 49156
  108.5 1.4 %copy-start.9 = (f32[256,256,1,1,1]{1,0,4,3,2:T(8,128)S(1)}, f32[256,256,1,1,1]{1,0,4,3,2:T(8,128)}, u32[]{:S(2)}) copy-start(f32[256,256,1,1,1]{1,0,4,3,2:T(8,128)} %constant.116) | copy-start | bytes 786436
  109.9 2.6 %copy-start.15 = (f32[68,128]{1,0:T(8,128)S(1)}, f32[68,128]{1,0:T(8,128)}, u32[]{:S(2)}) copy-start(f32[68,128]{1,0:T(8,128)} %constant.109.clone) | copy-start | bytes 104452
  112.5 4.7 %copy-start.16 = (f32[68,128]{1,0:T(8,128)S(1)}, f32[68,128]{1,0:T(8,128)}, u32[]{:S(2)}) copy-start(f32[68,128]{1,0:T(8,128)} %constant.108.clone) | copy-start | bytes 104452

commit v4 on v3

--- a/solution.py
+++ b/solution.py
@@ -59,66 +59,77 @@
 EXCHANGE_IDS = [0]
 
 
-def exchange_kernel(size_x, size_y, *refs):
+def windows(offset, size, halo_len):
+    if offset == 1:
+        return size - halo_len, halo_len
+    if offset == -1:
+        return 0, halo_len
+    return 0, size
+
+
+def exchange_kernel(layouts, mesh_x, mesh_y, *refs):
     count = len(OFFSETS)
-    total = (len(refs) - 2) // 2
-    sources, targets = refs[:total], refs[total : 2 * total]
-    send_sem, recv_sem = refs[2 * total], refs[2 * total + 1]
+    arrays = len(layouts)
+    sources = refs[:arrays]
+    targets = refs[arrays : arrays + arrays * count]
+    send_sem, recv_sem = refs[arrays + arrays * count], refs[arrays + arrays * count + 1]
     me_x = lax.axis_index("gx")
     me_y = lax.axis_index("gy")
     peers = [
-        (lax.rem(me_x + np.int32(dx + size_x), np.int32(size_x)), lax.rem(me_y + np.int32(dy + size_y), np.int32(size_y)))
-        for dx, dy in OFFSETS
+        (lax.rem(me_x + np.int32(ox + mesh_x), np.int32(mesh_x)), lax.rem(me_y + np.int32(oy + mesh_y), np.int32(mesh_y)))
+        for ox, oy in OFFSETS
     ]
     barrier = pltpu.get_barrier_semaphore()
     for peer in peers:
         pl.semaphore_signal(barrier, inc=1, device_id=peer, device_id_type=pl.DeviceIdType.MESH)
     pl.semaphore_wait(barrier, count)
     copies = []
-    for slot in range(len(sources)):
-        peer = peers[slot % count]
-        copy = pltpu.make_async_remote_copy(
-            src_ref=sources[slot],
-            dst_ref=targets[slot],
-            send_sem=send_sem.at[slot],
-            recv_sem=recv_sem.at[slot],
-            device_id=peer,
-            device_id_type=pl.DeviceIdType.MESH,
-        )
-        copy.start()
-        copies.append(copy)
+    for n, (ndim, dx, hx, size_x, dy, hy, size_y) in enumerate(layouts):
+        for s, ((ox, oy), peer) in enumerate(zip(OFFSETS, peers)):
+            index = [slice(None)] * ndim
+            index[dx] = pl.ds(*windows(ox, size_x, hx))
+            index[dy] = pl.ds(*windows(oy, size_y, hy))
+            slot = n * count + s
+            copy = pltpu.make_async_remote_copy(
+                src_ref=sources[n].at[tuple(index)],
+                dst_ref=targets[slot],
+                send_sem=send_sem.at[slot],
+                recv_sem=recv_sem.at[slot],
+                device_id=peer,
+                device_id_type=pl.DeviceIdType.MESH,
+            )
+            copy.start()
+            copies.append(copy)
     for copy in copies:
         copy.wait()
 
 
-def exchange(pieces):
+def piece_shape(array, dx, hx, dy, hy, offset):
+    shape = list(array.shape)
+    shape[dx] = windows(offset[0], shape[dx], hx)[1]
+    shape[dy] = windows(offset[1], shape[dy], hy)[1]
+    return jax.ShapeDtypeStruct(tuple(shape), array.dtype)
+
+
+def halos(requests):
     cid = EXCHANGE_IDS[0]
     EXCHANGE_IDS[0] += 1
-    count = len(pieces)
-    return pl.pallas_call(
-        functools.partial(exchange_kernel, lax.axis_size("gx"), lax.axis_size("gy")),
-        out_shape=[jax.ShapeDtypeStruct(p.shape, p.dtype) for p in pieces],
-        in_specs=[pl.BlockSpec(memory_space=pl.ANY)] * count,
-        out_specs=[pl.BlockSpec(memory_space=pl.ANY)] * count,
-        scratch_shapes=[pltpu.SemaphoreType.DMA((count,)), pltpu.SemaphoreType.DMA((count,))],
+    count = len(OFFSETS)
+    layouts = tuple(
+        (array.ndim, dx, hx, array.shape[dx], dy, hy, array.shape[dy]) for array, dx, hx, dy, hy in requests
+    )
+    shapes = [piece_shape(array, dx, hx, dy, hy, offset) for array, dx, hx, dy, hy in requests for offset in OFFSETS]
+    received = pl.pallas_call(
+        functools.partial(exchange_kernel, layouts, lax.axis_size("gx"), lax.axis_size("gy")),
+        out_shape=shapes,
+        in_specs=[pl.BlockSpec(memory_space=pl.ANY)] * len(requests),
+        out_specs=[pl.BlockSpec(memory_space=pl.ANY)] * len(shapes),
+        scratch_shapes=[pltpu.SemaphoreType.DMA((len(shapes),)), pltpu.SemaphoreType.DMA((len(shapes),))],
         compiler_params=pltpu.CompilerParams(collective_id=cid, has_side_effects=True),
-    )(*pieces)
-
-
-def halo_pieces(array, dx, hx, dy, hy):
-    size_x, size_y = array.shape[dx], array.shape[dy]
-    cut = lax.slice_in_dim
-    last_x = cut(array, size_x - hx, size_x, axis=dx)
-    first_x = cut(array, 0, hx, axis=dx)
+    )(*[request[0] for request in requests])
     return [
-        last_x,
-        first_x,
-        cut(array, size_y - hy, size_y, axis=dy),
-        cut(array, 0, hy, axis=dy),
-        cut(last_x, size_y - hy, size_y, axis=dy),
-        cut(last_x, 0, hy, axis=dy),
-        cut(first_x, size_y - hy, size_y, axis=dy),
-        cut(first_x, 0, hy, axis=dy),
+        assemble(array, dx, dy, received[n * count : (n + 1) * count])
+        for n, (array, dx, hx, dy, hy) in enumerate(requests)
     ]
 
 
@@ -128,18 +139,6 @@
     mid = jnp.concatenate([before_y, array, after_y], axis=dy)
     bottom = jnp.concatenate([corner_ab, after_x, corner_aa], axis=dy)
     return jnp.concatenate([top, mid, bottom], axis=dx)
-
-
-def halos(requests):
-    pieces = []
-    for array, dx, hx, dy, hy in requests:
-        pieces += halo_pieces(array, dx, hx, dy, hy)
-    received = exchange(pieces)
-    count = len(OFFSETS)
-    return [
-        assemble(array, dx, dy, received[n * count : (n + 1) * count])
-        for n, (array, dx, hx, dy, hy) in enumerate(requests)
-    ]
 
 
 def halo(array, dx, hx, dy, hy):

time: 133 us -> 122 us (0.917)
  local copies, waits for them, and re-layouts: 27.1 us -> 15.7 us
    slice x10 -> x0, local copies, waits for them, and re-layouts: 12 us -> none  [the longest x3 4.73 us: halo_pieces(): first_x = cut(array, 0, hx, axis=dx)]
    unnamed x64 -> x62, local copies, waits for them, and re-layouts: 2.97 us -> 3.61 us
where the time goes in v4:
time: 122 us; the launch traced here: 121 us
  Pallas kernels  46.5 us (38%)
  matrix products  43.1 us (35%)
  local copies, waits for them, and re-layouts  15.7 us (13%)
  other arithmetic  15.2 us (12%)
    pallas_call x3, Pallas kernels, halos(): pl.pallas_call(functools.partial(exchange_kernel, layouts, lax.axis_size(...  46.5 us
    dot_general x15, matrix products, contract(): lax.dot_general(left, right, (dims, batch), precision=PREC, preferred_ele...  43.1 us
    concatenate x3, other arithmetic, assemble(): return jnp.concatenate([top, mid, bottom], axis=dx)  5.64 us
    another operation x3, local copies, waits for them, and re-layouts, synthesise_lead(): joined = jnp.stack([even, odd], axis=1)  5.42 us
    another operation x6, other arithmetic, synthesise_lead(): joined = jnp.stack([even, odd], axis=1)  5.37 us
    unnamed x62, local copies, waits for them, and re-layouts  3.61 us
    scatter x1, local copies, waits for them, and re-layouts, local(): recon1 = synthesis_ext(shrunk1.at[0, :, 0, :, :half_z].set(recon2))  3.46 us
    add x3, other arithmetic, analyse_lead(): low = low + filt_low[j] * taken  3.26 us

profile of v4, /device:TPU:8, one launch (start us, length us, event | category | flops | bytes accessed | tf_op | source)
XLA Modules:
  0.0 121.2 jit_solution(18160595588103001369)
XLA Ops:
  0.0 16.7 %shard_map.172 = (f32[3,128,256]{2,1,0:T(8,128)}, f32[3,128,256]{2,1,0:T(8,128)}, f32[32,3,256]{2,1,0:T(4,128)}, f32[32,3,256]{2,1,0:T(4,128)}, f32[3,3,256]{2,1...) custom-call(f32[32,128,256]{2,1,0:T(8,128)} %refs_0_.1), custom_call_target="tpu_custom_call" | custom-call | tf_op jit(solution)/shard_map/pallas_call | solution.py:122
  16.8 3.2 %maximum_maximum_fusion.1 = f32[38,134,256]{2,1,0:T(8,128)S(1)} fusion(f32[3,3,256]{2,1,0:T(4,128)} %get-tuple-element.68, f32[3,128,256]{2,1,0:T(8,128)} %get-tuple-element.67, f32[3,3,256]{2,1,0:T(4,128)} %get-tuple-element.66, f32[32,3,256]{2,1,0:T(4,128)} %get-tuple-element.65, f32[32,128,256]{2,1,0:T(8,128)} %refs_0_.1, ...), kind=kLoop, calls=%fused_computation.8 | loop fusion | flops 10428416 | bytes 10428416 | tf_op jit(solution)/shard_map/concatenate | solution.py:141
  20.0 0.7 copy-done
  20.6 0.0 copy-done.4
  20.7 0.5 pad_maximum_fusion
  21.2 0.0 copy-start.11
  21.2 2.5 %multiply_add_fusion.1 = (f32[16,134,256]{2,1,0:T(8,128)S(1)}, f32[16,134,256]{2,1,0:T(8,128)S(1)}) fusion(f32[38,134,256]{2,1,0:T(8,128)S(1)} %maximum_maximum_fusion.1, f32[32,134,256]{2,1,0:T(8,128)S(1)} %pad_maximum_fusion), kind=kLoop, calls=%fused_computation.29 | loop fusion | flops 16465920 | bytes 21954560 | tf_op jit(solution)/shard_map/add | solution.py:165
  23.7 0.0 copy-start.27
  23.8 3.8 %fusion = f32[32,128,256]{2,1,0:T(8,128)S(1)} fusion(f32[16,134,256]{2,1,0:T(8,128)S(1)} %get-tuple-element.97, f32[16,134,256]{2,1,0:T(8,128)S(1)} %get-tuple-element.96, f32[134,128]{1,0:T(8,128)S(1)} %copy-done.11), kind=kOutput, calls=%fused_computation.11 | convolution fusion | flops 844152832 | bytes 8653824 | tf_op jit(solution)/shard_map/dot_general | solution.py:149
  27.6 0.2 select_reduce_fusion
  27.8 0.7 fusion.75
  28.5 0.1 broadcast_add_fusion.1
  28.5 10.3 %maximum_multiply_fusion = (f32[32,128,256]{2,1,0:T(8,128)}, f32[32,128,256]{2,1,0:T(8,128)S(1)}) fusion(f32[]{:T(128)} %bitcast.8, f32[]{:T(128)} %bitcast.7, f32[]{:T(128)} %bitcast.6, f32[]{:T(128)} %bitcast.5, f32[]{:T(128)} %bitcast.4, f32[]{:T(128)} %bitcast.3, f32[]{:T(128)} %bitcast.2, s32[256]{0:T(256)S(1)} %compare_convert_fusion.1, ...), kind=kOutput, calls=%fused_computation.16 | convolution fusion | flops 1631584256 | bytes 12862492 | tf_op jit(solution)/shard_map/dot_general | solution.py:149
  38.8 0.8 slice.486.refs_0_
  39.6 19.0 %shard_map.173 = (f32[9,64,128]{2,1,0:T(8,128)}, f32[9,64,128]{2,1,0:T(8,128)}, f32[16,9,128]{2,1,0:T(8,128)}, f32[16,9,128]{2,1,0:T(8,128)}, f32[9,9,128]{2,1,0...) custom-call(f32[16,64,128]{2,1,0:T(8,128)} %slice.486.refs_0_, ...), custom_call_target="tpu_custom_call" | custom-call | tf_op jit(solution)/shard_map/pallas_call | solution.py:122
  58.6 1.4 %maximum_maximum_fusion.2 = f32[34,82,128]{2,1,0:T(8,128)S(1)} fusion(f32[9,9,128]{2,1,0:T(8,128)} %get-tuple-element.84, f32[9,64,128]{2,1,0:T(8,128)} %get-tuple-element.83, f32[9,9,128]{2,1,0:T(8,128)} %get-tuple-element.82, f32[16,9,128]{2,1,0:T(8,128)} %get-tuple-element.81, f32[16,64,128]{2,1,0:T(8,128)S(1)} %copy-done.2, ...), kind=kLoop, calls=%fused_computation.42 | loop fusion | flops 2854912 | bytes 2854912 | tf_op jit(solution)/shard_map/concatenate | solution.py:141
  60.0 0.0 copy-start.13
  60.1 0.7 multiply_add_fusion.3
  60.7 0.0 copy-start.28
  60.7 0.1 copy-done.13
  60.8 0.7 fusion.15
  61.5 0.7 fusion.73
  62.2 0.1 broadcast_add_fusion
  62.3 0.0 copy-start.30
  62.3 6.0 %maximum_multiply_fusion.1 = (f32[28,76,128]{2,1,0:T(8,128)S(1)}, f32[28,76,128]{2,1,0:T(8,128)S(1)}) fusion(f32[]{:T(128)} %bitcast.18, f32[]{:T(128)} %bitcast.17, f32[]{:T(128)} %bitcast.16, f32[]{:T(128)} %bitcast.15, f32[]{:T(128)} %bitcast.14, f32[]{:T(128)} %bitcast.13, f32[]{:T(128)} %bitcast.12, s32[128]{0:T(128)S(1)} %compare_convert_fusion.2, ...), kind=kOutput, calls=%fused_computation.51 | convolution fusion | flops 214638592 | bytes 3343196 | tf_op jit(solution)/shard_map/dot_general | solution.py:149
  68.3 0.0 copy-start.29
  68.4 0.0 copy-start.24
  68.4 0.1 multiply_add_fusion.5
  68.5 0.2 fusion.62
  68.7 0.0 copy-start.23
  68.8 0.1 broadcast_add_fusion.2
  68.8 4.7 %maximum_multiply_fusion.2 = (f32[8,32,64]{2,1,0:T(8,128)S(1)}, f32[8,32,64]{2,1,0:T(8,128)S(1)}) fusion(f32[]{:T(128)} %bitcast.27, f32[]{:T(128)} %bitcast.26, f32[]{:T(128)} %bitcast.25, f32[]{:T(128)} %bitcast.24, f32[]{:T(128)} %bitcast.23, f32[]{:T(128)} %bitcast.22, f32[]{:T(128)} %bitcast.21, s32[64]{0:T(128)S(1)} %compare_convert_fusion, ...), kind=kOutput, calls=%fused_computation.124 | convolution fusion | flops 6619136 | bytes 214300 | tf_op jit(solution)/shard_map/dot_general | solution.py:149
  73.5 0.8 dynamic_update_slice.3
  74.4 0.6 copy-done.10
  75.0 10.8 %shard_map.174 = (f32[2,4,2,16,64]{4,3,2,1,0:T(8,128)}, f32[2,4,2,16,64]{4,3,2,1,0:T(8,128)}, f32[2,4,2,4,64]{4,3,2,1,0:T(4,128)}, f32[2,4,2,4,64]{4,3,2,1,0:T(4...) custom-call(f32[2,4,2,16,64]{4,3,2,1,0:T(8,128)} %bitcast.120), custom_call_target="tpu_custom_call" | custom-call | tf_op jit(solution)/shard_map/pallas_call | solution.py:122
  85.8 1.6 %fusion.23 = f32[2,12,2,24,64]{4,3,2,1,0:T(8,128)S(1)} fusion(f32[64,64,1,1,1]{1,0,4,3,2:T(8,128)S(1)} %copy-done.29, f32[2,4,2,4,64]{4,3,2,1,0:T(4,128)} %get-tuple-element.92, f32[2,4,2,16,64]{4,3,2,1,0:T(8,128)} %get-tuple-element.91, f32[2,4,2,4,64]{4,3,2,1,0:T(4,128)} %get-tuple-element.90, f32[2,4,2,4,64]{4,3,2,1,0:T(4,128)} %get-tuple-element.89, ...), kind=kOutput, calls=%fused_computation.58 | convolution fusion | flops 28901376 | bytes 606208 | tf_op jit(solution)/shard_map/dot_general | solution.py:149
  87.4 0.6 fusion.51
  88.0 0.6 fusion.19
  88.7 0.2 fusion.61
  88.8 0.0 copy-start.12
  88.9 0.0 copy-start.16
  89.0 0.1 reshape.284
  89.1 0.0 copy-start.17
  89.1 3.5 %scatter.6 = f32[2,14,2,38,128]{4,3,2,1,0:T(8,128)S(1)} dynamic-update-slice(f32[2,14,2,38,128]{4,3,2,1,0:T(8,128)S(1)} %reshape.284, f32[1,14,1,38,64]{4,3,2,1,0:T(8,128)S(1)} %slice_bitcast_fusion.14, s32[]{:T(128)} %constant.85.clone.1, s32[]{:T(128)} %constant.85.clone.1, s32[]{:T(128)} %constant.85.clone.1, s32[]{:T(128)} %constant.85.clone.1, s32[]{:T(128)} %constant.85.clone.1) | dynamic-update-slice | bytes 272388 | tf_op jit(solution)/shard_map/scatter | solution.py:244
  92.5 0.6 fusion.76
  93.2 1.1 fusion.41
  94.3 1.1 fusion.14
  95.3 0.4 fusion.50
  95.8 0.1 pad_maximum_fusion.2
  95.9 1.6 %copy-done.1 = f32[32,128,256]{2,1,0:T(8,128)S(1)} copy-done((f32[32,128,256]{2,1,0:T(8,128)S(1)}, f32[32,128,256]{2,1,0:T(8,128)}, u32[]{:S(2)}) %copy-start.1) | copy-done | bytes 4194328
  97.5 0.2 copy-done.5
  97.7 0.2 copy-done.6
  97.9 0.0 copy-done.8
  97.9 0.0 copy-done.9
  98.0 0.0 copy-start.7
  98.0 1.1 maximum_maximum_fusion
  99.0 0.1 constant_dynamic-update-slice_fusion
  99.1 0.0 copy-start.14
  99.1 2.6 %fusion.77 = f32[2,20,2,68,256]{4,3,2,1,0:T(8,128)S(1)} fusion(f32[2,20,2,68,256]{4,3,2,1,0:T(8,128)S(1)} %constant_dynamic-update-slice_fusion, f32[256,256,1,1,1]{1,0,4,3,2:T(8,128)S(1)} %copy-done.7), kind=kOutput, calls=%fused_computation.158 | convolution fusion | flops 2139095040 | bytes 11403264 | tf_op jit(solution)/shard_map/dot_general | solution.py:149
  101.8 4.7 %fusion.4 = f32[40,256,128]{2,1,0:T(8,128)S(1)} fusion(f32[40,2,68,256]{3,2,1,0:T(8,128)S(1)} %bitcast.110, f32[68,128]{1,0:T(8,128)S(1)} %copy-done.14), kind=kOutput, calls=%fused_computation.25 | convolution fusion | flops 534773760 | bytes 8228864 | tf_op jit(solution)/shard_map/dot_general | solution.py:149
  106.5 4.7 %add_bitcast_fusion = f32[40,128,256]{1,2,0:T(8,128)S(1)} fusion(f32[40,256,128]{2,1,0:T(8,128)S(1)} %fusion.4, f32[40,2,68,256]{3,2,1,0:T(8,128)S(1)} %bitcast.111, f32[68,128]{1,0:T(8,128)S(1)} %copy-done.15), kind=kOutput, calls=%fused_computation.9 | convolution fusion | flops 536084480 | bytes 13471744 | tf_op jit(solution)/shard_map/dot_general | solution.py:149
  111.2 2.3 %fusion.13 = (f32[16,1,128,256]{2,3,0,1:T(8,128)S(1)}, f32[16,1,128,256]{2,3,0,1:T(8,128)S(1)}) fusion(f32[40,128,256]{1,2,0:T(8,128)S(1)} %add_bitcast_fusion), kind=kLoop, calls=%fused_computation.40 | loop fusion | flops 15728640 | bytes 25165824 | tf_op jit(solution)/shard_map/stack | solution.py:184
  113.5 2.4 %pad_maximum_fusion.1 = f32[16,2,128,256]{2,3,0,1:T(8,128)} fusion(f32[16,1,128,256]{2,3,0,1:T(8,128)S(1)} %get-tuple-element.99, f32[16,1,128,256]{2,3,0,1:T(8,128)S(1)} %get-tuple-element.98), kind=kLoop, calls=%fused_computation.15 | loop fusion | flops 1048576 | bytes 8388608 | tf_op jit(solution)/shard_map/stack | solution.py:184
  115.9 5.3 %copy.43 = f32[16,2,128,256]{3,2,1,0:T(8,128)} copy(f32[16,2,128,256]{2,3,0,1:T(8,128)} %pad_maximum_fusion.1) | data formatting | bytes 8388608 | tf_op jit(solution)/shard_map/stack | solution.py:184
  (56 shorter events, 0.3 us)
Async XLA Ops:
  16.7 3.9 %copy-start = (f32[32,128,256]{2,1,0:T(8,128)S(1)}, f32[32,128,256]{2,1,0:T(8,128)}, u32[]{:S(2)}) copy-start(f32[32,128,256]{2,1,0:T(8,128)} %refs_0_.1) | copy-start | bytes 12582916
  16.7 3.9 %copy-start.3 = (f32[32,3,256]{2,1,0:T(4,128)S(1)}, f32[32,3,256]{2,1,0:T(4,128)}, u32[]{:S(2)}) copy-start(f32[32,3,256]{2,1,0:T(4,128)} %get-tuple-element.64) | copy-start | bytes 294916
  16.8 3.9 %copy-start.4 = (f32[32,3,256]{2,1,0:T(4,128)S(1)}, f32[32,3,256]{2,1,0:T(4,128)}, u32[]{:S(2)}) copy-start(f32[32,3,256]{2,1,0:T(4,128)} %get-tuple-element.65) | copy-start | bytes 294916
  21.2 2.5 %copy-start.11 = (f32[134,128]{1,0:T(8,128)S(1)}, f32[134,128]{1,0:T(8,128)}, u32[]{:S(2)}) copy-start(f32[134,128]{1,0:T(8,128)} %constant.98.clone) | copy-start | bytes 205828
  23.7 3.8 %copy-start.25 = (s32[3,7]{1,0:T(4,128)S(1)}, s32[3,7]{1,0:T(4,128)}, u32[]{:S(2)}) copy-start(s32[3,7]{1,0:T(4,128)} %param.24) | copy-start | bytes 256
  23.7 3.8 %copy-start.26 = (f32[16]{0:T(128)S(1)}, f32[16]{0:T(128)}, u32[]{:S(2)}) copy-start(f32[16]{0:T(128)} %param.23) | copy-start | bytes 196
  23.7 4.8 %copy-start.27 = (f32[256,256,1]{1,0,2:T(8,128)S(1)}, f32[256,256,1]{1,0,2:T(8,128)}, u32[]{:S(2)}) copy-start(f32[256,256,1]{1,0,2:T(8,128)} %constant.111) | copy-start | bytes 786436
  39.6 19.0 %copy-start.2 = (f32[16,64,128]{2,1,0:T(8,128)S(1)}, f32[16,64,128]{2,1,0:T(8,128)}, u32[]{:S(2)}) copy-start(f32[16,64,128]{2,1,0:T(8,128)} %slice.486.refs_0_) | copy-start | bytes 1572868
  60.0 0.8 copy-start.13
  60.7 1.6 %copy-start.28 = (f32[128,128,1]{1,0,2:T(8,128)S(1)}, f32[128,128,1]{1,0,2:T(8,128)}, u32[]{:S(2)}) copy-start(f32[128,128,1]{1,0,2:T(8,128)} %constant.112) | copy-start | bytes 196612
  62.3 6.2 %copy-start.22 = (f32[38,32]{0,1:T(8,128)S(1)}, f32[38,32]{0,1:T(8,128)}, u32[]{:S(2)}) copy-start(f32[38,32]{0,1:T(8,128)} %constant.102.clone) | copy-start | bytes 14596
  62.3 6.5 %copy-start.30 = (f32[64,64,1]{1,0,2:T(8,128)S(1)}, f32[64,64,1]{1,0,2:T(8,128)}, u32[]{:S(2)}) copy-start(f32[64,64,1]{1,0,2:T(8,128)} %constant.113) | copy-start | bytes 49156
  68.3 17.5 %copy-start.29 = (f32[64,64,1,1,1]{1,0,4,3,2:T(8,128)S(1)}, f32[64,64,1,1,1]{1,0,4,3,2:T(8,128)}, u32[]{:S(2)}) copy-start(f32[64,64,1,1,1]{1,0,4,3,2:T(8,128)} %constant.114) | copy-start | bytes 49156
  68.4 19.0 %copy-start.24 = (f32[24,40]{1,0:T(8,128)S(1)}, f32[24,40]{1,0:T(8,128)}, u32[]{:S(2)}) copy-start(f32[24,40]{1,0:T(8,128)} %constant.104.clone) | copy-start | bytes 11524
  68.7 19.3 %copy-start.23 = (f32[24,40]{1,0:T(8,128)S(1)}, f32[24,40]{1,0:T(8,128)}, u32[]{:S(2)}) copy-start(f32[24,40]{1,0:T(8,128)} %constant.105.clone) | copy-start | bytes 11524
  74.3 0.7 copy-start.10
  88.8 3.7 %copy-start.12 = (f32[128,128,1,1,1]{1,0,4,3,2:T(8,128)S(1)}, f32[128,128,1,1,1]{1,0,4,3,2:T(8,128)}, u32[]{:S(2)}) copy-start(f32[128,128,1,1,1]{1,0,4,3,2:T(8,128)} %constant.115) | copy-start | bytes 196612
  88.9 4.2 %copy-start.16 = (f32[38,68]{1,0:T(8,128)S(1)}, f32[38,68]{1,0:T(8,128)}, u32[]{:S(2)}) copy-start(f32[38,68]{1,0:T(8,128)} %constant.106.clone) | copy-start | bytes 31012
  89.1 5.2 %copy-start.17 = (f32[38,68]{1,0:T(8,128)S(1)}, f32[38,68]{1,0:T(8,128)}, u32[]{:S(2)}) copy-start(f32[38,68]{1,0:T(8,128)} %constant.107.clone) | copy-start | bytes 31012
  95.3 2.2 %copy-start.1 = (f32[32,128,256]{2,1,0:T(8,128)S(1)}, f32[32,128,256]{2,1,0:T(8,128)}, u32[]{:S(2)}) copy-start(f32[32,128,256]{2,1,0:T(8,128)} %get-tuple-element.132) | copy-start | bytes 12582916
  95.7 2.0 %copy-start.5 = (f32[2,2,2,64,256]{4,3,2,1,0:T(8,128)S(1)}, f32[2,2,2,64,256]{4,3,2,1,0:T(8,128)}, u32[]{:S(2)}) copy-start(f32[2,2,2,64,256]{4,3,2,1,0:T(8,128)} %get-tuple-element.70) | copy-start | bytes 1572868
  95.7 2.1 %copy-start.6 = (f32[2,2,2,64,256]{4,3,2,1,0:T(8,128)S(1)}, f32[2,2,2,64,256]{4,3,2,1,0:T(8,128)}, u32[]{:S(2)}) copy-start(f32[2,2,2,64,256]{4,3,2,1,0:T(8,128)} %get-tuple-element.75) | copy-start | bytes 1572868
  95.8 2.1 %copy-start.8 = (f32[2,16,2,2,256]{4,3,2,1,0:T(2,128)S(1)}, f32[2,16,2,2,256]{4,3,2,1,0:T(2,128)}, u32[]{:S(2)}) copy-start(f32[2,16,2,2,256]{4,3,2,1,0:T(2,128)} %get-tuple-element.72) | copy-start | bytes 393220
  95.8 2.2 %copy-start.9 = (f32[2,16,2,2,256]{4,3,2,1,0:T(2,128)S(1)}, f32[2,16,2,2,256]{4,3,2,1,0:T(2,128)}, u32[]{:S(2)}) copy-start(f32[2,16,2,2,256]{4,3,2,1,0:T(2,128)} %get-tuple-element.73) | copy-start | bytes 393220
  95.8 2.2 %copy-start.18 = (f32[2,2,2,2,256]{4,3,2,1,0:T(2,128)S(1)}, f32[2,2,2,2,256]{4,3,2,1,0:T(2,128)}, u32[]{:S(2)}) copy-start(f32[2,2,2,2,256]{4,3,2,1,0:T(2,128)} %get-tuple-element.69) | copy-start | bytes 49156
  95.8 2.2 %copy-start.19 = (f32[2,2,2,2,256]{4,3,2,1,0:T(2,128)S(1)}, f32[2,2,2,2,256]{4,3,2,1,0:T(2,128)}, u32[]{:S(2)}) copy-start(f32[2,2,2,2,256]{4,3,2,1,0:T(2,128)} %get-tuple-element.71) | copy-start | bytes 49156
  95.8 2.2 %copy-start.20 = (f32[2,2,2,2,256]{4,3,2,1,0:T(2,128)S(1)}, f32[2,2,2,2,256]{4,3,2,1,0:T(2,128)}, u32[]{:S(2)}) copy-start(f32[2,2,2,2,256]{4,3,2,1,0:T(2,128)} %get-tuple-element.74) | copy-start | bytes 49156
  95.8 2.1 %copy-start.21 = (f32[2,2,2,2,256]{4,3,2,1,0:T(2,128)S(1)}, f32[2,2,2,2,256]{4,3,2,1,0:T(2,128)}, u32[]{:S(2)}) copy-start(f32[2,2,2,2,256]{4,3,2,1,0:T(2,128)} %get-tuple-element.76) | copy-start | bytes 49156
  98.0 1.2 copy-start.7
  99.1 2.6 %copy-start.14 = (f32[68,128]{1,0:T(8,128)S(1)}, f32[68,128]{1,0:T(8,128)}, u32[]{:S(2)}) copy-start(f32[68,128]{1,0:T(8,128)} %constant.109.clone) | copy-start | bytes 104452
  101.8 4.7 %copy-start.15 = (f32[68,128]{1,0:T(8,128)S(1)}, f32[68,128]{1,0:T(8,128)}, u32[]{:S(2)}) copy-start(f32[68,128]{1,0:T(8,128)} %constant.108.clone) | copy-start | bytes 104452

commit v5 on v4

--- a/solution.py
+++ b/solution.py
@@ -218,6 +218,77 @@
     return synthesise_lead(y_part[0], y_part[1])
 
 
+def split_bf16(values):
+    high = values.astype(jnp.bfloat16)
+    low = (values - high.astype(jnp.float32)).astype(jnp.bfloat16)
+    return high, low
+
+
+def synth_yx_kernel(matrix_ref, in_ref, out_ref, rows_ref):
+    n_rows = in_ref.shape[0]
+    hx4 = n_rows // 2
+    half = hx4 - 4
+
+    def y_row(r, carry):
+        total = None
+        for band in range(2):
+            high, low = split_bf16(in_ref[r, band])
+            m_high = matrix_ref[band, 0]
+            m_low = matrix_ref[band, 1]
+            part = jnp.dot(m_high, high, preferred_element_type=jnp.float32)
+            part = part + jnp.dot(m_high, low, preferred_element_type=jnp.float32)
+            part = part + jnp.dot(m_low, high, preferred_element_type=jnp.float32)
+            total = part if total is None else total + part
+        rows_ref[r] = total
+        return carry
+
+    lax.fori_loop(0, n_rows, y_row, 0)
+
+    def x_row(q, carry):
+        even = None
+        odd = None
+        for j in range(8):
+            start = (3 - j) // 2 + 2 if j % 2 == 1 else (4 - j) // 2 + 2
+            term = filt_low[j] * rows_ref[q + start] + filt_high[j] * rows_ref[hx4 + q + start]
+            if j % 2 == 1:
+                even = term if even is None else even + term
+            else:
+                odd = term if odd is None else odd + term
+        out_ref[2 * q] = even
+        out_ref[2 * q + 1] = odd
+        return carry
+
+    lax.fori_loop(0, half, x_row, 0)
+
+
+def synthesis_yx(z_part, size_y):
+    n_rows, _, hy4, size_z = z_part.shape
+    matrix = split_synthesis(size_y)
+    turned = np.ascontiguousarray(np.transpose(matrix, (0, 2, 1)))
+    m_high = turned.astype(jnp.bfloat16)
+    m_low = (turned - m_high.astype(np.float32)).astype(jnp.bfloat16)
+    parts = jnp.asarray(np.stack([m_high, m_low], axis=1))
+    block_z = 128
+    size_x = 2 * (n_rows // 2 - 4)
+    return pl.pallas_call(
+        synth_yx_kernel,
+        grid=(size_z // block_z,),
+        in_specs=[
+            pl.BlockSpec(parts.shape, lambda i: (0, 0, 0, 0)),
+            pl.BlockSpec((n_rows, 2, hy4, block_z), lambda i: (0, 0, 0, i)),
+        ],
+        out_specs=pl.BlockSpec((size_x, size_y, block_z), lambda i: (0, 0, i)),
+        out_shape=jax.ShapeDtypeStruct((size_x, size_y, size_z), jnp.float32),
+        scratch_shapes=[pltpu.VMEM((n_rows, size_y, block_z), jnp.float32)],
+    )(parts, z_part)
+
+
+def synthesis_level0(extended):
+    two, hx4, _, hy4, size_z = extended.shape
+    z_part = contract(extended, jnp.asarray(periodic_analysis(size_z)), ((4,), (1,)), ((), ()))
+    return synthesis_yx(z_part.reshape(2 * hx4, 2, hy4, size_z), 2 * (hy4 - 4))
+
+
 def blocked(cube):
     size_x, size_y, size_z = cube.shape
     return cube.reshape(2, size_x // 2, 2, size_y // 2, size_z)
@@ -243,7 +314,7 @@
     half_z = shrunk1.shape[4] // 2
     recon1 = synthesis_ext(shrunk1.at[0, :, 0, :, :half_z].set(recon2))
     half_z = ext0.shape[4] // 2
-    return synthesis_ext(ext0.at[0, :, 0, :, :half_z].set(recon1))
+    return synthesis_level0(ext0.at[0, :, 0, :, :half_z].set(recon1))
 
 
 def solution(mesh):

time: 122 us -> 126 us (1.033)
  Pallas kernels: 46.5 us -> 67.8 us
  matrix products: 43.1 us -> 36.2 us
  local copies, waits for them, and re-layouts: 15.7 us -> 10.3 us
  other arithmetic: 15.2 us -> 10.6 us
    pallas_call x0 -> x1, Pallas kernels: none -> 21.3 us  [synthesis_yx(): pl.pallas_call(synth_yx_kernel, grid=(size_z // block_z,), in_specs=[pl.B...]
    dot_general x15 -> x13, matrix products: 43.1 us -> 36.2 us  [contract(): lax.dot_general(left, right, (dims, batch), precision=PREC, preferred_ele...]
    another operation x3 -> x2, local copies, waits for them, and re-layouts: 5.42 us -> 0.07 us  [synthesise_lead(): joined = jnp.stack([even, odd], axis=1)]
    another operation x6 -> x4, other arithmetic: 5.37 us -> 0.64 us  [synthesise_lead(): joined = jnp.stack([even, odd], axis=1)]
    unnamed x62 -> x58, local copies, waits for them, and re-layouts: 3.61 us -> 3.59 us
where the time goes in v5:
time: 126 us
  Pallas kernels  67.8 us (54%)
  matrix products  36.2 us (29%)
  other arithmetic  10.6 us (8%)
  local copies, waits for them, and re-layouts  10.3 us (8%)
    pallas_call x3, Pallas kernels, halos(): pl.pallas_call(functools.partial(exchange_kernel, layouts, lax.axis_size(...  46.5 us
    dot_general x13, matrix products, contract(): lax.dot_general(left, right, (dims, batch), precision=PREC, preferred_ele...  36.2 us
    pallas_call x1, Pallas kernels, synthesis_yx(): pl.pallas_call(synth_yx_kernel, grid=(size_z // block_z,), in_specs=[pl.B...  21.3 us
    concatenate x3, other arithmetic, assemble(): return jnp.concatenate([top, mid, bottom], axis=dx)  5.69 us
    unnamed x58, local copies, waits for them, and re-layouts  3.59 us
    scatter x1, local copies, waits for them, and re-layouts, local(): recon1 = synthesis_ext(shrunk1.at[0, :, 0, :, :half_z].set(recon2))  3.46 us
    add x3, other arithmetic, analyse_lead(): low = low + filt_low[j] * taken  3.26 us

profile of v5, /device:TPU:8, one launch (start us, length us, event | category | flops | bytes accessed | tf_op | source)
XLA Modules:
  0.0 125.6 jit_solution(811370536019473350)
XLA Ops:
  0.0 16.7 %shard_map.163 = (f32[3,128,256]{2,1,0:T(8,128)}, f32[3,128,256]{2,1,0:T(8,128)}, f32[32,3,256]{2,1,0:T(4,128)}, f32[32,3,256]{2,1,0:T(4,128)}, f32[3,3,256]{2,1...) custom-call(f32[32,128,256]{2,1,0:T(8,128)} %refs_0_.1), custom_call_target="tpu_custom_call" | custom-call | tf_op jit(solution)/shard_map/pallas_call | solution.py:122
  16.7 0.0 copy-start
  16.8 3.2 %maximum_maximum_fusion.1 = f32[38,134,256]{2,1,0:T(8,128)S(1)} fusion(f32[3,3,256]{2,1,0:T(4,128)} %get-tuple-element.68, f32[3,128,256]{2,1,0:T(8,128)} %get-tuple-element.67, f32[3,3,256]{2,1,0:T(4,128)} %get-tuple-element.66, f32[32,3,256]{2,1,0:T(4,128)} %get-tuple-element.65, f32[32,128,256]{2,1,0:T(8,128)} %refs_0_.1, ...), kind=kLoop, calls=%fused_computation.8 | loop fusion | flops 10428416 | bytes 10428416 | tf_op jit(solution)/shard_map/concatenate | solution.py:141
  20.0 0.7 copy-done
  20.6 0.0 copy-done.4
  20.7 0.5 pad_maximum_fusion
  21.2 0.0 copy-start.11
  21.2 2.5 %multiply_add_fusion.1 = (f32[16,134,256]{2,1,0:T(8,128)S(1)}, f32[16,134,256]{2,1,0:T(8,128)S(1)}) fusion(f32[38,134,256]{2,1,0:T(8,128)S(1)} %maximum_maximum_fusion.1, f32[32,134,256]{2,1,0:T(8,128)S(1)} %pad_maximum_fusion), kind=kLoop, calls=%fused_computation.23 | loop fusion | flops 16465920 | bytes 21954560 | tf_op jit(solution)/shard_map/add | solution.py:165
  23.7 0.0 copy-start.23
  23.7 0.0 copy-start.24
  23.7 0.0 copy-start.25
  23.8 3.8 %fusion = f32[32,128,256]{2,1,0:T(8,128)S(1)} fusion(f32[16,134,256]{2,1,0:T(8,128)S(1)} %get-tuple-element.97, f32[16,134,256]{2,1,0:T(8,128)S(1)} %get-tuple-element.96, f32[134,128]{1,0:T(8,128)S(1)} %copy-done.11), kind=kOutput, calls=%fused_computation.10 | convolution fusion | flops 844152832 | bytes 8653824 | tf_op jit(solution)/shard_map/dot_general | solution.py:149
  27.5 0.0 copy-done.23
  27.6 0.2 select_reduce_fusion
  27.8 0.7 fusion.63
  28.5 0.1 broadcast_add_fusion.1
  28.5 10.3 %maximum_multiply_fusion = (f32[32,128,256]{2,1,0:T(8,128)}, f32[32,128,256]{2,1,0:T(8,128)S(1)}) fusion(f32[]{:T(128)} %bitcast.8, f32[]{:T(128)} %bitcast.7, f32[]{:T(128)} %bitcast.6, f32[]{:T(128)} %bitcast.5, f32[]{:T(128)} %bitcast.4, f32[]{:T(128)} %bitcast.3, f32[]{:T(128)} %bitcast.2, s32[256]{0:T(256)S(1)} %compare_convert_fusion.1, ...), kind=kOutput, calls=%fused_computation.14 | convolution fusion | flops 1631584256 | bytes 12862492 | tf_op jit(solution)/shard_map/dot_general | solution.py:149
  38.9 0.8 slice.416.refs_0_
  39.7 19.0 %shard_map.164 = (f32[9,64,128]{2,1,0:T(8,128)}, f32[9,64,128]{2,1,0:T(8,128)}, f32[16,9,128]{2,1,0:T(8,128)}, f32[16,9,128]{2,1,0:T(8,128)}, f32[9,9,128]{2,1,0...) custom-call(f32[16,64,128]{2,1,0:T(8,128)} %slice.416.refs_0_, ...), custom_call_target="tpu_custom_call" | custom-call | tf_op jit(solution)/shard_map/pallas_call | solution.py:122
  58.7 1.4 %maximum_maximum_fusion.2 = f32[34,82,128]{2,1,0:T(8,128)S(1)} fusion(f32[9,9,128]{2,1,0:T(8,128)} %get-tuple-element.84, f32[9,64,128]{2,1,0:T(8,128)} %get-tuple-element.83, f32[9,9,128]{2,1,0:T(8,128)} %get-tuple-element.82, f32[16,9,128]{2,1,0:T(8,128)} %get-tuple-element.81, f32[16,64,128]{2,1,0:T(8,128)S(1)} %copy-done.2, ...), kind=kLoop, calls=%fused_computation.24 | loop fusion | flops 2854912 | bytes 2854912 | tf_op jit(solution)/shard_map/concatenate | solution.py:141
  60.1 0.0 copy-start.13
  60.1 0.7 multiply_add_fusion.3
  60.8 0.0 copy-start.26
  60.8 0.1 copy-done.13
  60.9 0.7 fusion.5
  61.5 0.7 fusion.61
  62.3 0.1 broadcast_add_fusion
  62.4 0.0 copy-start.28
  62.4 6.1 %maximum_multiply_fusion.1 = (f32[28,76,128]{2,1,0:T(8,128)S(1)}, f32[28,76,128]{2,1,0:T(8,128)S(1)}) fusion(f32[]{:T(128)} %bitcast.18, f32[]{:T(128)} %bitcast.17, f32[]{:T(128)} %bitcast.16, f32[]{:T(128)} %bitcast.15, f32[]{:T(128)} %bitcast.14, f32[]{:T(128)} %bitcast.13, f32[]{:T(128)} %bitcast.12, s32[128]{0:T(128)S(1)} %compare_convert_fusion.2, ...), kind=kOutput, calls=%fused_computation.33 | convolution fusion | flops 214638592 | bytes 3343196 | tf_op jit(solution)/shard_map/dot_general | solution.py:149
  68.4 0.0 copy-start.27
  68.5 0.0 copy-start.22
  68.5 0.1 multiply_add_fusion.5
  68.6 0.2 fusion.50
  68.8 0.0 copy-start.21
  68.9 0.1 broadcast_add_fusion.2
  68.9 4.6 %maximum_multiply_fusion.2 = (f32[8,32,64]{2,1,0:T(8,128)S(1)}, f32[8,32,64]{2,1,0:T(8,128)S(1)}) fusion(f32[]{:T(128)} %bitcast.27, f32[]{:T(128)} %bitcast.26, f32[]{:T(128)} %bitcast.25, f32[]{:T(128)} %bitcast.24, f32[]{:T(128)} %bitcast.23, f32[]{:T(128)} %bitcast.22, f32[]{:T(128)} %bitcast.21, s32[64]{0:T(128)S(1)} %compare_convert_fusion, ...), kind=kOutput, calls=%fused_computation.104 | convolution fusion | flops 6619136 | bytes 214300 | tf_op jit(solution)/shard_map/dot_general | solution.py:149
  73.6 0.8 dynamic_update_slice.3
  74.4 0.6 copy-done.10
  75.0 10.8 %shard_map.165 = (f32[2,4,2,16,64]{4,3,2,1,0:T(8,128)}, f32[2,4,2,16,64]{4,3,2,1,0:T(8,128)}, f32[2,4,2,4,64]{4,3,2,1,0:T(4,128)}, f32[2,4,2,4,64]{4,3,2,1,0:T(4...) custom-call(f32[2,4,2,16,64]{4,3,2,1,0:T(8,128)} %bitcast.100), custom_call_target="tpu_custom_call" | custom-call | tf_op jit(solution)/shard_map/pallas_call | solution.py:122
  85.9 1.6 %fusion.11 = f32[2,12,2,24,64]{4,3,2,1,0:T(8,128)S(1)} fusion(f32[64,64,1,1,1]{1,0,4,3,2:T(8,128)S(1)} %copy-done.27, f32[2,4,2,4,64]{4,3,2,1,0:T(4,128)} %get-tuple-element.92, f32[2,4,2,16,64]{4,3,2,1,0:T(8,128)} %get-tuple-element.91, f32[2,4,2,4,64]{4,3,2,1,0:T(4,128)} %get-tuple-element.90, f32[2,4,2,4,64]{4,3,2,1,0:T(4,128)} %get-tuple-element.89, ...), kind=kOutput, calls=%fused_computation.38 | convolution fusion | flops 28901376 | bytes 606208 | tf_op jit(solution)/shard_map/dot_general | solution.py:149
  87.5 0.6 fusion.39
  88.1 0.6 fusion.9
  88.7 0.2 fusion.49
  88.9 0.0 copy-start.12
  89.0 0.0 copy-start.14
  89.0 0.1 reshape.274
  89.1 0.0 copy-start.15
  89.1 3.5 %scatter.6 = f32[2,14,2,38,128]{4,3,2,1,0:T(8,128)S(1)} dynamic-update-slice(f32[2,14,2,38,128]{4,3,2,1,0:T(8,128)S(1)} %reshape.274, f32[1,14,1,38,64]{4,3,2,1,0:T(8,128)S(1)} %slice_bitcast_fusion.8, s32[]{:T(128)} %constant.84.clone.1, s32[]{:T(128)} %constant.84.clone.1, s32[]{:T(128)} %constant.84.clone.1, s32[]{:T(128)} %constant.84.clone.1, s32[]{:T(128)} %constant.84.clone.1) | dynamic-update-slice | bytes 272388 | tf_op jit(solution)/shard_map/scatter | solution.py:315
  92.6 0.6 fusion.64
  93.3 1.1 fusion.29
  94.3 1.1 fusion.4
  95.4 0.0 copy-start.1
  95.4 0.4 fusion.38
  95.9 0.1 pad_maximum_fusion.1
  96.0 1.6 %copy-done.1 = f32[32,128,256]{2,1,0:T(8,128)S(1)} copy-done((f32[32,128,256]{2,1,0:T(8,128)S(1)}, f32[32,128,256]{2,1,0:T(8,128)}, u32[]{:S(2)}) %copy-start.1) | copy-done | bytes 4194328
  97.6 0.2 copy-done.5
  97.8 0.2 copy-done.6
  97.9 0.0 copy-done.8
  98.0 0.0 copy-done.9
  98.0 0.0 copy-start.7
  98.0 1.1 maximum_maximum_fusion
  99.1 0.1 constant_dynamic-update-slice_fusion
  99.2 5.0 %fusion.65 = f32[2,20,2,68,256]{4,3,2,1,0:T(8,128)} fusion(f32[2,20,2,68,256]{4,3,2,1,0:T(8,128)S(1)} %constant_dynamic-update-slice_fusion, f32[256,256,1,1,1]{1,0,4,3,2:T(8,128)S(1)} %copy-done.7), kind=kOutput, calls=%fused_computation.138 | convolution fusion | flops 2139095040 | bytes 11403264 | tf_op jit(solution)/shard_map/dot_general | solution.py:149
  104.3 21.3 %shard_map.166 = f32[32,128,256]{2,1,0:T(8,128)} custom-call(bf16[2,2,128,68]{3,2,1,0:T(8,128)(2,1)} %constant.107.clone.matrix_ref, f32[40,2,68,256]{3,2,1,0:T(8,128)} %bitcast.91), custom_call_target="tpu_custom_call" | custom-call | tf_op jit(solution)/shard_map/pallas_call | solution.py:273
  (48 shorter events, 0.2 us)
Async XLA Ops:
  16.7 3.9 %copy-start = (f32[32,128,256]{2,1,0:T(8,128)S(1)}, f32[32,128,256]{2,1,0:T(8,128)}, u32[]{:S(2)}) copy-start(f32[32,128,256]{2,1,0:T(8,128)} %refs_0_.1) | copy-start | bytes 12582916
  16.7 3.9 %copy-start.3 = (f32[32,3,256]{2,1,0:T(4,128)S(1)}, f32[32,3,256]{2,1,0:T(4,128)}, u32[]{:S(2)}) copy-start(f32[32,3,256]{2,1,0:T(4,128)} %get-tuple-element.64) | copy-start | bytes 294916
  16.8 3.9 %copy-start.4 = (f32[32,3,256]{2,1,0:T(4,128)S(1)}, f32[32,3,256]{2,1,0:T(4,128)}, u32[]{:S(2)}) copy-start(f32[32,3,256]{2,1,0:T(4,128)} %get-tuple-element.65) | copy-start | bytes 294916
  21.2 2.5 %copy-start.11 = (f32[134,128]{1,0:T(8,128)S(1)}, f32[134,128]{1,0:T(8,128)}, u32[]{:S(2)}) copy-start(f32[134,128]{1,0:T(8,128)} %constant.97.clone) | copy-start | bytes 205828
  23.7 3.8 %copy-start.23 = (s32[3,7]{1,0:T(4,128)S(1)}, s32[3,7]{1,0:T(4,128)}, u32[]{:S(2)}) copy-start(s32[3,7]{1,0:T(4,128)} %param.23) | copy-start | bytes 256
  23.7 3.8 %copy-start.24 = (f32[16]{0:T(128)S(1)}, f32[16]{0:T(128)}, u32[]{:S(2)}) copy-start(f32[16]{0:T(128)} %param.22) | copy-start | bytes 196
  23.7 4.8 %copy-start.25 = (f32[256,256,1]{1,0,2:T(8,128)S(1)}, f32[256,256,1]{1,0,2:T(8,128)}, u32[]{:S(2)}) copy-start(f32[256,256,1]{1,0,2:T(8,128)} %constant.109) | copy-start | bytes 786436
  39.7 19.0 %copy-start.2 = (f32[16,64,128]{2,1,0:T(8,128)S(1)}, f32[16,64,128]{2,1,0:T(8,128)}, u32[]{:S(2)}) copy-start(f32[16,64,128]{2,1,0:T(8,128)} %slice.416.refs_0_) | copy-start | bytes 1572868
  60.1 0.8 copy-start.13
  60.8 1.6 %copy-start.26 = (f32[128,128,1]{1,0,2:T(8,128)S(1)}, f32[128,128,1]{1,0,2:T(8,128)}, u32[]{:S(2)}) copy-start(f32[128,128,1]{1,0,2:T(8,128)} %constant.110) | copy-start | bytes 196612
  62.4 6.2 %copy-start.20 = (f32[38,32]{0,1:T(8,128)S(1)}, f32[38,32]{0,1:T(8,128)}, u32[]{:S(2)}) copy-start(f32[38,32]{0,1:T(8,128)} %constant.101.clone) | copy-start | bytes 14596
  62.4 6.6 %copy-start.28 = (f32[64,64,1]{1,0,2:T(8,128)S(1)}, f32[64,64,1]{1,0,2:T(8,128)}, u32[]{:S(2)}) copy-start(f32[64,64,1]{1,0,2:T(8,128)} %constant.222) | copy-start | bytes 49156
  68.4 17.4 %copy-start.27 = (f32[64,64,1,1,1]{1,0,4,3,2:T(8,128)S(1)}, f32[64,64,1,1,1]{1,0,4,3,2:T(8,128)}, u32[]{:S(2)}) copy-start(f32[64,64,1,1,1]{1,0,4,3,2:T(8,128)} %constant.223) | copy-start | bytes 49156
  68.5 19.0 %copy-start.22 = (f32[24,40]{1,0:T(8,128)S(1)}, f32[24,40]{1,0:T(8,128)}, u32[]{:S(2)}) copy-start(f32[24,40]{1,0:T(8,128)} %constant.103.clone) | copy-start | bytes 11524
  68.8 19.3 %copy-start.21 = (f32[24,40]{1,0:T(8,128)S(1)}, f32[24,40]{1,0:T(8,128)}, u32[]{:S(2)}) copy-start(f32[24,40]{1,0:T(8,128)} %constant.104.clone) | copy-start | bytes 11524
  74.4 0.6 copy-start.10
  88.9 3.7 %copy-start.12 = (f32[128,128,1,1,1]{1,0,4,3,2:T(8,128)S(1)}, f32[128,128,1,1,1]{1,0,4,3,2:T(8,128)}, u32[]{:S(2)}) copy-start(f32[128,128,1,1,1]{1,0,4,3,2:T(8,128)} %constant.224) | copy-start | bytes 196612
  89.0 4.2 %copy-start.14 = (f32[38,68]{1,0:T(8,128)S(1)}, f32[38,68]{1,0:T(8,128)}, u32[]{:S(2)}) copy-start(f32[38,68]{1,0:T(8,128)} %constant.105.clone) | copy-start | bytes 31012
  89.1 5.2 %copy-start.15 = (f32[38,68]{1,0:T(8,128)S(1)}, f32[38,68]{1,0:T(8,128)}, u32[]{:S(2)}) copy-start(f32[38,68]{1,0:T(8,128)} %constant.106.clone) | copy-start | bytes 31012
  95.4 2.2 %copy-start.1 = (f32[32,128,256]{2,1,0:T(8,128)S(1)}, f32[32,128,256]{2,1,0:T(8,128)}, u32[]{:S(2)}) copy-start(f32[32,128,256]{2,1,0:T(8,128)} %get-tuple-element.130) | copy-start | bytes 12582916
  95.8 2.0 %copy-start.5 = (f32[2,2,2,64,256]{4,3,2,1,0:T(8,128)S(1)}, f32[2,2,2,64,256]{4,3,2,1,0:T(8,128)}, u32[]{:S(2)}) copy-start(f32[2,2,2,64,256]{4,3,2,1,0:T(8,128)} %get-tuple-element.70) | copy-start | bytes 1572868
  95.8 2.1 %copy-start.6 = (f32[2,2,2,64,256]{4,3,2,1,0:T(8,128)S(1)}, f32[2,2,2,64,256]{4,3,2,1,0:T(8,128)}, u32[]{:S(2)}) copy-start(f32[2,2,2,64,256]{4,3,2,1,0:T(8,128)} %get-tuple-element.75) | copy-start | bytes 1572868
  95.8 2.1 %copy-start.8 = (f32[2,16,2,2,256]{4,3,2,1,0:T(2,128)S(1)}, f32[2,16,2,2,256]{4,3,2,1,0:T(2,128)}, u32[]{:S(2)}) copy-start(f32[2,16,2,2,256]{4,3,2,1,0:T(2,128)} %get-tuple-element.72) | copy-start | bytes 393220
  95.8 2.2 %copy-start.9 = (f32[2,16,2,2,256]{4,3,2,1,0:T(2,128)S(1)}, f32[2,16,2,2,256]{4,3,2,1,0:T(2,128)}, u32[]{:S(2)}) copy-start(f32[2,16,2,2,256]{4,3,2,1,0:T(2,128)} %get-tuple-element.73) | copy-start | bytes 393220
  95.8 2.2 %copy-start.16 = (f32[2,2,2,2,256]{4,3,2,1,0:T(2,128)S(1)}, f32[2,2,2,2,256]{4,3,2,1,0:T(2,128)}, u32[]{:S(2)}) copy-start(f32[2,2,2,2,256]{4,3,2,1,0:T(2,128)} %get-tuple-element.69) | copy-start | bytes 49156
  95.8 2.2 %copy-start.17 = (f32[2,2,2,2,256]{4,3,2,1,0:T(2,128)S(1)}, f32[2,2,2,2,256]{4,3,2,1,0:T(2,128)}, u32[]{:S(2)}) copy-start(f32[2,2,2,2,256]{4,3,2,1,0:T(2,128)} %get-tuple-element.71) | copy-start | bytes 49156
  95.9 2.2 %copy-start.18 = (f32[2,2,2,2,256]{4,3,2,1,0:T(2,128)S(1)}, f32[2,2,2,2,256]{4,3,2,1,0:T(2,128)}, u32[]{:S(2)}) copy-start(f32[2,2,2,2,256]{4,3,2,1,0:T(2,128)} %get-tuple-element.74) | copy-start | bytes 49156
  95.9 2.1 %copy-start.19 = (f32[2,2,2,2,256]{4,3,2,1,0:T(2,128)S(1)}, f32[2,2,2,2,256]{4,3,2,1,0:T(2,128)}, u32[]{:S(2)}) copy-start(f32[2,2,2,2,256]{4,3,2,1,0:T(2,128)} %get-tuple-element.76) | copy-start | bytes 49156
  98.0 1.2 copy-start.7

commit v6 on v4

--- a/solution.py
+++ b/solution.py
@@ -188,8 +188,12 @@
 def analysis_ext(extended):
     x_part = analyse_lead(extended)
     y_part = batched_left(split_analysis(x_part.shape[1] - 6), x_part)
-    size_z = y_part.shape[2]
-    return contract(y_part, jnp.asarray(periodic_analysis(size_z)), ((2,), (0,)), ((), ()))
+    size_x, size_y, size_z = y_part.shape
+    matrix = jnp.asarray(periodic_analysis(size_z))
+    if size_y % 8 == 0:
+        flat = contract(y_part.reshape(size_x * size_y, size_z), matrix, ((1,), (0,)), ((), ()))
+        return flat.reshape(size_x, size_y, size_z)
+    return contract(y_part, matrix, ((2,), (0,)), ((), ()))
 
 
 def shrink_field(coeffs, thr_table, indices):
@@ -199,11 +203,16 @@
     eight = jnp.concatenate([jnp.zeros((1,), jnp.float32), seven])
     high_x = (jnp.arange(size_x, dtype=jnp.int32) >= size_x // 2).astype(jnp.int32)
     high_y = (jnp.arange(size_y, dtype=jnp.int32) >= size_y // 2).astype(jnp.int32)
-    high_z = (jnp.arange(size_z, dtype=jnp.int32) >= size_z // 2).astype(jnp.int32)
-    band_ids = 4 * high_x[:, None, None] + 2 * high_y[None, :, None] + high_z[None, None, :]
-    thresh = jnp.zeros(coeffs.shape, jnp.float32)
+    plane_ids = 4 * high_x[:, None] + 2 * high_y[None, :]
+    low_z = jnp.zeros((size_x, size_y), jnp.float32)
+    high_z = jnp.zeros((size_x, size_y), jnp.float32)
     for band_no in range(1, 8):
-        thresh = jnp.where(band_ids == band_no, eight[band_no], thresh)
+        if band_no % 2 == 0:
+            low_z = jnp.where(plane_ids == band_no, eight[band_no], low_z)
+        else:
+            high_z = jnp.where(plane_ids + 1 == band_no, eight[band_no], high_z)
+    in_high = (jnp.arange(size_z, dtype=jnp.int32) >= size_z // 2)[None, None, :]
+    thresh = jnp.where(in_high, high_z[:, :, None], low_z[:, :, None])
     return jnp.sign(coeffs) * jnp.maximum(jnp.abs(coeffs) - thresh, 0.0)
 
 

time: 122 us -> 119 us (0.975)
  matrix products: 43.1 us -> 27.6 us
  other arithmetic: 15.2 us -> 28.2 us
    dot_general x15, matrix products: 43.1 us -> 27.6 us  [contract(): lax.dot_general(left, right, (dims, batch), precision=PREC, preferred_ele...]
    select_n x0 -> x3, other arithmetic: none -> 13.2 us  [shrink_field(): high_z = jnp.where(plane_ids + 1 == band_no, eight[band_no], high_z)]
where the time goes in v6:
time: 119 us
  Pallas kernels  46.5 us (39%)
  other arithmetic  28.2 us (24%)
  matrix products  27.6 us (23%)
  local copies, waits for them, and re-layouts  15.7 us (13%)
    pallas_call x3, Pallas kernels, halos(): pl.pallas_call(functools.partial(exchange_kernel, layouts, lax.axis_size(...  46.5 us
    dot_general x15, matrix products, contract(): lax.dot_general(left, right, (dims, batch), precision=PREC, preferred_ele...  27.6 us
    select_n x3, other arithmetic, shrink_field(): high_z = jnp.where(plane_ids + 1 == band_no, eight[band_no], high_z)  13.2 us
    concatenate x3, other arithmetic, assemble(): return jnp.concatenate([top, mid, bottom], axis=dx)  5.64 us
    another operation x3, local copies, waits for them, and re-layouts, synthesise_lead(): joined = jnp.stack([even, odd], axis=1)  5.42 us
    another operation x6, other arithmetic, synthesise_lead(): joined = jnp.stack([even, odd], axis=1)  5.38 us
    unnamed x62, local copies, waits for them, and re-layouts  3.61 us
    scatter x1, local copies, waits for them, and re-layouts, local(): recon1 = synthesis_ext(shrunk1.at[0, :, 0, :, :half_z].set(recon2))  3.46 us

profile of v6, /device:TPU:8, one launch (start us, length us, event | category | flops | bytes accessed | tf_op | source)
XLA Modules:
  0.0 118.8 jit_solution(14705702190060641873)
XLA Ops:
  0.0 16.7 %shard_map.172 = (f32[3,128,256]{2,1,0:T(8,128)}, f32[3,128,256]{2,1,0:T(8,128)}, f32[32,3,256]{2,1,0:T(4,128)}, f32[32,3,256]{2,1,0:T(4,128)}, f32[3,3,256]{2,1...) custom-call(f32[32,128,256]{2,1,0:T(8,128)} %refs_0_.1), custom_call_target="tpu_custom_call" | custom-call | tf_op jit(solution)/shard_map/pallas_call | solution.py:122
  16.8 3.2 %maximum_maximum_fusion.1 = f32[38,134,256]{2,1,0:T(8,128)S(1)} fusion(f32[3,3,256]{2,1,0:T(4,128)} %get-tuple-element.68, f32[3,128,256]{2,1,0:T(8,128)} %get-tuple-element.67, f32[3,3,256]{2,1,0:T(4,128)} %get-tuple-element.66, f32[32,3,256]{2,1,0:T(4,128)} %get-tuple-element.65, f32[32,128,256]{2,1,0:T(8,128)} %refs_0_.1, ...), kind=kLoop, calls=%fused_computation.1 | loop fusion | flops 10428416 | bytes 10428416 | tf_op jit(solution)/shard_map/concatenate | solution.py:141
  20.0 0.7 copy-done
  20.6 0.0 copy-done.4
  20.7 0.5 pad_maximum_fusion
  21.2 0.0 copy-start.12
  21.2 2.5 %multiply_add_fusion.1 = (f32[16,134,256]{2,1,0:T(8,128)S(1)}, f32[16,134,256]{2,1,0:T(8,128)S(1)}) fusion(f32[38,134,256]{2,1,0:T(8,128)S(1)} %maximum_maximum_fusion.1, f32[32,134,256]{2,1,0:T(8,128)S(1)} %pad_maximum_fusion), kind=kLoop, calls=%fused_computation.15 | loop fusion | flops 16465920 | bytes 21954560 | tf_op jit(solution)/shard_map/add | solution.py:165
  23.7 0.0 copy-start.9
  23.8 3.8 %fusion = f32[32,128,256]{2,1,0:T(8,128)S(1)} fusion(f32[16,134,256]{2,1,0:T(8,128)S(1)} %get-tuple-element.97, f32[16,134,256]{2,1,0:T(8,128)S(1)} %get-tuple-element.96, f32[134,128]{1,0:T(8,128)S(1)} %copy-done.12), kind=kOutput, calls=%fused_computation.4 | convolution fusion | flops 844152832 | bytes 8653824 | tf_op jit(solution)/shard_map/dot_general | solution.py:149
  27.6 0.2 select_reduce_fusion
  27.8 0.7 fusion.87
  28.5 4.4 %select_select_fusion.3 = (f32[32,128]{1,0:T(8,128)S(1)}, f32[32,128]{1,0:T(8,128)S(1)}) fusion(f32[]{:T(128)} %bitcast.5, f32[]{:T(128)} %bitcast.4, f32[]{:T(128)} %bitcast.3, f32[]{:T(128)} %bitcast.2, s32[128]{0:T(128)S(1)} %broadcast_select_fusion, s32[32]{0:T(128)S(1)} %compare_select_fusion.4, f32[]{:T(128)} %bitcast.8, f32[]{:T(128)} %bitcast.7, ...), kind=kLoop, calls=%fused_computation.126 | loop fusion | flops 65536 | bytes 33436 | tf_op jit(solution)/shard_map/jit(_where)/select_n | solution.py:213
  32.9 4.4 %maximum_multiply_fusion = (f32[32,128,256]{2,1,0:T(8,128)}, f32[32,128,256]{2,1,0:T(8,128)S(1)}) fusion(f32[32,128]{1,0:T(8,128)S(1)} %get-tuple-element.116, f32[32,128]{1,0:T(8,128)S(1)} %get-tuple-element.115, pred[256]{0:T(512)(128)(4,1)S(1)} %iota_compare_fusion.3, f32[32,128,256]{2,1,0:T(8,128)S(1)} %fusion, f32[256,256,1]{1,0,2:T(8,128)S(1)} %copy-done.9), kind=kOutput, calls=%fused_computation.9 | convolution fusion | flops 1616904192 | bytes 12878080 | tf_op jit(solution)/shard_map/dot_general | solution.py:149
  37.2 0.8 slice.486.refs_0_
  38.1 19.0 %shard_map.173 = (f32[9,64,128]{2,1,0:T(8,128)}, f32[9,64,128]{2,1,0:T(8,128)}, f32[16,9,128]{2,1,0:T(8,128)}, f32[16,9,128]{2,1,0:T(8,128)}, f32[9,9,128]{2,1,0...) custom-call(f32[16,64,128]{2,1,0:T(8,128)} %slice.486.refs_0_, ...), custom_call_target="tpu_custom_call" | custom-call | tf_op jit(solution)/shard_map/pallas_call | solution.py:122
  57.0 1.4 %maximum_maximum_fusion.2 = f32[34,82,128]{2,1,0:T(8,128)S(1)} fusion(f32[9,9,128]{2,1,0:T(8,128)} %get-tuple-element.84, f32[9,64,128]{2,1,0:T(8,128)} %get-tuple-element.83, f32[9,9,128]{2,1,0:T(8,128)} %get-tuple-element.82, f32[16,9,128]{2,1,0:T(8,128)} %get-tuple-element.81, f32[16,64,128]{2,1,0:T(8,128)S(1)} %copy-done.2, ...), kind=kLoop, calls=%fused_computation.28 | loop fusion | flops 2854912 | bytes 2854912 | tf_op jit(solution)/shard_map/concatenate | solution.py:141
  58.5 0.0 copy-start.15
  58.5 0.7 multiply_add_fusion.3
  59.1 0.0 copy-start.14
  59.1 0.1 copy-done.15
  59.2 0.7 fusion.15
  59.9 0.7 fusion.85
  60.6 4.4 %select_select_fusion.1 = (f32[28,76]{1,0:T(8,128)S(1)}, f32[28,76]{1,0:T(8,128)S(1)}) fusion(f32[]{:T(128)} %bitcast.15, f32[]{:T(128)} %bitcast.14, f32[]{:T(128)} %bitcast.13, f32[]{:T(128)} %bitcast.12, s32[76]{0:T(128)S(1)} %compare_select_fusion.1, s32[28]{0:T(128)S(1)} %compare_select_fusion.2, f32[]{:T(128)} %bitcast.18, f32[]{:T(128)} %bitcast.17, ...), kind=kLoop, calls=%fused_computation.124 | loop fusion | flops 34048 | bytes 17468 | tf_op jit(solution)/shard_map/jit(_where)/select_n | solution.py:213
  65.0 0.0 copy-start.18
  65.1 0.0 copy-start.30
  65.1 0.9 maximum_multiply_fusion.1
  66.0 0.0 copy-start.27
  66.0 0.1 multiply_add_fusion.5
  66.1 0.2 fusion.62
  66.4 4.4 %select_select_fusion.5 = (f32[8,32]{1,0:T(8,128)S(1)}, f32[8,32]{1,0:T(8,128)S(1)}) fusion(f32[]{:T(128)} %bitcast.24, f32[]{:T(128)} %bitcast.23, f32[]{:T(128)} %bitcast.22, f32[]{:T(128)} %bitcast.21, s32[32]{0:T(128)S(1)} %compare_select_fusion.3, s32[8]{0:T(128)S(1)} %compare_select_fusion, f32[]{:T(128)} %bitcast.27, f32[]{:T(128)} %bitcast.26, ...), kind=kLoop, calls=%fused_computation.136 | loop fusion | flops 4096 | bytes 2236 | tf_op jit(solution)/shard_map/jit(_where)/select_n | solution.py:213
  70.8 0.2 maximum_multiply_fusion.2
  71.0 0.8 dynamic_update_slice.3
  71.9 0.6 copy-done.7
  72.5 10.8 %shard_map.174 = (f32[2,4,2,16,64]{4,3,2,1,0:T(8,128)}, f32[2,4,2,16,64]{4,3,2,1,0:T(8,128)}, f32[2,4,2,4,64]{4,3,2,1,0:T(4,128)}, f32[2,4,2,4,64]{4,3,2,1,0:T(4...) custom-call(f32[2,4,2,16,64]{4,3,2,1,0:T(8,128)} %bitcast.120), custom_call_target="tpu_custom_call" | custom-call | tf_op jit(solution)/shard_map/pallas_call | solution.py:122
  83.3 1.6 %fusion.23 = f32[2,12,2,24,64]{4,3,2,1,0:T(8,128)S(1)} fusion(f32[64,64,1,1,1]{1,0,4,3,2:T(8,128)S(1)} %copy-done.30, f32[2,4,2,4,64]{4,3,2,1,0:T(4,128)} %get-tuple-element.92, f32[2,4,2,16,64]{4,3,2,1,0:T(8,128)} %get-tuple-element.91, f32[2,4,2,4,64]{4,3,2,1,0:T(4,128)} %get-tuple-element.90, f32[2,4,2,4,64]{4,3,2,1,0:T(4,128)} %get-tuple-element.89, ...), kind=kOutput, calls=%fused_computation.44 | convolution fusion | flops 28901376 | bytes 606208 | tf_op jit(solution)/shard_map/dot_general | solution.py:149
  84.9 0.6 fusion.51
  85.6 0.6 fusion.19
  86.2 0.2 fusion.61
  86.3 0.0 copy-start.13
  86.5 0.0 copy-start.19
  86.5 0.1 reshape.397
  86.6 0.0 copy-start.20
  86.6 3.5 %scatter.6 = f32[2,14,2,38,128]{4,3,2,1,0:T(8,128)S(1)} dynamic-update-slice(f32[2,14,2,38,128]{4,3,2,1,0:T(8,128)S(1)} %reshape.397, f32[1,14,1,38,64]{4,3,2,1,0:T(8,128)S(1)} %slice_bitcast_fusion.14, s32[]{:T(128)} %constant.86.clone.1, s32[]{:T(128)} %constant.86.clone.1, s32[]{:T(128)} %constant.86.clone.1, s32[]{:T(128)} %constant.86.clone.1, s32[]{:T(128)} %constant.86.clone.1) | dynamic-update-slice | bytes 272388 | tf_op jit(solution)/shard_map/scatter | solution.py:253
  90.1 0.6 fusion.88
  90.7 1.0 fusion.41
  91.8 1.1 fusion.14
  92.8 0.4 fusion.50
  93.3 0.1 pad_maximum_fusion.2
  93.4 1.6 %copy-done.1 = f32[32,128,256]{2,1,0:T(8,128)S(1)} copy-done((f32[32,128,256]{2,1,0:T(8,128)S(1)}, f32[32,128,256]{2,1,0:T(8,128)}, u32[]{:S(2)}) %copy-start.1) | copy-done | bytes 4194328
  95.0 0.2 copy-done.5
  95.2 0.2 copy-done.6
  95.4 0.0 copy-done.10
  95.4 0.0 copy-done.11
  95.5 0.0 copy-start.8
  95.5 1.1 maximum_maximum_fusion
  96.5 0.1 constant_dynamic-update-slice_fusion
  96.6 0.0 copy-start.16
  96.6 2.6 %fusion.89 = f32[2,20,2,68,256]{4,3,2,1,0:T(8,128)S(1)} fusion(f32[2,20,2,68,256]{4,3,2,1,0:T(8,128)S(1)} %constant_dynamic-update-slice_fusion, f32[256,256,1,1,1]{1,0,4,3,2:T(8,128)S(1)} %copy-done.8), kind=kOutput, calls=%fused_computation.164 | convolution fusion | flops 2139095040 | bytes 11403264 | tf_op jit(solution)/shard_map/dot_general | solution.py:149
  99.3 0.0 copy-start.17
  99.3 4.7 %fusion.4 = f32[40,256,128]{2,1,0:T(8,128)S(1)} fusion(f32[40,2,68,256]{3,2,1,0:T(8,128)S(1)} %bitcast.112, f32[68,128]{1,0:T(8,128)S(1)} %copy-done.16), kind=kOutput, calls=%fused_computation.11 | convolution fusion | flops 534773760 | bytes 8228864 | tf_op jit(solution)/shard_map/dot_general | solution.py:149
  104.0 4.7 %add_bitcast_fusion = f32[40,128,256]{1,2,0:T(8,128)S(1)} fusion(f32[40,256,128]{2,1,0:T(8,128)S(1)} %fusion.4, f32[40,2,68,256]{3,2,1,0:T(8,128)S(1)} %bitcast.113, f32[68,128]{1,0:T(8,128)S(1)} %copy-done.17), kind=kOutput, calls=%fused_computation.2 | convolution fusion | flops 536084480 | bytes 13471744 | tf_op jit(solution)/shard_map/dot_general | solution.py:149
  108.7 2.3 %fusion.13 = (f32[16,1,128,256]{2,3,0,1:T(8,128)S(1)}, f32[16,1,128,256]{2,3,0,1:T(8,128)S(1)}) fusion(f32[40,128,256]{1,2,0:T(8,128)S(1)} %add_bitcast_fusion), kind=kLoop, calls=%fused_computation.26 | loop fusion | flops 15728640 | bytes 25165824 | tf_op jit(solution)/shard_map/stack | solution.py:184
  111.0 2.4 %pad_maximum_fusion.1 = f32[16,2,128,256]{2,3,0,1:T(8,128)} fusion(f32[16,1,128,256]{2,3,0,1:T(8,128)S(1)} %get-tuple-element.99, f32[16,1,128,256]{2,3,0,1:T(8,128)S(1)} %get-tuple-element.98), kind=kLoop, calls=%fused_computation.8 | loop fusion | flops 1048576 | bytes 8388608 | tf_op jit(solution)/shard_map/stack | solution.py:184
  113.4 5.3 %copy.43 = f32[16,2,128,256]{3,2,1,0:T(8,128)} copy(f32[16,2,128,256]{2,3,0,1:T(8,128)} %pad_maximum_fusion.1) | data formatting | bytes 8388608 | tf_op jit(solution)/shard_map/stack | solution.py:184
  (56 shorter events, 0.3 us)
Async XLA Ops:
  16.7 3.9 %copy-start = (f32[32,128,256]{2,1,0:T(8,128)S(1)}, f32[32,128,256]{2,1,0:T(8,128)}, u32[]{:S(2)}) copy-start(f32[32,128,256]{2,1,0:T(8,128)} %refs_0_.1) | copy-start | bytes 12582916
  16.7 3.9 %copy-start.3 = (f32[32,3,256]{2,1,0:T(4,128)S(1)}, f32[32,3,256]{2,1,0:T(4,128)}, u32[]{:S(2)}) copy-start(f32[32,3,256]{2,1,0:T(4,128)} %get-tuple-element.64) | copy-start | bytes 294916
  16.8 3.9 %copy-start.4 = (f32[32,3,256]{2,1,0:T(4,128)S(1)}, f32[32,3,256]{2,1,0:T(4,128)}, u32[]{:S(2)}) copy-start(f32[32,3,256]{2,1,0:T(4,128)} %get-tuple-element.65) | copy-start | bytes 294916
  21.2 2.5 %copy-start.12 = (f32[134,128]{1,0:T(8,128)S(1)}, f32[134,128]{1,0:T(8,128)}, u32[]{:S(2)}) copy-start(f32[134,128]{1,0:T(8,128)} %constant.98.clone) | copy-start | bytes 205828
  23.7 3.8 %copy-start.28 = (s32[3,7]{1,0:T(4,128)S(1)}, s32[3,7]{1,0:T(4,128)}, u32[]{:S(2)}) copy-start(s32[3,7]{1,0:T(4,128)} %param.24) | copy-start | bytes 256
  23.7 3.8 %copy-start.29 = (f32[16]{0:T(128)S(1)}, f32[16]{0:T(128)}, u32[]{:S(2)}) copy-start(f32[16]{0:T(128)} %param.23) | copy-start | bytes 196
  23.7 9.1 %copy-start.9 = (f32[256,256,1]{1,0,2:T(8,128)S(1)}, f32[256,256,1]{1,0,2:T(8,128)}, u32[]{:S(2)}) copy-start(f32[256,256,1]{1,0,2:T(8,128)} %constant.111) | copy-start | bytes 786436
  38.1 19.0 %copy-start.2 = (f32[16,64,128]{2,1,0:T(8,128)S(1)}, f32[16,64,128]{2,1,0:T(8,128)}, u32[]{:S(2)}) copy-start(f32[16,64,128]{2,1,0:T(8,128)} %slice.486.refs_0_) | copy-start | bytes 1572868
  58.5 0.8 copy-start.15
  59.1 5.9 %copy-start.14 = (f32[128,128,1]{1,0,2:T(8,128)S(1)}, f32[128,128,1]{1,0,2:T(8,128)}, u32[]{:S(2)}) copy-start(f32[128,128,1]{1,0,2:T(8,128)} %constant.112) | copy-start | bytes 196612
  65.0 1.1 copy-start.25
  65.0 5.8 %copy-start.18 = (f32[64,64,1]{1,0,2:T(8,128)S(1)}, f32[64,64,1]{1,0,2:T(8,128)}, u32[]{:S(2)}) copy-start(f32[64,64,1]{1,0,2:T(8,128)} %constant.113) | copy-start | bytes 49156
  65.1 18.3 %copy-start.30 = (f32[64,64,1,1,1]{1,0,4,3,2:T(8,128)S(1)}, f32[64,64,1,1,1]{1,0,4,3,2:T(8,128)}, u32[]{:S(2)}) copy-start(f32[64,64,1,1,1]{1,0,4,3,2:T(8,128)} %constant.114) | copy-start | bytes 49156
  66.0 18.9 %copy-start.27 = (f32[24,40]{1,0:T(8,128)S(1)}, f32[24,40]{1,0:T(8,128)}, u32[]{:S(2)}) copy-start(f32[24,40]{1,0:T(8,128)} %constant.104.clone) | copy-start | bytes 11524
  66.1 19.4 %copy-start.26 = (f32[24,40]{1,0:T(8,128)S(1)}, f32[24,40]{1,0:T(8,128)}, u32[]{:S(2)}) copy-start(f32[24,40]{1,0:T(8,128)} %constant.105.clone) | copy-start | bytes 11524
  71.8 0.7 copy-start.7
  86.3 3.7 %copy-start.13 = (f32[128,128,1,1,1]{1,0,4,3,2:T(8,128)S(1)}, f32[128,128,1,1,1]{1,0,4,3,2:T(8,128)}, u32[]{:S(2)}) copy-start(f32[128,128,1,1,1]{1,0,4,3,2:T(8,128)} %constant.115) | copy-start | bytes 196612
  86.5 4.2 %copy-start.19 = (f32[38,68]{1,0:T(8,128)S(1)}, f32[38,68]{1,0:T(8,128)}, u32[]{:S(2)}) copy-start(f32[38,68]{1,0:T(8,128)} %constant.106.clone) | copy-start | bytes 31012
  86.6 5.2 %copy-start.20 = (f32[38,68]{1,0:T(8,128)S(1)}, f32[38,68]{1,0:T(8,128)}, u32[]{:S(2)}) copy-start(f32[38,68]{1,0:T(8,128)} %constant.107.clone) | copy-start | bytes 31012
  92.8 2.2 %copy-start.1 = (f32[32,128,256]{2,1,0:T(8,128)S(1)}, f32[32,128,256]{2,1,0:T(8,128)}, u32[]{:S(2)}) copy-start(f32[32,128,256]{2,1,0:T(8,128)} %get-tuple-element.138) | copy-start | bytes 12582916
  93.2 2.0 %copy-start.5 = (f32[2,2,2,64,256]{4,3,2,1,0:T(8,128)S(1)}, f32[2,2,2,64,256]{4,3,2,1,0:T(8,128)}, u32[]{:S(2)}) copy-start(f32[2,2,2,64,256]{4,3,2,1,0:T(8,128)} %get-tuple-element.70) | copy-start | bytes 1572868
  93.2 2.1 %copy-start.6 = (f32[2,2,2,64,256]{4,3,2,1,0:T(8,128)S(1)}, f32[2,2,2,64,256]{4,3,2,1,0:T(8,128)}, u32[]{:S(2)}) copy-start(f32[2,2,2,64,256]{4,3,2,1,0:T(8,128)} %get-tuple-element.75) | copy-start | bytes 1572868
  93.3 2.1 %copy-start.10 = (f32[2,16,2,2,256]{4,3,2,1,0:T(2,128)S(1)}, f32[2,16,2,2,256]{4,3,2,1,0:T(2,128)}, u32[]{:S(2)}) copy-start(f32[2,16,2,2,256]{4,3,2,1,0:T(2,128)} %get-tuple-element.72) | copy-start | bytes 393220
  93.3 2.2 %copy-start.11 = (f32[2,16,2,2,256]{4,3,2,1,0:T(2,128)S(1)}, f32[2,16,2,2,256]{4,3,2,1,0:T(2,128)}, u32[]{:S(2)}) copy-start(f32[2,16,2,2,256]{4,3,2,1,0:T(2,128)} %get-tuple-element.73) | copy-start | bytes 393220
  93.3 2.2 %copy-start.21 = (f32[2,2,2,2,256]{4,3,2,1,0:T(2,128)S(1)}, f32[2,2,2,2,256]{4,3,2,1,0:T(2,128)}, u32[]{:S(2)}) copy-start(f32[2,2,2,2,256]{4,3,2,1,0:T(2,128)} %get-tuple-element.69) | copy-start | bytes 49156
  93.3 2.2 %copy-start.22 = (f32[2,2,2,2,256]{4,3,2,1,0:T(2,128)S(1)}, f32[2,2,2,2,256]{4,3,2,1,0:T(2,128)}, u32[]{:S(2)}) copy-start(f32[2,2,2,2,256]{4,3,2,1,0:T(2,128)} %get-tuple-element.71) | copy-start | bytes 49156
  93.3 2.2 %copy-start.23 = (f32[2,2,2,2,256]{4,3,2,1,0:T(2,128)S(1)}, f32[2,2,2,2,256]{4,3,2,1,0:T(2,128)}, u32[]{:S(2)}) copy-start(f32[2,2,2,2,256]{4,3,2,1,0:T(2,128)} %get-tuple-element.74) | copy-start | bytes 49156
  93.3 2.1 %copy-start.24 = (f32[2,2,2,2,256]{4,3,2,1,0:T(2,128)S(1)}, f32[2,2,2,2,256]{4,3,2,1,0:T(2,128)}, u32[]{:S(2)}) copy-start(f32[2,2,2,2,256]{4,3,2,1,0:T(2,128)} %get-tuple-element.76) | copy-start | bytes 49156
  95.5 1.2 copy-start.8
  96.6 2.6 %copy-start.16 = (f32[68,128]{1,0:T(8,128)S(1)}, f32[68,128]{1,0:T(8,128)}, u32[]{:S(2)}) copy-start(f32[68,128]{1,0:T(8,128)} %constant.109.clone) | copy-start | bytes 104452
  99.3 4.7 %copy-start.17 = (f32[68,128]{1,0:T(8,128)S(1)}, f32[68,128]{1,0:T(8,128)}, u32[]{:S(2)}) copy-start(f32[68,128]{1,0:T(8,128)} %constant.108.clone) | copy-start | bytes 104452

commit v7 on v4

--- a/solution.py
+++ b/solution.py
@@ -188,8 +188,12 @@
 def analysis_ext(extended):
     x_part = analyse_lead(extended)
     y_part = batched_left(split_analysis(x_part.shape[1] - 6), x_part)
-    size_z = y_part.shape[2]
-    return contract(y_part, jnp.asarray(periodic_analysis(size_z)), ((2,), (0,)), ((), ()))
+    size_x, size_y, size_z = y_part.shape
+    matrix = jnp.asarray(periodic_analysis(size_z))
+    if size_y % 8 == 0:
+        flat = contract(y_part.reshape(size_x * size_y, size_z), matrix, ((1,), (0,)), ((), ()))
+        return flat.reshape(size_x, size_y, size_z)
+    return contract(y_part, matrix, ((2,), (0,)), ((), ()))
 
 
 def shrink_field(coeffs, thr_table, indices):

time: 122 us -> 122 us (level)
  no operation moved by 1% of the time
where the time goes in v7:
time: 122 us; the launch traced here: 121 us
  Pallas kernels  46.5 us (38%)
  matrix products  43.1 us (35%)
  local copies, waits for them, and re-layouts  15.7 us (13%)
  other arithmetic  15.2 us (12%)
    pallas_call x3, Pallas kernels, halos(): pl.pallas_call(functools.partial(exchange_kernel, layouts, lax.axis_size(...  46.5 us
    dot_general x15, matrix products, contract(): lax.dot_general(left, right, (dims, batch), precision=PREC, preferred_ele...  43.1 us
    concatenate x3, other arithmetic, assemble(): return jnp.concatenate([top, mid, bottom], axis=dx)  5.64 us
    another operation x3, local copies, waits for them, and re-layouts, synthesise_lead(): joined = jnp.stack([even, odd], axis=1)  5.42 us
    another operation x6, other arithmetic, synthesise_lead(): joined = jnp.stack([even, odd], axis=1)  5.37 us
    unnamed x62, local copies, waits for them, and re-layouts  3.61 us
    scatter x1, local copies, waits for them, and re-layouts, local(): recon1 = synthesis_ext(shrunk1.at[0, :, 0, :, :half_z].set(recon2))  3.46 us
    add x3, other arithmetic, analyse_lead(): low = low + filt_low[j] * taken  3.26 us

profile of v7, /device:TPU:8, one launch (start us, length us, event | category | flops | bytes accessed | tf_op | source)
XLA Modules:
  0.0 121.2 jit_solution(18160595588103001369)
XLA Ops:
  0.0 16.7 %shard_map.172 = (f32[3,128,256]{2,1,0:T(8,128)}, f32[3,128,256]{2,1,0:T(8,128)}, f32[32,3,256]{2,1,0:T(4,128)}, f32[32,3,256]{2,1,0:T(4,128)}, f32[3,3,256]{2,1...) custom-call(f32[32,128,256]{2,1,0:T(8,128)} %refs_0_.1), custom_call_target="tpu_custom_call" | custom-call | tf_op jit(solution)/shard_map/pallas_call | solution.py:122
  16.8 3.2 %maximum_maximum_fusion.1 = f32[38,134,256]{2,1,0:T(8,128)S(1)} fusion(f32[3,3,256]{2,1,0:T(4,128)} %get-tuple-element.68, f32[3,128,256]{2,1,0:T(8,128)} %get-tuple-element.67, f32[3,3,256]{2,1,0:T(4,128)} %get-tuple-element.66, f32[32,3,256]{2,1,0:T(4,128)} %get-tuple-element.65, f32[32,128,256]{2,1,0:T(8,128)} %refs_0_.1, ...), kind=kLoop, calls=%fused_computation.8 | loop fusion | flops 10428416 | bytes 10428416 | tf_op jit(solution)/shard_map/concatenate | solution.py:141
  20.0 0.7 copy-done
  20.6 0.0 copy-done.4
  20.7 0.5 pad_maximum_fusion
  21.2 0.0 copy-start.11
  21.2 2.5 %multiply_add_fusion.1 = (f32[16,134,256]{2,1,0:T(8,128)S(1)}, f32[16,134,256]{2,1,0:T(8,128)S(1)}) fusion(f32[38,134,256]{2,1,0:T(8,128)S(1)} %maximum_maximum_fusion.1, f32[32,134,256]{2,1,0:T(8,128)S(1)} %pad_maximum_fusion), kind=kLoop, calls=%fused_computation.29 | loop fusion | flops 16465920 | bytes 21954560 | tf_op jit(solution)/shard_map/add | solution.py:165
  23.7 0.0 copy-start.27
  23.8 3.8 %fusion = f32[32,128,256]{2,1,0:T(8,128)S(1)} fusion(f32[16,134,256]{2,1,0:T(8,128)S(1)} %get-tuple-element.97, f32[16,134,256]{2,1,0:T(8,128)S(1)} %get-tuple-element.96, f32[134,128]{1,0:T(8,128)S(1)} %copy-done.11), kind=kOutput, calls=%fused_computation.11 | convolution fusion | flops 844152832 | bytes 8653824 | tf_op jit(solution)/shard_map/dot_general | solution.py:149
  27.6 0.2 select_reduce_fusion
  27.8 0.7 fusion.75
  28.5 0.1 broadcast_add_fusion.1
  28.5 10.3 %maximum_multiply_fusion = (f32[32,128,256]{2,1,0:T(8,128)}, f32[32,128,256]{2,1,0:T(8,128)S(1)}) fusion(f32[]{:T(128)} %bitcast.8, f32[]{:T(128)} %bitcast.7, f32[]{:T(128)} %bitcast.6, f32[]{:T(128)} %bitcast.5, f32[]{:T(128)} %bitcast.4, f32[]{:T(128)} %bitcast.3, f32[]{:T(128)} %bitcast.2, s32[256]{0:T(256)S(1)} %compare_convert_fusion.1, ...), kind=kOutput, calls=%fused_computation.16 | convolution fusion | flops 1631584256 | bytes 12862492 | tf_op jit(solution)/shard_map/dot_general | solution.py:149
  38.8 0.8 slice.486.refs_0_
  39.6 19.0 %shard_map.173 = (f32[9,64,128]{2,1,0:T(8,128)}, f32[9,64,128]{2,1,0:T(8,128)}, f32[16,9,128]{2,1,0:T(8,128)}, f32[16,9,128]{2,1,0:T(8,128)}, f32[9,9,128]{2,1,0...) custom-call(f32[16,64,128]{2,1,0:T(8,128)} %slice.486.refs_0_, ...), custom_call_target="tpu_custom_call" | custom-call | tf_op jit(solution)/shard_map/pallas_call | solution.py:122
  58.6 1.4 %maximum_maximum_fusion.2 = f32[34,82,128]{2,1,0:T(8,128)S(1)} fusion(f32[9,9,128]{2,1,0:T(8,128)} %get-tuple-element.84, f32[9,64,128]{2,1,0:T(8,128)} %get-tuple-element.83, f32[9,9,128]{2,1,0:T(8,128)} %get-tuple-element.82, f32[16,9,128]{2,1,0:T(8,128)} %get-tuple-element.81, f32[16,64,128]{2,1,0:T(8,128)S(1)} %copy-done.2, ...), kind=kLoop, calls=%fused_computation.42 | loop fusion | flops 2854912 | bytes 2854912 | tf_op jit(solution)/shard_map/concatenate | solution.py:141
  60.0 0.0 copy-start.13
  60.1 0.7 multiply_add_fusion.3
  60.7 0.0 copy-start.28
  60.7 0.1 copy-done.13
  60.8 0.7 fusion.15
  61.5 0.7 fusion.73
  62.2 0.1 broadcast_add_fusion
  62.3 0.0 copy-start.30
  62.3 6.0 %maximum_multiply_fusion.1 = (f32[28,76,128]{2,1,0:T(8,128)S(1)}, f32[28,76,128]{2,1,0:T(8,128)S(1)}) fusion(f32[]{:T(128)} %bitcast.18, f32[]{:T(128)} %bitcast.17, f32[]{:T(128)} %bitcast.16, f32[]{:T(128)} %bitcast.15, f32[]{:T(128)} %bitcast.14, f32[]{:T(128)} %bitcast.13, f32[]{:T(128)} %bitcast.12, s32[128]{0:T(128)S(1)} %compare_convert_fusion.2, ...), kind=kOutput, calls=%fused_computation.51 | convolution fusion | flops 214638592 | bytes 3343196 | tf_op jit(solution)/shard_map/dot_general | solution.py:149
  68.3 0.0 copy-start.29
  68.4 0.0 copy-start.24
  68.4 0.1 multiply_add_fusion.5
  68.5 0.2 fusion.62
  68.7 0.0 copy-start.23
  68.8 0.1 broadcast_add_fusion.2
  68.8 4.7 %maximum_multiply_fusion.2 = (f32[8,32,64]{2,1,0:T(8,128)S(1)}, f32[8,32,64]{2,1,0:T(8,128)S(1)}) fusion(f32[]{:T(128)} %bitcast.27, f32[]{:T(128)} %bitcast.26, f32[]{:T(128)} %bitcast.25, f32[]{:T(128)} %bitcast.24, f32[]{:T(128)} %bitcast.23, f32[]{:T(128)} %bitcast.22, f32[]{:T(128)} %bitcast.21, s32[64]{0:T(128)S(1)} %compare_convert_fusion, ...), kind=kOutput, calls=%fused_computation.124 | convolution fusion | flops 6619136 | bytes 214300 | tf_op jit(solution)/shard_map/dot_general | solution.py:149
  73.5 0.8 dynamic_update_slice.3
  74.4 0.6 copy-done.10
  75.0 10.8 %shard_map.174 = (f32[2,4,2,16,64]{4,3,2,1,0:T(8,128)}, f32[2,4,2,16,64]{4,3,2,1,0:T(8,128)}, f32[2,4,2,4,64]{4,3,2,1,0:T(4,128)}, f32[2,4,2,4,64]{4,3,2,1,0:T(4...) custom-call(f32[2,4,2,16,64]{4,3,2,1,0:T(8,128)} %bitcast.120), custom_call_target="tpu_custom_call" | custom-call | tf_op jit(solution)/shard_map/pallas_call | solution.py:122
  85.8 1.6 %fusion.23 = f32[2,12,2,24,64]{4,3,2,1,0:T(8,128)S(1)} fusion(f32[64,64,1,1,1]{1,0,4,3,2:T(8,128)S(1)} %copy-done.29, f32[2,4,2,4,64]{4,3,2,1,0:T(4,128)} %get-tuple-element.92, f32[2,4,2,16,64]{4,3,2,1,0:T(8,128)} %get-tuple-element.91, f32[2,4,2,4,64]{4,3,2,1,0:T(4,128)} %get-tuple-element.90, f32[2,4,2,4,64]{4,3,2,1,0:T(4,128)} %get-tuple-element.89, ...), kind=kOutput, calls=%fused_computation.58 | convolution fusion | flops 28901376 | bytes 606208 | tf_op jit(solution)/shard_map/dot_general | solution.py:149
  87.4 0.6 fusion.51
  88.0 0.6 fusion.19
  88.7 0.2 fusion.61
  88.8 0.0 copy-start.12
  88.9 0.0 copy-start.16
  89.0 0.1 reshape.292
  89.1 0.0 copy-start.17
  89.1 3.5 %scatter.6 = f32[2,14,2,38,128]{4,3,2,1,0:T(8,128)S(1)} dynamic-update-slice(f32[2,14,2,38,128]{4,3,2,1,0:T(8,128)S(1)} %reshape.292, f32[1,14,1,38,64]{4,3,2,1,0:T(8,128)S(1)} %slice_bitcast_fusion.14, s32[]{:T(128)} %constant.85.clone.1, s32[]{:T(128)} %constant.85.clone.1, s32[]{:T(128)} %constant.85.clone.1, s32[]{:T(128)} %constant.85.clone.1, s32[]{:T(128)} %constant.85.clone.1) | dynamic-update-slice | bytes 272388 | tf_op jit(solution)/shard_map/scatter | solution.py:248
  92.5 0.6 fusion.76
  93.2 1.1 fusion.41
  94.3 1.1 fusion.14
  95.3 0.4 fusion.50
  95.8 0.1 pad_maximum_fusion.2
  95.9 1.6 %copy-done.1 = f32[32,128,256]{2,1,0:T(8,128)S(1)} copy-done((f32[32,128,256]{2,1,0:T(8,128)S(1)}, f32[32,128,256]{2,1,0:T(8,128)}, u32[]{:S(2)}) %copy-start.1) | copy-done | bytes 4194328
  97.5 0.2 copy-done.5
  97.7 0.2 copy-done.6
  97.9 0.0 copy-done.8
  97.9 0.0 copy-done.9
  98.0 0.0 copy-start.7
  98.0 1.1 maximum_maximum_fusion
  99.0 0.1 constant_dynamic-update-slice_fusion
  99.1 0.0 copy-start.14
  99.1 2.6 %fusion.77 = f32[2,20,2,68,256]{4,3,2,1,0:T(8,128)S(1)} fusion(f32[2,20,2,68,256]{4,3,2,1,0:T(8,128)S(1)} %constant_dynamic-update-slice_fusion, f32[256,256,1,1,1]{1,0,4,3,2:T(8,128)S(1)} %copy-done.7), kind=kOutput, calls=%fused_computation.158 | convolution fusion | flops 2139095040 | bytes 11403264 | tf_op jit(solution)/shard_map/dot_general | solution.py:149
  101.8 4.7 %fusion.4 = f32[40,256,128]{2,1,0:T(8,128)S(1)} fusion(f32[40,2,68,256]{3,2,1,0:T(8,128)S(1)} %bitcast.110, f32[68,128]{1,0:T(8,128)S(1)} %copy-done.14), kind=kOutput, calls=%fused_computation.25 | convolution fusion | flops 534773760 | bytes 8228864 | tf_op jit(solution)/shard_map/dot_general | solution.py:149
  106.5 4.7 %add_bitcast_fusion = f32[40,128,256]{1,2,0:T(8,128)S(1)} fusion(f32[40,256,128]{2,1,0:T(8,128)S(1)} %fusion.4, f32[40,2,68,256]{3,2,1,0:T(8,128)S(1)} %bitcast.111, f32[68,128]{1,0:T(8,128)S(1)} %copy-done.15), kind=kOutput, calls=%fused_computation.9 | convolution fusion | flops 536084480 | bytes 13471744 | tf_op jit(solution)/shard_map/dot_general | solution.py:149
  111.2 2.3 %fusion.13 = (f32[16,1,128,256]{2,3,0,1:T(8,128)S(1)}, f32[16,1,128,256]{2,3,0,1:T(8,128)S(1)}) fusion(f32[40,128,256]{1,2,0:T(8,128)S(1)} %add_bitcast_fusion), kind=kLoop, calls=%fused_computation.40 | loop fusion | flops 15728640 | bytes 25165824 | tf_op jit(solution)/shard_map/stack | solution.py:184
  113.5 2.4 %pad_maximum_fusion.1 = f32[16,2,128,256]{2,3,0,1:T(8,128)} fusion(f32[16,1,128,256]{2,3,0,1:T(8,128)S(1)} %get-tuple-element.99, f32[16,1,128,256]{2,3,0,1:T(8,128)S(1)} %get-tuple-element.98), kind=kLoop, calls=%fused_computation.15 | loop fusion | flops 1048576 | bytes 8388608 | tf_op jit(solution)/shard_map/stack | solution.py:184
  115.9 5.3 %copy.43 = f32[16,2,128,256]{3,2,1,0:T(8,128)} copy(f32[16,2,128,256]{2,3,0,1:T(8,128)} %pad_maximum_fusion.1) | data formatting | bytes 8388608 | tf_op jit(solution)/shard_map/stack | solution.py:184
  (56 shorter events, 0.3 us)
Async XLA Ops:
  16.7 3.9 %copy-start = (f32[32,128,256]{2,1,0:T(8,128)S(1)}, f32[32,128,256]{2,1,0:T(8,128)}, u32[]{:S(2)}) copy-start(f32[32,128,256]{2,1,0:T(8,128)} %refs_0_.1) | copy-start | bytes 12582916
  16.7 3.9 %copy-start.3 = (f32[32,3,256]{2,1,0:T(4,128)S(1)}, f32[32,3,256]{2,1,0:T(4,128)}, u32[]{:S(2)}) copy-start(f32[32,3,256]{2,1,0:T(4,128)} %get-tuple-element.64) | copy-start | bytes 294916
  16.8 3.9 %copy-start.4 = (f32[32,3,256]{2,1,0:T(4,128)S(1)}, f32[32,3,256]{2,1,0:T(4,128)}, u32[]{:S(2)}) copy-start(f32[32,3,256]{2,1,0:T(4,128)} %get-tuple-element.65) | copy-start | bytes 294916
  21.2 2.5 %copy-start.11 = (f32[134,128]{1,0:T(8,128)S(1)}, f32[134,128]{1,0:T(8,128)}, u32[]{:S(2)}) copy-start(f32[134,128]{1,0:T(8,128)} %constant.98.clone) | copy-start | bytes 205828
  23.7 3.8 %copy-start.25 = (s32[3,7]{1,0:T(4,128)S(1)}, s32[3,7]{1,0:T(4,128)}, u32[]{:S(2)}) copy-start(s32[3,7]{1,0:T(4,128)} %param.24) | copy-start | bytes 256
  23.7 3.8 %copy-start.26 = (f32[16]{0:T(128)S(1)}, f32[16]{0:T(128)}, u32[]{:S(2)}) copy-start(f32[16]{0:T(128)} %param.23) | copy-start | bytes 196
  23.7 4.8 %copy-start.27 = (f32[256,256,1]{1,0,2:T(8,128)S(1)}, f32[256,256,1]{1,0,2:T(8,128)}, u32[]{:S(2)}) copy-start(f32[256,256,1]{1,0,2:T(8,128)} %constant.111) | copy-start | bytes 786436
  39.6 19.0 %copy-start.2 = (f32[16,64,128]{2,1,0:T(8,128)S(1)}, f32[16,64,128]{2,1,0:T(8,128)}, u32[]{:S(2)}) copy-start(f32[16,64,128]{2,1,0:T(8,128)} %slice.486.refs_0_) | copy-start | bytes 1572868
  60.0 0.8 copy-start.13
  60.7 1.6 %copy-start.28 = (f32[128,128,1]{1,0,2:T(8,128)S(1)}, f32[128,128,1]{1,0,2:T(8,128)}, u32[]{:S(2)}) copy-start(f32[128,128,1]{1,0,2:T(8,128)} %constant.112) | copy-start | bytes 196612
  62.3 6.2 %copy-start.22 = (f32[38,32]{0,1:T(8,128)S(1)}, f32[38,32]{0,1:T(8,128)}, u32[]{:S(2)}) copy-start(f32[38,32]{0,1:T(8,128)} %constant.102.clone) | copy-start | bytes 14596
  62.3 6.5 %copy-start.30 = (f32[64,64,1]{1,0,2:T(8,128)S(1)}, f32[64,64,1]{1,0,2:T(8,128)}, u32[]{:S(2)}) copy-start(f32[64,64,1]{1,0,2:T(8,128)} %constant.113) | copy-start | bytes 49156
  68.3 17.5 %copy-start.29 = (f32[64,64,1,1,1]{1,0,4,3,2:T(8,128)S(1)}, f32[64,64,1,1,1]{1,0,4,3,2:T(8,128)}, u32[]{:S(2)}) copy-start(f32[64,64,1,1,1]{1,0,4,3,2:T(8,128)} %constant.114) | copy-start | bytes 49156
  68.4 19.0 %copy-start.24 = (f32[24,40]{1,0:T(8,128)S(1)}, f32[24,40]{1,0:T(8,128)}, u32[]{:S(2)}) copy-start(f32[24,40]{1,0:T(8,128)} %constant.104.clone) | copy-start | bytes 11524
  68.7 19.3 %copy-start.23 = (f32[24,40]{1,0:T(8,128)S(1)}, f32[24,40]{1,0:T(8,128)}, u32[]{:S(2)}) copy-start(f32[24,40]{1,0:T(8,128)} %constant.105.clone) | copy-start | bytes 11524
  74.3 0.7 copy-start.10
  88.8 3.7 %copy-start.12 = (f32[128,128,1,1,1]{1,0,4,3,2:T(8,128)S(1)}, f32[128,128,1,1,1]{1,0,4,3,2:T(8,128)}, u32[]{:S(2)}) copy-start(f32[128,128,1,1,1]{1,0,4,3,2:T(8,128)} %constant.115) | copy-start | bytes 196612
  88.9 4.2 %copy-start.16 = (f32[38,68]{1,0:T(8,128)S(1)}, f32[38,68]{1,0:T(8,128)}, u32[]{:S(2)}) copy-start(f32[38,68]{1,0:T(8,128)} %constant.106.clone) | copy-start | bytes 31012
  89.1 5.2 %copy-start.17 = (f32[38,68]{1,0:T(8,128)S(1)}, f32[38,68]{1,0:T(8,128)}, u32[]{:S(2)}) copy-start(f32[38,68]{1,0:T(8,128)} %constant.107.clone) | copy-start | bytes 31012
  95.3 2.2 %copy-start.1 = (f32[32,128,256]{2,1,0:T(8,128)S(1)}, f32[32,128,256]{2,1,0:T(8,128)}, u32[]{:S(2)}) copy-start(f32[32,128,256]{2,1,0:T(8,128)} %get-tuple-element.132) | copy-start | bytes 12582916
  95.7 2.0 %copy-start.5 = (f32[2,2,2,64,256]{4,3,2,1,0:T(8,128)S(1)}, f32[2,2,2,64,256]{4,3,2,1,0:T(8,128)}, u32[]{:S(2)}) copy-start(f32[2,2,2,64,256]{4,3,2,1,0:T(8,128)} %get-tuple-element.70) | copy-start | bytes 1572868
  95.7 2.1 %copy-start.6 = (f32[2,2,2,64,256]{4,3,2,1,0:T(8,128)S(1)}, f32[2,2,2,64,256]{4,3,2,1,0:T(8,128)}, u32[]{:S(2)}) copy-start(f32[2,2,2,64,256]{4,3,2,1,0:T(8,128)} %get-tuple-element.75) | copy-start | bytes 1572868
  95.8 2.1 %copy-start.8 = (f32[2,16,2,2,256]{4,3,2,1,0:T(2,128)S(1)}, f32[2,16,2,2,256]{4,3,2,1,0:T(2,128)}, u32[]{:S(2)}) copy-start(f32[2,16,2,2,256]{4,3,2,1,0:T(2,128)} %get-tuple-element.72) | copy-start | bytes 393220
  95.8 2.2 %copy-start.9 = (f32[2,16,2,2,256]{4,3,2,1,0:T(2,128)S(1)}, f32[2,16,2,2,256]{4,3,2,1,0:T(2,128)}, u32[]{:S(2)}) copy-start(f32[2,16,2,2,256]{4,3,2,1,0:T(2,128)} %get-tuple-element.73) | copy-start | bytes 393220
  95.8 2.2 %copy-start.18 = (f32[2,2,2,2,256]{4,3,2,1,0:T(2,128)S(1)}, f32[2,2,2,2,256]{4,3,2,1,0:T(2,128)}, u32[]{:S(2)}) copy-start(f32[2,2,2,2,256]{4,3,2,1,0:T(2,128)} %get-tuple-element.69) | copy-start | bytes 49156
  95.8 2.2 %copy-start.19 = (f32[2,2,2,2,256]{4,3,2,1,0:T(2,128)S(1)}, f32[2,2,2,2,256]{4,3,2,1,0:T(2,128)}, u32[]{:S(2)}) copy-start(f32[2,2,2,2,256]{4,3,2,1,0:T(2,128)} %get-tuple-element.71) | copy-start | bytes 49156
  95.8 2.2 %copy-start.20 = (f32[2,2,2,2,256]{4,3,2,1,0:T(2,128)S(1)}, f32[2,2,2,2,256]{4,3,2,1,0:T(2,128)}, u32[]{:S(2)}) copy-start(f32[2,2,2,2,256]{4,3,2,1,0:T(2,128)} %get-tuple-element.74) | copy-start | bytes 49156
  95.8 2.1 %copy-start.21 = (f32[2,2,2,2,256]{4,3,2,1,0:T(2,128)S(1)}, f32[2,2,2,2,256]{4,3,2,1,0:T(2,128)}, u32[]{:S(2)}) copy-start(f32[2,2,2,2,256]{4,3,2,1,0:T(2,128)} %get-tuple-element.76) | copy-start | bytes 49156
  98.0 1.2 copy-start.7
  99.1 2.6 %copy-start.14 = (f32[68,128]{1,0:T(8,128)S(1)}, f32[68,128]{1,0:T(8,128)}, u32[]{:S(2)}) copy-start(f32[68,128]{1,0:T(8,128)} %constant.109.clone) | copy-start | bytes 104452
  101.8 4.7 %copy-start.15 = (f32[68,128]{1,0:T(8,128)S(1)}, f32[68,128]{1,0:T(8,128)}, u32[]{:S(2)}) copy-start(f32[68,128]{1,0:T(8,128)} %constant.108.clone) | copy-start | bytes 104452

commit v8 on v6

--- a/solution.py
+++ b/solution.py
@@ -216,14 +216,16 @@
     return jnp.sign(coeffs) * jnp.maximum(jnp.abs(coeffs) - thresh, 0.0)
 
 
-def synthesis_ext(extended):
+def synthesis_ext(extended, trim=0):
     two, hx4, _, hy4, size_z = extended.shape
     z_part = contract(extended, jnp.asarray(periodic_analysis(size_z)), ((4,), (1,)), ((), ()))
     z_part = z_part.reshape(2 * hx4, 2, hy4, size_z)
     size_y = 2 * (hy4 - 4)
     matrix = split_synthesis(size_y)
+    if trim:
+        matrix = np.ascontiguousarray(matrix[:, :, trim : size_y - trim])
     y_part = batched_left(matrix[0], z_part[:, 0]) + batched_left(matrix[1], z_part[:, 1])
-    y_part = y_part.reshape(2, hx4, size_y, size_z)
+    y_part = y_part.reshape(2, hx4, matrix.shape[2], size_z)
     return synthesise_lead(y_part[0], y_part[1])
 
 
@@ -241,16 +243,17 @@
     EXCHANGE_IDS[0] = 0
     cube0 = analysis_ext(halo(velocity, 0, 3, 1, 3))
     shrunk0 = blocked(shrink_field(cube0, threshold_table, band_index[0]))
-    ext1, ext0 = halos([(low_corner(cube0), 0, 9, 1, 9), (shrunk0, 1, 2, 3, 2)])
+    ext1, ext0 = halos([(low_corner(cube0), 0, 9, 1, 11), (shrunk0, 1, 2, 3, 2)])
     cube1 = analysis_ext(ext1)
     shrunk1 = blocked(shrink_field(cube1, threshold_table, band_index[1]))
-    cube2 = analysis_ext(low_corner(cube1))
+    approx2 = low_corner(cube1)
+    cube2 = analysis_ext(approx2[:, 1 : approx2.shape[1] - 1])
     shrunk2 = shrink_field(cube2, threshold_table, band_index[2])
     full2 = lax.dynamic_update_slice(shrunk2, low_corner(cube2), (0, 0, 0))
     recon2 = synthesis_ext(halo(blocked(full2), 1, 4, 3, 4))
-    recon2 = recon2[1 : recon2.shape[0] - 1, 1 : recon2.shape[1] - 1]
+    recon2 = recon2[1 : recon2.shape[0] - 1]
     half_z = shrunk1.shape[4] // 2
-    recon1 = synthesis_ext(shrunk1.at[0, :, 0, :, :half_z].set(recon2))
+    recon1 = synthesis_ext(shrunk1.at[0, :, 0, :, :half_z].set(recon2), trim=2)
     half_z = ext0.shape[4] // 2
     return synthesis_ext(ext0.at[0, :, 0, :, :half_z].set(recon1))
 

time: 119 us -> 119 us (level)
  no operation moved by 1% of the time
where the time goes in v8:
time: 119 us
  Pallas kernels  46.7 us (39%)
  other arithmetic  28.2 us (24%)
  matrix products  27.6 us (23%)
  local copies, waits for them, and re-layouts  15.6 us (13%)
    pallas_call x3, Pallas kernels, halos(): pl.pallas_call(functools.partial(exchange_kernel, layouts, lax.axis_size(...  46.7 us
    dot_general x15, matrix products, contract(): lax.dot_general(left, right, (dims, batch), precision=PREC, preferred_ele...  27.6 us
    select_n x3, other arithmetic, shrink_field(): high_z = jnp.where(plane_ids + 1 == band_no, eight[band_no], high_z)  13.2 us
    concatenate x3, other arithmetic, assemble(): return jnp.concatenate([top, mid, bottom], axis=dx)  5.64 us
    another operation x3, local copies, waits for them, and re-layouts, synthesise_lead(): joined = jnp.stack([even, odd], axis=1)  5.42 us
    another operation x6, other arithmetic, synthesise_lead(): joined = jnp.stack([even, odd], axis=1)  5.38 us
    unnamed x62, local copies, waits for them, and re-layouts  3.61 us
    scatter x1, local copies, waits for them, and re-layouts, local(): recon1 = synthesis_ext(shrunk1.at[0, :, 0, :, :half_z].set(recon2), trim=2)  3.46 us

profile of v8, /device:TPU:8, one launch (start us, length us, event | category | flops | bytes accessed | tf_op | source)
XLA Modules:
  0.0 118.9 jit_solution(16965806867115704634)
XLA Ops:
  0.0 16.7 %shard_map.172 = (f32[3,128,256]{2,1,0:T(8,128)}, f32[3,128,256]{2,1,0:T(8,128)}, f32[32,3,256]{2,1,0:T(4,128)}, f32[32,3,256]{2,1,0:T(4,128)}, f32[3,3,256]{2,1...) custom-call(f32[32,128,256]{2,1,0:T(8,128)} %refs_0_.1), custom_call_target="tpu_custom_call" | custom-call | tf_op jit(solution)/shard_map/pallas_call | solution.py:122
  16.8 3.2 %maximum_maximum_fusion.1 = f32[38,134,256]{2,1,0:T(8,128)S(1)} fusion(f32[3,3,256]{2,1,0:T(4,128)} %get-tuple-element.68, f32[3,128,256]{2,1,0:T(8,128)} %get-tuple-element.67, f32[3,3,256]{2,1,0:T(4,128)} %get-tuple-element.66, f32[32,3,256]{2,1,0:T(4,128)} %get-tuple-element.65, f32[32,128,256]{2,1,0:T(8,128)} %refs_0_.1, ...), kind=kLoop, calls=%fused_computation.1 | loop fusion | flops 10428416 | bytes 10428416 | tf_op jit(solution)/shard_map/concatenate | solution.py:141
  20.0 0.7 copy-done
  20.6 0.0 copy-done.4
  20.7 0.5 pad_maximum_fusion
  21.2 0.0 copy-start.12
  21.2 2.5 %multiply_add_fusion.1 = (f32[16,134,256]{2,1,0:T(8,128)S(1)}, f32[16,134,256]{2,1,0:T(8,128)S(1)}) fusion(f32[38,134,256]{2,1,0:T(8,128)S(1)} %maximum_maximum_fusion.1, f32[32,134,256]{2,1,0:T(8,128)S(1)} %pad_maximum_fusion), kind=kLoop, calls=%fused_computation.15 | loop fusion | flops 16465920 | bytes 21954560 | tf_op jit(solution)/shard_map/add | solution.py:165
  23.7 0.0 copy-start.9
  23.8 3.8 %fusion = f32[32,128,256]{2,1,0:T(8,128)S(1)} fusion(f32[16,134,256]{2,1,0:T(8,128)S(1)} %get-tuple-element.97, f32[16,134,256]{2,1,0:T(8,128)S(1)} %get-tuple-element.96, f32[134,128]{1,0:T(8,128)S(1)} %copy-done.12), kind=kOutput, calls=%fused_computation.4 | convolution fusion | flops 844152832 | bytes 8653824 | tf_op jit(solution)/shard_map/dot_general | solution.py:149
  27.6 0.2 select_reduce_fusion
  27.8 0.7 fusion.87
  28.5 4.4 %select_select_fusion.3 = (f32[32,128]{1,0:T(8,128)S(1)}, f32[32,128]{1,0:T(8,128)S(1)}) fusion(f32[]{:T(128)} %bitcast.5, f32[]{:T(128)} %bitcast.4, f32[]{:T(128)} %bitcast.3, f32[]{:T(128)} %bitcast.2, s32[128]{0:T(128)S(1)} %broadcast_select_fusion, s32[32]{0:T(128)S(1)} %compare_select_fusion.4, f32[]{:T(128)} %bitcast.8, f32[]{:T(128)} %bitcast.7, ...), kind=kLoop, calls=%fused_computation.126 | loop fusion | flops 65536 | bytes 33436 | tf_op jit(solution)/shard_map/jit(_where)/select_n | solution.py:213
  32.9 4.4 %maximum_multiply_fusion = (f32[32,128,256]{2,1,0:T(8,128)}, f32[32,128,256]{2,1,0:T(8,128)S(1)}) fusion(f32[32,128]{1,0:T(8,128)S(1)} %get-tuple-element.116, f32[32,128]{1,0:T(8,128)S(1)} %get-tuple-element.115, pred[256]{0:T(512)(128)(4,1)S(1)} %iota_compare_fusion.3, f32[32,128,256]{2,1,0:T(8,128)S(1)} %fusion, f32[256,256,1]{1,0,2:T(8,128)S(1)} %copy-done.9), kind=kOutput, calls=%fused_computation.9 | convolution fusion | flops 1616904192 | bytes 12878080 | tf_op jit(solution)/shard_map/dot_general | solution.py:149
  37.2 0.8 slice.488.refs_0_
  38.1 19.2 %shard_map.173 = (f32[9,64,128]{2,1,0:T(8,128)}, f32[9,64,128]{2,1,0:T(8,128)}, f32[16,11,128]{2,1,0:T(8,128)}, f32[16,11,128]{2,1,0:T(8,128)}, f32[9,11,128]{2,...) custom-call(f32[16,64,128]{2,1,0:T(8,128)} %slice.488.refs_0_, ...), custom_call_target="tpu_custom_call" | custom-call | tf_op jit(solution)/shard_map/pallas_call | solution.py:122
  57.2 1.4 %maximum_maximum_fusion.2 = f32[34,86,128]{2,1,0:T(8,128)S(1)} fusion(f32[9,11,128]{2,1,0:T(8,128)} %get-tuple-element.84, f32[9,64,128]{2,1,0:T(8,128)} %get-tuple-element.83, f32[9,11,128]{2,1,0:T(8,128)} %get-tuple-element.82, f32[16,11,128]{2,1,0:T(8,128)} %get-tuple-element.81, f32[16,64,128]{2,1,0:T(8,128)S(1)} %copy-done.2, ...), kind=kLoop, calls=%fused_computation.28 | loop fusion | flops 2994176 | bytes 2994176 | tf_op jit(solution)/shard_map/concatenate | solution.py:141
  58.7 0.0 copy-start.15
  58.7 0.7 multiply_add_fusion.3
  59.3 0.0 copy-start.14
  59.3 0.1 copy-done.15
  59.4 0.7 fusion.15
  60.1 0.7 fusion.85
  60.8 4.4 %select_select_fusion.1 = (f32[28,80]{1,0:T(8,128)S(1)}, f32[28,80]{1,0:T(8,128)S(1)}) fusion(f32[]{:T(128)} %bitcast.15, f32[]{:T(128)} %bitcast.14, f32[]{:T(128)} %bitcast.13, f32[]{:T(128)} %bitcast.12, s32[80]{0:T(128)S(1)} %compare_select_fusion.1, s32[28]{0:T(128)S(1)} %compare_select_fusion.2, f32[]{:T(128)} %bitcast.18, f32[]{:T(128)} %bitcast.17, ...), kind=kLoop, calls=%fused_computation.124 | loop fusion | flops 35840 | bytes 18380 | tf_op jit(solution)/shard_map/jit(_where)/select_n | solution.py:213
  65.2 0.0 copy-start.25
  65.2 0.0 copy-start.18
  65.2 0.0 copy-start.30
  65.3 0.9 maximum_multiply_fusion.1
  66.2 0.0 copy-start.27
  66.2 0.1 multiply_add_fusion.5
  66.3 0.0 copy-start.26
  66.3 0.2 fusion.62
  66.6 4.4 %select_select_fusion.5 = (f32[8,32]{1,0:T(8,128)S(1)}, f32[8,32]{1,0:T(8,128)S(1)}) fusion(f32[]{:T(128)} %bitcast.25, f32[]{:T(128)} %bitcast.24, f32[]{:T(128)} %bitcast.23, f32[]{:T(128)} %bitcast.22, s32[32]{0:T(128)S(1)} %compare_select_fusion.3, s32[8]{0:T(128)S(1)} %compare_select_fusion, f32[]{:T(128)} %bitcast.28, f32[]{:T(128)} %bitcast.27, ...), kind=kLoop, calls=%fused_computation.136 | loop fusion | flops 4096 | bytes 2236 | tf_op jit(solution)/shard_map/jit(_where)/select_n | solution.py:213
  71.0 0.2 maximum_multiply_fusion.2
  71.2 0.8 dynamic_update_slice.3
  72.0 0.6 copy-done.7
  72.7 10.8 %shard_map.174 = (f32[2,4,2,16,64]{4,3,2,1,0:T(8,128)}, f32[2,4,2,16,64]{4,3,2,1,0:T(8,128)}, f32[2,4,2,4,64]{4,3,2,1,0:T(4,128)}, f32[2,4,2,4,64]{4,3,2,1,0:T(4...) custom-call(f32[2,4,2,16,64]{4,3,2,1,0:T(8,128)} %bitcast.124), custom_call_target="tpu_custom_call" | custom-call | tf_op jit(solution)/shard_map/pallas_call | solution.py:122
  83.5 1.6 %fusion.23 = f32[2,12,2,24,64]{4,3,2,1,0:T(8,128)S(1)} fusion(f32[64,64,1,1,1]{1,0,4,3,2:T(8,128)S(1)} %copy-done.30, f32[2,4,2,4,64]{4,3,2,1,0:T(4,128)} %get-tuple-element.92, f32[2,4,2,16,64]{4,3,2,1,0:T(8,128)} %get-tuple-element.91, f32[2,4,2,4,64]{4,3,2,1,0:T(4,128)} %get-tuple-element.90, f32[2,4,2,4,64]{4,3,2,1,0:T(4,128)} %get-tuple-element.89, ...), kind=kOutput, calls=%fused_computation.44 | convolution fusion | flops 28901376 | bytes 606208 | tf_op jit(solution)/shard_map/dot_general | solution.py:149
  85.1 0.6 fusion.51
  85.8 0.6 fusion.19
  86.4 0.0 copy-start.13
  86.4 0.2 fusion.61
  86.6 0.0 copy-start.19
  86.7 0.0 copy-start.20
  86.7 3.5 %scatter.6 = f32[2,14,2,40,128]{4,3,2,1,0:T(8,128)S(1)} dynamic-update-slice(f32[2,14,2,40,128]{4,3,2,1,0:T(8,128)S(1)} %bitcast.119, f32[1,14,1,40,64]{4,3,2,1,0:T(8,128)S(1)} %slice_bitcast_fusion.14, s32[]{:T(128)} %constant.86.clone.1, s32[]{:T(128)} %constant.86.clone.1, s32[]{:T(128)} %constant.86.clone.1, s32[]{:T(128)} %constant.86.clone.1, s32[]{:T(128)} %constant.86.clone.1) | dynamic-update-slice | bytes 286724 | tf_op jit(solution)/shard_map/scatter | solution.py:256
  90.2 0.6 fusion.88
  90.8 1.0 fusion.41
  91.9 1.1 fusion.14
  93.0 0.4 fusion.50
  93.4 0.1 pad_maximum_fusion.2
  93.5 1.6 %copy-done.1 = f32[32,128,256]{2,1,0:T(8,128)S(1)} copy-done((f32[32,128,256]{2,1,0:T(8,128)S(1)}, f32[32,128,256]{2,1,0:T(8,128)}, u32[]{:S(2)}) %copy-start.1) | copy-done | bytes 4194328
  95.1 0.2 copy-done.5
  95.3 0.2 copy-done.6
  95.5 0.0 copy-done.10
  95.5 0.0 copy-done.11
  95.6 0.0 copy-start.8
  95.6 1.1 maximum_maximum_fusion
  96.6 0.1 constant_dynamic-update-slice_fusion
  96.7 2.6 %fusion.89 = f32[2,20,2,68,256]{4,3,2,1,0:T(8,128)S(1)} fusion(f32[2,20,2,68,256]{4,3,2,1,0:T(8,128)S(1)} %constant_dynamic-update-slice_fusion, f32[256,256,1,1,1]{1,0,4,3,2:T(8,128)S(1)} %copy-done.8), kind=kOutput, calls=%fused_computation.164 | convolution fusion | flops 2139095040 | bytes 11403264 | tf_op jit(solution)/shard_map/dot_general | solution.py:149
  99.4 0.0 copy-start.17
  99.4 4.7 %fusion.4 = f32[40,256,128]{2,1,0:T(8,128)S(1)} fusion(f32[40,2,68,256]{3,2,1,0:T(8,128)S(1)} %bitcast.115, f32[68,128]{1,0:T(8,128)S(1)} %copy-done.16), kind=kOutput, calls=%fused_computation.11 | convolution fusion | flops 534773760 | bytes 8228864 | tf_op jit(solution)/shard_map/dot_general | solution.py:149
  104.1 4.7 %add_bitcast_fusion = f32[40,128,256]{1,2,0:T(8,128)S(1)} fusion(f32[40,256,128]{2,1,0:T(8,128)S(1)} %fusion.4, f32[40,2,68,256]{3,2,1,0:T(8,128)S(1)} %bitcast.116, f32[68,128]{1,0:T(8,128)S(1)} %copy-done.17), kind=kOutput, calls=%fused_computation.2 | convolution fusion | flops 536084480 | bytes 13471744 | tf_op jit(solution)/shard_map/dot_general | solution.py:149
  108.8 2.3 %fusion.13 = (f32[16,1,128,256]{2,3,0,1:T(8,128)S(1)}, f32[16,1,128,256]{2,3,0,1:T(8,128)S(1)}) fusion(f32[40,128,256]{1,2,0:T(8,128)S(1)} %add_bitcast_fusion), kind=kLoop, calls=%fused_computation.26 | loop fusion | flops 15728640 | bytes 25165824 | tf_op jit(solution)/shard_map/stack | solution.py:184
  111.1 2.4 %pad_maximum_fusion.1 = f32[16,2,128,256]{2,3,0,1:T(8,128)} fusion(f32[16,1,128,256]{2,3,0,1:T(8,128)S(1)} %get-tuple-element.99, f32[16,1,128,256]{2,3,0,1:T(8,128)S(1)} %get-tuple-element.98), kind=kLoop, calls=%fused_computation.8 | loop fusion | flops 1048576 | bytes 8388608 | tf_op jit(solution)/shard_map/stack | solution.py:184
  113.5 5.3 %copy.45 = f32[16,2,128,256]{3,2,1,0:T(8,128)} copy(f32[16,2,128,256]{2,3,0,1:T(8,128)} %pad_maximum_fusion.1) | data formatting | bytes 8388608 | tf_op jit(solution)/shard_map/stack | solution.py:184
  (55 shorter events, 0.3 us)
Async XLA Ops:
  16.7 3.9 %copy-start = (f32[32,128,256]{2,1,0:T(8,128)S(1)}, f32[32,128,256]{2,1,0:T(8,128)}, u32[]{:S(2)}) copy-start(f32[32,128,256]{2,1,0:T(8,128)} %refs_0_.1) | copy-start | bytes 12582916
  16.7 3.9 %copy-start.3 = (f32[32,3,256]{2,1,0:T(4,128)S(1)}, f32[32,3,256]{2,1,0:T(4,128)}, u32[]{:S(2)}) copy-start(f32[32,3,256]{2,1,0:T(4,128)} %get-tuple-element.64) | copy-start | bytes 294916
  16.8 3.9 %copy-start.4 = (f32[32,3,256]{2,1,0:T(4,128)S(1)}, f32[32,3,256]{2,1,0:T(4,128)}, u32[]{:S(2)}) copy-start(f32[32,3,256]{2,1,0:T(4,128)} %get-tuple-element.65) | copy-start | bytes 294916
  21.2 2.5 %copy-start.12 = (f32[134,128]{1,0:T(8,128)S(1)}, f32[134,128]{1,0:T(8,128)}, u32[]{:S(2)}) copy-start(f32[134,128]{1,0:T(8,128)} %constant.98.clone) | copy-start | bytes 205828
  23.7 3.8 %copy-start.28 = (s32[3,7]{1,0:T(4,128)S(1)}, s32[3,7]{1,0:T(4,128)}, u32[]{:S(2)}) copy-start(s32[3,7]{1,0:T(4,128)} %param.24) | copy-start | bytes 256
  23.7 3.8 %copy-start.29 = (f32[16]{0:T(128)S(1)}, f32[16]{0:T(128)}, u32[]{:S(2)}) copy-start(f32[16]{0:T(128)} %param.23) | copy-start | bytes 196
  23.7 9.1 %copy-start.9 = (f32[256,256,1]{1,0,2:T(8,128)S(1)}, f32[256,256,1]{1,0,2:T(8,128)}, u32[]{:S(2)}) copy-start(f32[256,256,1]{1,0,2:T(8,128)} %constant.111) | copy-start | bytes 786436
  38.1 19.2 %copy-start.2 = (f32[16,64,128]{2,1,0:T(8,128)S(1)}, f32[16,64,128]{2,1,0:T(8,128)}, u32[]{:S(2)}) copy-start(f32[16,64,128]{2,1,0:T(8,128)} %slice.488.refs_0_) | copy-start | bytes 1572868
  58.7 0.8 copy-start.15
  59.3 5.9 %copy-start.14 = (f32[128,128,1]{1,0,2:T(8,128)S(1)}, f32[128,128,1]{1,0,2:T(8,128)}, u32[]{:S(2)}) copy-start(f32[128,128,1]{1,0,2:T(8,128)} %constant.112) | copy-start | bytes 196612
  65.2 1.1 copy-start.25
  65.2 5.8 %copy-start.18 = (f32[64,64,1]{1,0,2:T(8,128)S(1)}, f32[64,64,1]{1,0,2:T(8,128)}, u32[]{:S(2)}) copy-start(f32[64,64,1]{1,0,2:T(8,128)} %constant.113) | copy-start | bytes 49156
  65.2 18.3 %copy-start.30 = (f32[64,64,1,1,1]{1,0,4,3,2:T(8,128)S(1)}, f32[64,64,1,1,1]{1,0,4,3,2:T(8,128)}, u32[]{:S(2)}) copy-start(f32[64,64,1,1,1]{1,0,4,3,2:T(8,128)} %constant.114) | copy-start | bytes 49156
  66.2 18.9 %copy-start.27 = (f32[24,40]{1,0:T(8,128)S(1)}, f32[24,40]{1,0:T(8,128)}, u32[]{:S(2)}) copy-start(f32[24,40]{1,0:T(8,128)} %constant.104.clone) | copy-start | bytes 11524
  66.3 19.4 %copy-start.26 = (f32[24,40]{1,0:T(8,128)S(1)}, f32[24,40]{1,0:T(8,128)}, u32[]{:S(2)}) copy-start(f32[24,40]{1,0:T(8,128)} %constant.105.clone) | copy-start | bytes 11524
  72.0 0.7 copy-start.7
  86.4 3.8 %copy-start.13 = (f32[128,128,1,1,1]{1,0,4,3,2:T(8,128)S(1)}, f32[128,128,1,1,1]{1,0,4,3,2:T(8,128)}, u32[]{:S(2)}) copy-start(f32[128,128,1,1,1]{1,0,4,3,2:T(8,128)} %constant.115) | copy-start | bytes 196612
  86.6 4.2 %copy-start.19 = (f32[40,68]{1,0:T(8,128)S(1)}, f32[40,68]{1,0:T(8,128)}, u32[]{:S(2)}) copy-start(f32[40,68]{1,0:T(8,128)} %constant.106.clone) | copy-start | bytes 32644
  86.7 5.2 %copy-start.20 = (f32[40,68]{1,0:T(8,128)S(1)}, f32[40,68]{1,0:T(8,128)}, u32[]{:S(2)}) copy-start(f32[40,68]{1,0:T(8,128)} %constant.107.clone) | copy-start | bytes 32644
  92.9 2.2 %copy-start.1 = (f32[32,128,256]{2,1,0:T(8,128)S(1)}, f32[32,128,256]{2,1,0:T(8,128)}, u32[]{:S(2)}) copy-start(f32[32,128,256]{2,1,0:T(8,128)} %get-tuple-element.138) | copy-start | bytes 12582916
  93.3 2.0 %copy-start.5 = (f32[2,2,2,64,256]{4,3,2,1,0:T(8,128)S(1)}, f32[2,2,2,64,256]{4,3,2,1,0:T(8,128)}, u32[]{:S(2)}) copy-start(f32[2,2,2,64,256]{4,3,2,1,0:T(8,128)} %get-tuple-element.70) | copy-start | bytes 1572868
  93.4 2.1 %copy-start.6 = (f32[2,2,2,64,256]{4,3,2,1,0:T(8,128)S(1)}, f32[2,2,2,64,256]{4,3,2,1,0:T(8,128)}, u32[]{:S(2)}) copy-start(f32[2,2,2,64,256]{4,3,2,1,0:T(8,128)} %get-tuple-element.75) | copy-start | bytes 1572868
  93.4 2.1 %copy-start.10 = (f32[2,16,2,2,256]{4,3,2,1,0:T(2,128)S(1)}, f32[2,16,2,2,256]{4,3,2,1,0:T(2,128)}, u32[]{:S(2)}) copy-start(f32[2,16,2,2,256]{4,3,2,1,0:T(2,128)} %get-tuple-element.72) | copy-start | bytes 393220
  93.4 2.2 %copy-start.11 = (f32[2,16,2,2,256]{4,3,2,1,0:T(2,128)S(1)}, f32[2,16,2,2,256]{4,3,2,1,0:T(2,128)}, u32[]{:S(2)}) copy-start(f32[2,16,2,2,256]{4,3,2,1,0:T(2,128)} %get-tuple-element.73) | copy-start | bytes 393220
  93.4 2.2 %copy-start.21 = (f32[2,2,2,2,256]{4,3,2,1,0:T(2,128)S(1)}, f32[2,2,2,2,256]{4,3,2,1,0:T(2,128)}, u32[]{:S(2)}) copy-start(f32[2,2,2,2,256]{4,3,2,1,0:T(2,128)} %get-tuple-element.69) | copy-start | bytes 49156
  93.4 2.2 %copy-start.22 = (f32[2,2,2,2,256]{4,3,2,1,0:T(2,128)S(1)}, f32[2,2,2,2,256]{4,3,2,1,0:T(2,128)}, u32[]{:S(2)}) copy-start(f32[2,2,2,2,256]{4,3,2,1,0:T(2,128)} %get-tuple-element.71) | copy-start | bytes 49156
  93.4 2.2 %copy-start.23 = (f32[2,2,2,2,256]{4,3,2,1,0:T(2,128)S(1)}, f32[2,2,2,2,256]{4,3,2,1,0:T(2,128)}, u32[]{:S(2)}) copy-start(f32[2,2,2,2,256]{4,3,2,1,0:T(2,128)} %get-tuple-element.74) | copy-start | bytes 49156
  93.4 2.1 %copy-start.24 = (f32[2,2,2,2,256]{4,3,2,1,0:T(2,128)S(1)}, f32[2,2,2,2,256]{4,3,2,1,0:T(2,128)}, u32[]{:S(2)}) copy-start(f32[2,2,2,2,256]{4,3,2,1,0:T(2,128)} %get-tuple-element.76) | copy-start | bytes 49156
  95.6 1.2 copy-start.8
  96.7 2.6 %copy-start.16 = (f32[68,128]{1,0:T(8,128)S(1)}, f32[68,128]{1,0:T(8,128)}, u32[]{:S(2)}) copy-start(f32[68,128]{1,0:T(8,128)} %constant.109.clone) | copy-start | bytes 104452
  99.4 4.7 %copy-start.17 = (f32[68,128]{1,0:T(8,128)S(1)}, f32[68,128]{1,0:T(8,128)}, u32[]{:S(2)}) copy-start(f32[68,128]{1,0:T(8,128)} %constant.108.clone) | copy-start | bytes 104452

commit v9 on v8

--- a/solution.py
+++ b/solution.py
@@ -245,15 +245,21 @@
     shrunk0 = blocked(shrink_field(cube0, threshold_table, band_index[0]))
     ext1, ext0 = halos([(low_corner(cube0), 0, 9, 1, 11), (shrunk0, 1, 2, 3, 2)])
     cube1 = analysis_ext(ext1)
-    shrunk1 = blocked(shrink_field(cube1, threshold_table, band_index[1]))
     approx2 = low_corner(cube1)
     cube2 = analysis_ext(approx2[:, 1 : approx2.shape[1] - 1])
     shrunk2 = shrink_field(cube2, threshold_table, band_index[2])
     full2 = lax.dynamic_update_slice(shrunk2, low_corner(cube2), (0, 0, 0))
     recon2 = synthesis_ext(halo(blocked(full2), 1, 4, 3, 4))
     recon2 = recon2[1 : recon2.shape[0] - 1]
-    half_z = shrunk1.shape[4] // 2
-    recon1 = synthesis_ext(shrunk1.at[0, :, 0, :, :half_z].set(recon2), trim=2)
+    shrunk1 = shrink_field(cube1, threshold_table, band_index[1])
+    size1 = cube1.shape
+    padded2 = jnp.pad(recon2, [(0, size1[d] - recon2.shape[d]) for d in range(3)])
+    in_band0 = (
+        (lax.broadcasted_iota(jnp.int32, size1, 0) < size1[0] // 2)
+        & (lax.broadcasted_iota(jnp.int32, size1, 1) < size1[1] // 2)
+        & (lax.broadcasted_iota(jnp.int32, size1, 2) < size1[2] // 2)
+    )
+    recon1 = synthesis_ext(blocked(jnp.where(in_band0, padded2, shrunk1)), trim=2)
     half_z = ext0.shape[4] // 2
     return synthesis_ext(ext0.at[0, :, 0, :, :half_z].set(recon1))
 

time: 119 us -> 117 us (0.983)
  local copies, waits for them, and re-layouts: 15.6 us -> 12.2 us
    scatter x1 -> x0, local copies, waits for them, and re-layouts: 3.46 us -> none  [local(): recon1 = synthesis_ext(shrunk1.at[0, :, 0, :, :half_z].set(recon2), trim=2)]
where the time goes in v9:
time: 117 us; the launch traced here: 116 us
  Pallas kernels  46.7 us (40%)
  other arithmetic  29 us (25%)
  matrix products  27.3 us (23%)
  local copies, waits for them, and re-layouts  12.2 us (10%)
    pallas_call x3, Pallas kernels, halos(): pl.pallas_call(functools.partial(exchange_kernel, layouts, lax.axis_size(...  46.7 us
    dot_general x15, matrix products, contract(): lax.dot_general(left, right, (dims, batch), precision=PREC, preferred_ele...  27.3 us
    select_n x3, other arithmetic, shrink_field(): high_z = jnp.where(plane_ids + 1 == band_no, eight[band_no], high_z)  13.3 us
    concatenate x3, other arithmetic, assemble(): return jnp.concatenate([top, mid, bottom], axis=dx)  5.64 us
    another operation x3, local copies, waits for them, and re-layouts, synthesise_lead(): joined = jnp.stack([even, odd], axis=1)  5.42 us
    another operation x6, other arithmetic, synthesise_lead(): joined = jnp.stack([even, odd], axis=1)  5.38 us
    unnamed x62, local copies, waits for them, and re-layouts  3.67 us
    add x3, other arithmetic, analyse_lead(): low = low + filt_low[j] * taken  3.26 us

profile of v9, /device:TPU:8, one launch (start us, length us, event | category | flops | bytes accessed | tf_op | source)
XLA Modules:
  0.0 115.9 jit_solution(2334550823932335647)
XLA Ops:
  0.0 16.7 %shard_map.172 = (f32[3,128,256]{2,1,0:T(8,128)}, f32[3,128,256]{2,1,0:T(8,128)}, f32[32,3,256]{2,1,0:T(4,128)}, f32[32,3,256]{2,1,0:T(4,128)}, f32[3,3,256]{2,1...) custom-call(f32[32,128,256]{2,1,0:T(8,128)} %refs_0_.1), custom_call_target="tpu_custom_call" | custom-call | tf_op jit(solution)/shard_map/pallas_call | solution.py:122
  16.8 3.2 %maximum_maximum_fusion.1 = f32[38,134,256]{2,1,0:T(8,128)S(1)} fusion(f32[3,3,256]{2,1,0:T(4,128)} %get-tuple-element.56, f32[3,128,256]{2,1,0:T(8,128)} %get-tuple-element.55, f32[3,3,256]{2,1,0:T(4,128)} %get-tuple-element.54, f32[32,3,256]{2,1,0:T(4,128)} %get-tuple-element.53, f32[32,128,256]{2,1,0:T(8,128)} %refs_0_.1, ...), kind=kLoop, calls=%fused_computation.1 | loop fusion | flops 10428416 | bytes 10428416 | tf_op jit(solution)/shard_map/concatenate | solution.py:141
  20.0 0.7 copy-done
  20.6 0.0 copy-done.4
  20.7 0.5 pad_maximum_fusion
  21.2 0.0 copy-start.12
  21.2 2.5 %multiply_add_fusion.1 = (f32[16,134,256]{2,1,0:T(8,128)S(1)}, f32[16,134,256]{2,1,0:T(8,128)S(1)}) fusion(f32[38,134,256]{2,1,0:T(8,128)S(1)} %maximum_maximum_fusion.1, f32[32,134,256]{2,1,0:T(8,128)S(1)} %pad_maximum_fusion), kind=kLoop, calls=%fused_computation.15 | loop fusion | flops 16465920 | bytes 21954560 | tf_op jit(solution)/shard_map/add | solution.py:165
  23.7 0.0 copy-start.28
  23.7 0.0 copy-start.9
  23.8 3.8 %fusion = f32[32,128,256]{2,1,0:T(8,128)S(1)} fusion(f32[16,134,256]{2,1,0:T(8,128)S(1)} %get-tuple-element.85, f32[16,134,256]{2,1,0:T(8,128)S(1)} %get-tuple-element.84, f32[134,128]{1,0:T(8,128)S(1)} %copy-done.12), kind=kOutput, calls=%fused_computation.4 | convolution fusion | flops 844152832 | bytes 8653824 | tf_op jit(solution)/shard_map/dot_general | solution.py:149
  27.6 0.2 select_reduce_fusion
  27.8 0.7 fusion.87
  28.5 4.4 %select_select_fusion.3 = (f32[32,128]{1,0:T(8,128)S(1)}, f32[32,128]{1,0:T(8,128)S(1)}) fusion(f32[]{:T(128)} %bitcast.5, f32[]{:T(128)} %bitcast.4, f32[]{:T(128)} %bitcast.3, f32[]{:T(128)} %bitcast.2, s32[128]{0:T(128)S(1)} %broadcast_select_fusion, s32[32]{0:T(128)S(1)} %compare_select_fusion.4, f32[]{:T(128)} %bitcast.8, f32[]{:T(128)} %bitcast.7, ...), kind=kLoop, calls=%fused_computation.125 | loop fusion | flops 65536 | bytes 33436 | tf_op jit(solution)/shard_map/jit(_where)/select_n | solution.py:213
  32.9 4.4 %maximum_multiply_fusion = (f32[32,128,256]{2,1,0:T(8,128)}, f32[32,128,256]{2,1,0:T(8,128)S(1)}) fusion(f32[32,128]{1,0:T(8,128)S(1)} %get-tuple-element.104, f32[32,128]{1,0:T(8,128)S(1)} %get-tuple-element.103, pred[256]{0:T(512)(128)(4,1)S(1)} %iota_compare_fusion.3, f32[32,128,256]{2,1,0:T(8,128)S(1)} %fusion, f32[256,256,1]{1,0,2:T(8,128)S(1)} %copy-done.9), kind=kOutput, calls=%fused_computation.9 | convolution fusion | flops 1616904192 | bytes 12878080 | tf_op jit(solution)/shard_map/dot_general | solution.py:149
  37.2 0.8 slice.454.refs_0_
  38.1 19.2 %shard_map.173 = (f32[9,64,128]{2,1,0:T(8,128)}, f32[9,64,128]{2,1,0:T(8,128)}, f32[16,11,128]{2,1,0:T(8,128)}, f32[16,11,128]{2,1,0:T(8,128)}, f32[9,11,128]{2,...) custom-call(f32[16,64,128]{2,1,0:T(8,128)} %slice.454.refs_0_, ...), custom_call_target="tpu_custom_call" | custom-call | tf_op jit(solution)/shard_map/pallas_call | solution.py:122
  57.2 1.4 %maximum_maximum_fusion.2 = f32[34,86,128]{2,1,0:T(8,128)S(1)} fusion(f32[9,11,128]{2,1,0:T(8,128)} %get-tuple-element.72, f32[9,64,128]{2,1,0:T(8,128)} %get-tuple-element.71, f32[9,11,128]{2,1,0:T(8,128)} %get-tuple-element.70, f32[16,11,128]{2,1,0:T(8,128)} %get-tuple-element.69, f32[16,64,128]{2,1,0:T(8,128)S(1)} %copy-done.2, ...), kind=kLoop, calls=%fused_computation.28 | loop fusion | flops 2994176 | bytes 2994176 | tf_op jit(solution)/shard_map/concatenate | solution.py:141
  58.7 0.0 copy-start.15
  58.7 0.7 multiply_add_fusion.3
  59.3 0.0 copy-start.14
  59.3 0.1 copy-done.15
  59.4 0.7 fusion.15
  60.1 0.1 copy-done.14
  60.2 0.6 fusion.88
  60.8 0.0 copy-start.27
  60.8 0.1 multiply_add_fusion.5
  60.9 0.0 copy-start.26
  61.0 0.2 fusion.62
  61.2 0.7 fusion.85
  61.9 4.5 %select_select_fusion.5 = (f32[8,32]{1,0:T(8,128)S(1)}, f32[8,32]{1,0:T(8,128)S(1)}) fusion(f32[]{:T(128)} %bitcast.16, f32[]{:T(128)} %bitcast.15, f32[]{:T(128)} %bitcast.14, f32[]{:T(128)} %bitcast.13, s32[32]{0:T(128)S(1)} %compare_select_fusion.3, s32[8]{0:T(128)S(1)} %compare_select_fusion.2, f32[]{:T(128)} %bitcast.19, f32[]{:T(128)} %bitcast.18, ...), kind=kLoop, calls=%fused_computation.137 | loop fusion | flops 4096 | bytes 2236 | tf_op jit(solution)/shard_map/jit(_where)/select_n | solution.py:213
  66.4 0.2 maximum_multiply_fusion.1
  66.6 0.8 dynamic_update_slice.3
  67.4 0.6 copy-done.7
  68.1 10.8 %shard_map.174 = (f32[2,4,2,16,64]{4,3,2,1,0:T(8,128)}, f32[2,4,2,16,64]{4,3,2,1,0:T(8,128)}, f32[2,4,2,4,64]{4,3,2,1,0:T(4,128)}, f32[2,4,2,4,64]{4,3,2,1,0:T(4...) custom-call(f32[2,4,2,16,64]{4,3,2,1,0:T(8,128)} %bitcast.113), custom_call_target="tpu_custom_call" | custom-call | tf_op jit(solution)/shard_map/pallas_call | solution.py:122
  78.9 1.6 %fusion.23 = f32[2,12,2,24,64]{4,3,2,1,0:T(8,128)S(1)} fusion(f32[64,64,1,1,1]{1,0,4,3,2:T(8,128)S(1)} %copy-done.30, f32[2,4,2,4,64]{4,3,2,1,0:T(4,128)} %get-tuple-element.80, f32[2,4,2,16,64]{4,3,2,1,0:T(8,128)} %get-tuple-element.79, f32[2,4,2,4,64]{4,3,2,1,0:T(4,128)} %get-tuple-element.78, f32[2,4,2,4,64]{4,3,2,1,0:T(4,128)} %get-tuple-element.77, ...), kind=kOutput, calls=%fused_computation.44 | convolution fusion | flops 28901376 | bytes 606208 | tf_op jit(solution)/shard_map/dot_general | solution.py:149
  80.5 0.6 fusion.51
  81.1 0.6 fusion.19
  81.7 0.2 fusion.61
  81.9 0.0 copy-start.13
  82.0 4.4 %select_select_fusion.1 = (f32[28,80]{1,0:T(8,128)S(1)}, f32[28,80]{1,0:T(8,128)S(1)}) fusion(f32[]{:T(128)} %bitcast.34, f32[]{:T(128)} %bitcast.33, f32[]{:T(128)} %bitcast.32, f32[]{:T(128)} %bitcast.31, s32[80]{0:T(128)S(1)} %compare_select_fusion, s32[28]{0:T(128)S(1)} %compare_select_fusion.1, f32[]{:T(128)} %bitcast.37, f32[]{:T(128)} %bitcast.36, ...), kind=kLoop, calls=%fused_computation.123 | loop fusion | flops 35840 | bytes 18380 | tf_op jit(solution)/shard_map/jit(_where)/select_n | solution.py:213
  86.5 0.0 copy-start.19
  86.5 0.7 multiply_select_fusion
  87.2 0.0 copy-start.20
  87.3 0.6 fusion.89
  87.9 1.0 fusion.41
  89.0 1.1 fusion.14
  90.0 0.4 fusion.50
  90.5 0.1 pad_maximum_fusion.2
  90.6 1.6 %copy-done.1 = f32[32,128,256]{2,1,0:T(8,128)S(1)} copy-done((f32[32,128,256]{2,1,0:T(8,128)S(1)}, f32[32,128,256]{2,1,0:T(8,128)}, u32[]{:S(2)}) %copy-start.1) | copy-done | bytes 4194328
  92.2 0.2 copy-done.5
  92.4 0.2 copy-done.6
  92.6 0.0 copy-done.10
  92.6 0.0 copy-done.11
  92.6 0.0 copy-start.8
  92.7 1.1 maximum_maximum_fusion
  93.7 0.1 constant_dynamic-update-slice_fusion
  93.8 0.0 copy-start.16
  93.8 2.6 %fusion.90 = f32[2,20,2,68,256]{4,3,2,1,0:T(8,128)S(1)} fusion(f32[2,20,2,68,256]{4,3,2,1,0:T(8,128)S(1)} %constant_dynamic-update-slice_fusion, f32[256,256,1,1,1]{1,0,4,3,2:T(8,128)S(1)} %copy-done.8), kind=kOutput, calls=%fused_computation.167 | convolution fusion | flops 2139095040 | bytes 11403264 | tf_op jit(solution)/shard_map/dot_general | solution.py:149
  96.5 0.0 copy-start.17
  96.5 4.7 %fusion.4 = f32[40,256,128]{2,1,0:T(8,128)S(1)} fusion(f32[40,2,68,256]{3,2,1,0:T(8,128)S(1)} %bitcast.106, f32[68,128]{1,0:T(8,128)S(1)} %copy-done.16), kind=kOutput, calls=%fused_computation.11 | convolution fusion | flops 534773760 | bytes 8228864 | tf_op jit(solution)/shard_map/dot_general | solution.py:149
  101.2 4.7 %add_bitcast_fusion = f32[40,128,256]{1,2,0:T(8,128)S(1)} fusion(f32[40,256,128]{2,1,0:T(8,128)S(1)} %fusion.4, f32[40,2,68,256]{3,2,1,0:T(8,128)S(1)} %bitcast.107, f32[68,128]{1,0:T(8,128)S(1)} %copy-done.17), kind=kOutput, calls=%fused_computation.2 | convolution fusion | flops 536084480 | bytes 13471744 | tf_op jit(solution)/shard_map/dot_general | solution.py:149
  105.9 2.3 %fusion.13 = (f32[16,1,128,256]{2,3,0,1:T(8,128)S(1)}, f32[16,1,128,256]{2,3,0,1:T(8,128)S(1)}) fusion(f32[40,128,256]{1,2,0:T(8,128)S(1)} %add_bitcast_fusion), kind=kLoop, calls=%fused_computation.26 | loop fusion | flops 15728640 | bytes 25165824 | tf_op jit(solution)/shard_map/stack | solution.py:184
  108.2 2.4 %pad_maximum_fusion.1 = f32[16,2,128,256]{2,3,0,1:T(8,128)} fusion(f32[16,1,128,256]{2,3,0,1:T(8,128)S(1)} %get-tuple-element.87, f32[16,1,128,256]{2,3,0,1:T(8,128)S(1)} %get-tuple-element.86), kind=kLoop, calls=%fused_computation.8 | loop fusion | flops 1048576 | bytes 8388608 | tf_op jit(solution)/shard_map/stack | solution.py:184
  110.6 5.3 %copy.38 = f32[16,2,128,256]{3,2,1,0:T(8,128)} copy(f32[16,2,128,256]{2,3,0,1:T(8,128)} %pad_maximum_fusion.1) | data formatting | bytes 8388608 | tf_op jit(solution)/shard_map/stack | solution.py:184
  (57 shorter events, 0.3 us)
Async XLA Ops:
  16.7 3.9 %copy-start = (f32[32,128,256]{2,1,0:T(8,128)S(1)}, f32[32,128,256]{2,1,0:T(8,128)}, u32[]{:S(2)}) copy-start(f32[32,128,256]{2,1,0:T(8,128)} %refs_0_.1) | copy-start | bytes 12582916
  16.7 3.9 %copy-start.3 = (f32[32,3,256]{2,1,0:T(4,128)S(1)}, f32[32,3,256]{2,1,0:T(4,128)}, u32[]{:S(2)}) copy-start(f32[32,3,256]{2,1,0:T(4,128)} %get-tuple-element.52) | copy-start | bytes 294916
  16.8 3.9 %copy-start.4 = (f32[32,3,256]{2,1,0:T(4,128)S(1)}, f32[32,3,256]{2,1,0:T(4,128)}, u32[]{:S(2)}) copy-start(f32[32,3,256]{2,1,0:T(4,128)} %get-tuple-element.53) | copy-start | bytes 294916
  21.2 2.5 %copy-start.12 = (f32[134,128]{1,0:T(8,128)S(1)}, f32[134,128]{1,0:T(8,128)}, u32[]{:S(2)}) copy-start(f32[134,128]{1,0:T(8,128)} %constant.75.clone) | copy-start | bytes 205828
  23.7 3.8 %copy-start.28 = (s32[3,7]{1,0:T(4,128)S(1)}, s32[3,7]{1,0:T(4,128)}, u32[]{:S(2)}) copy-start(s32[3,7]{1,0:T(4,128)} %param.22) | copy-start | bytes 256
  23.7 3.8 %copy-start.29 = (f32[16]{0:T(128)S(1)}, f32[16]{0:T(128)}, u32[]{:S(2)}) copy-start(f32[16]{0:T(128)} %param.21) | copy-start | bytes 196
  23.7 9.1 %copy-start.9 = (f32[256,256,1]{1,0,2:T(8,128)S(1)}, f32[256,256,1]{1,0,2:T(8,128)}, u32[]{:S(2)}) copy-start(f32[256,256,1]{1,0,2:T(8,128)} %constant.90) | copy-start | bytes 786436
  38.1 19.2 %copy-start.2 = (f32[16,64,128]{2,1,0:T(8,128)S(1)}, f32[16,64,128]{2,1,0:T(8,128)}, u32[]{:S(2)}) copy-start(f32[16,64,128]{2,1,0:T(8,128)} %slice.454.refs_0_) | copy-start | bytes 1572868
  58.7 0.8 copy-start.15
  59.3 0.8 copy-start.14
  60.2 0.8 copy-start.25
  60.2 6.2 %copy-start.18 = (f32[64,64,1]{1,0,2:T(8,128)S(1)}, f32[64,64,1]{1,0,2:T(8,128)}, u32[]{:S(2)}) copy-start(f32[64,64,1]{1,0,2:T(8,128)} %constant.92) | copy-start | bytes 49156
  60.2 18.7 %copy-start.30 = (f32[64,64,1,1,1]{1,0,4,3,2:T(8,128)S(1)}, f32[64,64,1,1,1]{1,0,4,3,2:T(8,128)}, u32[]{:S(2)}) copy-start(f32[64,64,1,1,1]{1,0,4,3,2:T(8,128)} %constant.93) | copy-start | bytes 49156
  60.8 19.7 %copy-start.27 = (f32[24,40]{1,0:T(8,128)S(1)}, f32[24,40]{1,0:T(8,128)}, u32[]{:S(2)}) copy-start(f32[24,40]{1,0:T(8,128)} %constant.81.clone) | copy-start | bytes 11524
  60.9 20.2 %copy-start.26 = (f32[24,40]{1,0:T(8,128)S(1)}, f32[24,40]{1,0:T(8,128)}, u32[]{:S(2)}) copy-start(f32[24,40]{1,0:T(8,128)} %constant.82.clone) | copy-start | bytes 11524
  67.4 0.7 copy-start.7
  81.9 5.3 %copy-start.13 = (f32[128,128,1,1]{1,0,3,2:T(8,128)S(1)}, f32[128,128,1,1]{1,0,3,2:T(8,128)}, u32[]{:S(2)}) copy-start(f32[128,128,1,1]{1,0,3,2:T(8,128)} %constant.94) | copy-start | bytes 196612
  86.5 1.4 %copy-start.19 = (f32[40,68]{1,0:T(8,128)S(1)}, f32[40,68]{1,0:T(8,128)}, u32[]{:S(2)}) copy-start(f32[40,68]{1,0:T(8,128)} %constant.83.clone) | copy-start | bytes 32644
  87.2 1.7 %copy-start.20 = (f32[40,68]{1,0:T(8,128)S(1)}, f32[40,68]{1,0:T(8,128)}, u32[]{:S(2)}) copy-start(f32[40,68]{1,0:T(8,128)} %constant.84.clone) | copy-start | bytes 32644
  90.0 2.2 %copy-start.1 = (f32[32,128,256]{2,1,0:T(8,128)S(1)}, f32[32,128,256]{2,1,0:T(8,128)}, u32[]{:S(2)}) copy-start(f32[32,128,256]{2,1,0:T(8,128)} %get-tuple-element.126) | copy-start | bytes 12582916
  90.4 2.0 %copy-start.5 = (f32[2,2,2,64,256]{4,3,2,1,0:T(8,128)S(1)}, f32[2,2,2,64,256]{4,3,2,1,0:T(8,128)}, u32[]{:S(2)}) copy-start(f32[2,2,2,64,256]{4,3,2,1,0:T(8,128)} %get-tuple-element.58) | copy-start | bytes 1572868
  90.4 2.1 %copy-start.6 = (f32[2,2,2,64,256]{4,3,2,1,0:T(8,128)S(1)}, f32[2,2,2,64,256]{4,3,2,1,0:T(8,128)}, u32[]{:S(2)}) copy-start(f32[2,2,2,64,256]{4,3,2,1,0:T(8,128)} %get-tuple-element.63) | copy-start | bytes 1572868
  90.4 2.1 %copy-start.10 = (f32[2,16,2,2,256]{4,3,2,1,0:T(2,128)S(1)}, f32[2,16,2,2,256]{4,3,2,1,0:T(2,128)}, u32[]{:S(2)}) copy-start(f32[2,16,2,2,256]{4,3,2,1,0:T(2,128)} %get-tuple-element.60) | copy-start | bytes 393220
  90.5 2.2 %copy-start.11 = (f32[2,16,2,2,256]{4,3,2,1,0:T(2,128)S(1)}, f32[2,16,2,2,256]{4,3,2,1,0:T(2,128)}, u32[]{:S(2)}) copy-start(f32[2,16,2,2,256]{4,3,2,1,0:T(2,128)} %get-tuple-element.61) | copy-start | bytes 393220
  90.5 2.2 %copy-start.21 = (f32[2,2,2,2,256]{4,3,2,1,0:T(2,128)S(1)}, f32[2,2,2,2,256]{4,3,2,1,0:T(2,128)}, u32[]{:S(2)}) copy-start(f32[2,2,2,2,256]{4,3,2,1,0:T(2,128)} %get-tuple-element.57) | copy-start | bytes 49156
  90.5 2.2 %copy-start.22 = (f32[2,2,2,2,256]{4,3,2,1,0:T(2,128)S(1)}, f32[2,2,2,2,256]{4,3,2,1,0:T(2,128)}, u32[]{:S(2)}) copy-start(f32[2,2,2,2,256]{4,3,2,1,0:T(2,128)} %get-tuple-element.59) | copy-start | bytes 49156
  90.5 2.2 %copy-start.23 = (f32[2,2,2,2,256]{4,3,2,1,0:T(2,128)S(1)}, f32[2,2,2,2,256]{4,3,2,1,0:T(2,128)}, u32[]{:S(2)}) copy-start(f32[2,2,2,2,256]{4,3,2,1,0:T(2,128)} %get-tuple-element.62) | copy-start | bytes 49156
  90.5 2.1 %copy-start.24 = (f32[2,2,2,2,256]{4,3,2,1,0:T(2,128)S(1)}, f32[2,2,2,2,256]{4,3,2,1,0:T(2,128)}, u32[]{:S(2)}) copy-start(f32[2,2,2,2,256]{4,3,2,1,0:T(2,128)} %get-tuple-element.64) | copy-start | bytes 49156
  92.6 1.2 %copy-start.8 = (f32[256,256,1,1,1]{1,0,4,3,2:T(8,128)S(1)}, f32[256,256,1,1,1]{1,0,4,3,2:T(8,128)}, u32[]{:S(2)}) copy-start(f32[256,256,1,1,1]{1,0,4,3,2:T(8,128)} %constant.95) | copy-start | bytes 786436
  93.8 2.6 %copy-start.16 = (f32[68,128]{1,0:T(8,128)S(1)}, f32[68,128]{1,0:T(8,128)}, u32[]{:S(2)}) copy-start(f32[68,128]{1,0:T(8,128)} %constant.86.clone) | copy-start | bytes 104452
  96.5 4.7 %copy-start.17 = (f32[68,128]{1,0:T(8,128)S(1)}, f32[68,128]{1,0:T(8,128)}, u32[]{:S(2)}) copy-start(f32[68,128]{1,0:T(8,128)} %constant.85.clone) | copy-start | bytes 104452

commit v10 on v9

--- a/solution.py
+++ b/solution.py
@@ -260,8 +260,14 @@
         & (lax.broadcasted_iota(jnp.int32, size1, 2) < size1[2] // 2)
     )
     recon1 = synthesis_ext(blocked(jnp.where(in_band0, padded2, shrunk1)), trim=2)
-    half_z = ext0.shape[4] // 2
-    return synthesis_ext(ext0.at[0, :, 0, :, :half_z].set(recon1))
+    size0 = ext0.shape
+    padded1 = jnp.pad(recon1[None, :, None], [(0, size0[d] - recon1[None, :, None].shape[d]) for d in range(5)])
+    in_band0 = (
+        (lax.broadcasted_iota(jnp.int32, size0, 0) == 0)
+        & (lax.broadcasted_iota(jnp.int32, size0, 2) == 0)
+        & (lax.broadcasted_iota(jnp.int32, size0, 4) < size0[4] // 2)
+    )
+    return synthesis_ext(jnp.where(in_band0, padded1, ext0))
 
 
 def solution(mesh):

time: 117 us -> 116 us (level)
    concatenate x3 -> x2, other arithmetic: 5.64 us -> 4.58 us  [assemble(): return jnp.concatenate([top, mid, bottom], axis=dx)]
where the time goes in v10:
time: 116 us; the launch traced here: 115 us
  Pallas kernels  46.7 us (40%)
  other arithmetic  28 us (24%)
  matrix products  27.9 us (24%)
  local copies, waits for them, and re-layouts  12.2 us (11%)
    pallas_call x3, Pallas kernels, halos(): pl.pallas_call(functools.partial(exchange_kernel, layouts, lax.axis_size(...  46.7 us
    dot_general x15, matrix products, contract(): lax.dot_general(left, right, (dims, batch), precision=PREC, preferred_ele...  27.9 us
    select_n x3, other arithmetic, shrink_field(): high_z = jnp.where(plane_ids + 1 == band_no, eight[band_no], high_z)  13.3 us
    another operation x6, other arithmetic, synthesise_lead(): joined = jnp.stack([even, odd], axis=1)  5.42 us
    another operation x3, local copies, waits for them, and re-layouts, synthesise_lead(): joined = jnp.stack([even, odd], axis=1)  5.42 us
    concatenate x2, other arithmetic, assemble(): return jnp.concatenate([top, mid, bottom], axis=dx)  4.58 us
    unnamed x62, local copies, waits for them, and re-layouts  3.77 us
    add x3, other arithmetic, analyse_lead(): low = low + filt_low[j] * taken  3.26 us

profile of v10, /device:TPU:8, one launch (start us, length us, event | category | flops | bytes accessed | tf_op | source)
XLA Modules:
  0.0 115.5 jit_solution(10608693280740174258)
XLA Ops:
  0.0 16.7 %shard_map.172 = (f32[3,128,256]{2,1,0:T(8,128)}, f32[3,128,256]{2,1,0:T(8,128)}, f32[32,3,256]{2,1,0:T(4,128)}, f32[32,3,256]{2,1,0:T(4,128)}, f32[3,3,256]{2,1...) custom-call(f32[32,128,256]{2,1,0:T(8,128)} %refs_0_.1), custom_call_target="tpu_custom_call" | custom-call | tf_op jit(solution)/shard_map/pallas_call | solution.py:122
  16.8 3.2 %maximum_maximum_fusion = f32[38,134,256]{2,1,0:T(8,128)S(1)} fusion(f32[3,3,256]{2,1,0:T(4,128)} %get-tuple-element.44, f32[3,128,256]{2,1,0:T(8,128)} %get-tuple-element.43, f32[3,3,256]{2,1,0:T(4,128)} %get-tuple-element.42, f32[32,3,256]{2,1,0:T(4,128)} %get-tuple-element.41, f32[32,128,256]{2,1,0:T(8,128)} %refs_0_.1, ...), kind=kLoop, calls=%fused_computation.21 | loop fusion | flops 10428416 | bytes 10428416 | tf_op jit(solution)/shard_map/concatenate | solution.py:141
  20.0 0.7 copy-done
  20.6 0.0 copy-done.4
  20.7 0.5 pad_maximum_fusion
  21.2 0.0 copy-start.7
  21.2 2.5 %multiply_add_fusion.1 = (f32[16,134,256]{2,1,0:T(8,128)S(1)}, f32[16,134,256]{2,1,0:T(8,128)S(1)}) fusion(f32[38,134,256]{2,1,0:T(8,128)S(1)} %maximum_maximum_fusion, f32[32,134,256]{2,1,0:T(8,128)S(1)} %pad_maximum_fusion), kind=kLoop, calls=%fused_computation.38 | loop fusion | flops 16465920 | bytes 21954560 | tf_op jit(solution)/shard_map/add | solution.py:165
  23.7 0.0 copy-start.19
  23.7 0.0 copy-start.20
  23.7 0.0 copy-start.6
  23.8 3.8 %fusion.20 = f32[32,128,256]{2,1,0:T(8,128)S(1)} fusion(f32[16,134,256]{2,1,0:T(8,128)S(1)} %get-tuple-element.73, f32[16,134,256]{2,1,0:T(8,128)S(1)} %get-tuple-element.72, f32[134,128]{1,0:T(8,128)S(1)} %copy-done.7), kind=kOutput, calls=%fused_computation.24 | convolution fusion | flops 844152832 | bytes 8653824 | tf_op jit(solution)/shard_map/dot_general | solution.py:149
  27.6 0.2 select_reduce_fusion
  27.8 0.7 fusion.112
  28.5 4.4 %select_select_fusion.3 = (f32[32,128]{1,0:T(8,128)S(1)}, f32[32,128]{1,0:T(8,128)S(1)}) fusion(f32[]{:T(128)} %bitcast.5, f32[]{:T(128)} %bitcast.4, f32[]{:T(128)} %bitcast.3, f32[]{:T(128)} %bitcast.2, s32[128]{0:T(128)S(1)} %broadcast_select_fusion, s32[32]{0:T(128)S(1)} %compare_select_fusion.4, f32[]{:T(128)} %bitcast.8, f32[]{:T(128)} %bitcast.7, ...), kind=kLoop, calls=%fused_computation.148 | loop fusion | flops 65536 | bytes 33436 | tf_op jit(solution)/shard_map/jit(_where)/select_n | solution.py:213
  32.9 4.4 %maximum_multiply_fusion = (f32[32,128,256]{2,1,0:T(8,128)}, f32[32,128,256]{2,1,0:T(8,128)S(1)}) fusion(f32[32,128]{1,0:T(8,128)S(1)} %get-tuple-element.92, f32[32,128]{1,0:T(8,128)S(1)} %get-tuple-element.91, pred[256]{0:T(512)(128)(4,1)S(1)} %iota_compare_fusion.3, f32[32,128,256]{2,1,0:T(8,128)S(1)} %fusion.20, f32[256,256,1]{1,0,2:T(8,128)S(1)} %copy-done.6), kind=kOutput, calls=%fused_computation.29 | convolution fusion | flops 1616904192 | bytes 12878080 | tf_op jit(solution)/shard_map/dot_general | solution.py:149
  37.2 0.8 slice.420.refs_0_
  38.1 19.2 %shard_map.173 = (f32[9,64,128]{2,1,0:T(8,128)}, f32[9,64,128]{2,1,0:T(8,128)}, f32[16,11,128]{2,1,0:T(8,128)}, f32[16,11,128]{2,1,0:T(8,128)}, f32[9,11,128]{2,...) custom-call(f32[16,64,128]{2,1,0:T(8,128)} %slice.420.refs_0_, ...), custom_call_target="tpu_custom_call" | custom-call | tf_op jit(solution)/shard_map/pallas_call | solution.py:122
  57.2 1.4 %maximum_maximum_fusion.1 = f32[34,86,128]{2,1,0:T(8,128)S(1)} fusion(f32[9,11,128]{2,1,0:T(8,128)} %get-tuple-element.52, f32[9,64,128]{2,1,0:T(8,128)} %get-tuple-element.51, f32[9,11,128]{2,1,0:T(8,128)} %get-tuple-element.50, f32[16,11,128]{2,1,0:T(8,128)} %get-tuple-element.49, f32[16,64,128]{2,1,0:T(8,128)S(1)} %copy-done.2, ...), kind=kLoop, calls=%fused_computation.51 | loop fusion | flops 2994176 | bytes 2994176 | tf_op jit(solution)/shard_map/concatenate | solution.py:141
  58.7 0.0 copy-start.10
  58.7 0.7 multiply_add_fusion.3
  59.3 0.0 copy-start.9
  59.3 0.1 copy-done.10
  59.4 0.7 fusion.38
  60.1 0.1 copy-done.9
  60.2 0.6 fusion.113
  60.8 0.0 copy-start.18
  60.8 0.1 multiply_add_fusion.5
  60.9 0.0 copy-start.17
  61.0 0.2 fusion.85
  61.2 0.7 fusion.110
  61.9 4.5 %select_select_fusion.5 = (f32[8,32]{1,0:T(8,128)S(1)}, f32[8,32]{1,0:T(8,128)S(1)}) fusion(f32[]{:T(128)} %bitcast.16, f32[]{:T(128)} %bitcast.15, f32[]{:T(128)} %bitcast.14, f32[]{:T(128)} %bitcast.13, s32[32]{0:T(128)S(1)} %compare_select_fusion.3, s32[8]{0:T(128)S(1)} %compare_select_fusion.2, f32[]{:T(128)} %bitcast.19, f32[]{:T(128)} %bitcast.18, ...), kind=kLoop, calls=%fused_computation.160 | loop fusion | flops 4096 | bytes 2236 | tf_op jit(solution)/shard_map/jit(_where)/select_n | solution.py:213
  66.4 0.2 maximum_multiply_fusion.1
  66.6 0.8 dynamic_update_slice.3
  67.4 0.6 copy-done.5
  68.1 10.8 %shard_map.174 = (f32[2,4,2,16,64]{4,3,2,1,0:T(8,128)}, f32[2,4,2,16,64]{4,3,2,1,0:T(8,128)}, f32[2,4,2,4,64]{4,3,2,1,0:T(4,128)}, f32[2,4,2,4,64]{4,3,2,1,0:T(4...) custom-call(f32[2,4,2,16,64]{4,3,2,1,0:T(8,128)} %bitcast.112), custom_call_target="tpu_custom_call" | custom-call | tf_op jit(solution)/shard_map/pallas_call | solution.py:122
  78.9 1.6 %fusion.46 = f32[2,12,2,24,64]{4,3,2,1,0:T(8,128)S(1)} fusion(f32[64,64,1,1,1]{1,0,4,3,2:T(8,128)S(1)} %copy-done.30, f32[2,4,2,4,64]{4,3,2,1,0:T(4,128)} %get-tuple-element.60, f32[2,4,2,16,64]{4,3,2,1,0:T(8,128)} %get-tuple-element.59, f32[2,4,2,4,64]{4,3,2,1,0:T(4,128)} %get-tuple-element.58, f32[2,4,2,4,64]{4,3,2,1,0:T(4,128)} %get-tuple-element.57, ...), kind=kOutput, calls=%fused_computation.67 | convolution fusion | flops 28901376 | bytes 606208 | tf_op jit(solution)/shard_map/dot_general | solution.py:149
  80.5 0.6 fusion.74
  81.1 0.6 fusion.42
  81.7 0.2 fusion.84
  81.9 0.0 copy-start.8
  82.0 4.4 %select_select_fusion.1 = (f32[28,80]{1,0:T(8,128)S(1)}, f32[28,80]{1,0:T(8,128)S(1)}) fusion(f32[]{:T(128)} %bitcast.34, f32[]{:T(128)} %bitcast.33, f32[]{:T(128)} %bitcast.32, f32[]{:T(128)} %bitcast.31, s32[80]{0:T(128)S(1)} %compare_select_fusion, s32[28]{0:T(128)S(1)} %compare_select_fusion.1, f32[]{:T(128)} %bitcast.37, f32[]{:T(128)} %bitcast.36, ...), kind=kLoop, calls=%fused_computation.146 | loop fusion | flops 35840 | bytes 18380 | tf_op jit(solution)/shard_map/jit(_where)/select_n | solution.py:213
  86.5 0.0 copy-start.14
  86.5 0.7 multiply_select_fusion
  87.2 0.0 copy-start.15
  87.3 0.6 fusion.114
  87.9 1.0 fusion.64
  89.0 1.1 fusion.37
  90.0 0.0 copy-start.1
  90.0 0.4 fusion.73
  90.5 0.0 copy-start.29
  90.5 0.1 pad_maximum_fusion.2
  90.7 1.6 %copy-done.1 = f32[32,128,256]{2,1,0:T(8,128)S(1)} copy-done((f32[32,128,256]{2,1,0:T(8,128)S(1)}, f32[32,128,256]{2,1,0:T(8,128)}, u32[]{:S(2)}) %copy-start.1) | copy-done | bytes 4194328
  92.2 0.2 copy-done.21
  92.4 0.2 copy-done.22
  92.6 0.0 copy-done.23
  92.6 0.0 copy-done.24
  92.6 0.1 copy-done.29
  92.8 2.9 %fusion = f32[2,20,2,68,256]{4,3,2,1,0:T(8,128)S(1)} fusion(f32[256,256,1,1,1]{1,0,4,3,2:T(8,128)S(1)} %copy-done.29, f32[2,2,2,2,256]{4,3,2,1,0:T(2,128)S(1)} %copy-done.28, f32[2,2,2,64,256]{4,3,2,1,0:T(8,128)S(1)} %copy-done.22, f32[2,2,2,2,256]{4,3,2,1,0:T(2,128)S(1)} %copy-done.27, f32[2,16,2,2,256]{4,3,2,1,0:T(2,128)S(1)} %copy-done.24, ...), kind=kOutput, calls=%fused_computation.1 | convolution fusion | flops 2154414080 | bytes 12099842 | tf_op jit(solution)/shard_map/dot_general | solution.py:149
  95.7 0.0 copy-start.12
  95.7 4.9 %fusion.24 = f32[40,256,128]{2,1,0:T(8,128)S(1)} fusion(f32[40,2,68,256]{3,2,1,0:T(8,128)S(1)} %bitcast.105, f32[68,128]{1,0:T(8,128)S(1)} %copy-done.11), kind=kOutput, calls=%fused_computation.31 | convolution fusion | flops 534773760 | bytes 8228864 | tf_op jit(solution)/shard_map/dot_general | solution.py:149
  100.6 4.7 %add_bitcast_fusion = f32[40,128,256]{1,2,0:T(8,128)S(1)} fusion(f32[40,256,128]{2,1,0:T(8,128)S(1)} %fusion.24, f32[40,2,68,256]{3,2,1,0:T(8,128)S(1)} %bitcast.106, f32[68,128]{1,0:T(8,128)S(1)} %copy-done.12), kind=kOutput, calls=%fused_computation.22 | convolution fusion | flops 536084480 | bytes 13471744 | tf_op jit(solution)/shard_map/dot_general | solution.py:149
  105.3 2.5 %fusion.36 = (f32[16,1,128,256]{2,3,0,1:T(8,128)S(1)}, f32[16,1,128,256]{2,3,0,1:T(8,128)S(1)}) fusion(f32[40,128,256]{1,2,0:T(8,128)S(1)} %add_bitcast_fusion), kind=kLoop, calls=%fused_computation.49 | loop fusion | flops 15728640 | bytes 25165824 | tf_op jit(solution)/shard_map/stack | solution.py:184
  107.9 2.3 %pad_maximum_fusion.1 = f32[16,2,128,256]{2,3,0,1:T(8,128)} fusion(f32[16,1,128,256]{2,3,0,1:T(8,128)S(1)} %get-tuple-element.75, f32[16,1,128,256]{2,3,0,1:T(8,128)S(1)} %get-tuple-element.74), kind=kLoop, calls=%fused_computation.28 | loop fusion | flops 1048576 | bytes 8388608 | tf_op jit(solution)/shard_map/stack | solution.py:184
  110.1 5.3 %copy.38 = f32[16,2,128,256]{3,2,1,0:T(8,128)} copy(f32[16,2,128,256]{2,3,0,1:T(8,128)} %pad_maximum_fusion.1) | data formatting | bytes 8388608 | tf_op jit(solution)/shard_map/stack | solution.py:184
  (57 shorter events, 0.3 us)
Async XLA Ops:
  16.7 3.9 %copy-start = (f32[32,128,256]{2,1,0:T(8,128)S(1)}, f32[32,128,256]{2,1,0:T(8,128)}, u32[]{:S(2)}) copy-start(f32[32,128,256]{2,1,0:T(8,128)} %refs_0_.1) | copy-start | bytes 12582916
  16.7 3.9 %copy-start.3 = (f32[32,3,256]{2,1,0:T(4,128)S(1)}, f32[32,3,256]{2,1,0:T(4,128)}, u32[]{:S(2)}) copy-start(f32[32,3,256]{2,1,0:T(4,128)} %get-tuple-element.40) | copy-start | bytes 294916
  16.8 3.9 %copy-start.4 = (f32[32,3,256]{2,1,0:T(4,128)S(1)}, f32[32,3,256]{2,1,0:T(4,128)}, u32[]{:S(2)}) copy-start(f32[32,3,256]{2,1,0:T(4,128)} %get-tuple-element.41) | copy-start | bytes 294916
  21.2 2.5 %copy-start.7 = (f32[134,128]{1,0:T(8,128)S(1)}, f32[134,128]{1,0:T(8,128)}, u32[]{:S(2)}) copy-start(f32[134,128]{1,0:T(8,128)} %constant.66.clone) | copy-start | bytes 205828
  23.7 3.8 %copy-start.19 = (s32[3,7]{1,0:T(4,128)S(1)}, s32[3,7]{1,0:T(4,128)}, u32[]{:S(2)}) copy-start(s32[3,7]{1,0:T(4,128)} %param.20) | copy-start | bytes 256
  23.7 3.8 %copy-start.20 = (f32[16]{0:T(128)S(1)}, f32[16]{0:T(128)}, u32[]{:S(2)}) copy-start(f32[16]{0:T(128)} %param.19) | copy-start | bytes 196
  23.7 9.1 %copy-start.6 = (f32[256,256,1]{1,0,2:T(8,128)S(1)}, f32[256,256,1]{1,0,2:T(8,128)}, u32[]{:S(2)}) copy-start(f32[256,256,1]{1,0,2:T(8,128)} %constant.24) | copy-start | bytes 786436
  38.1 19.2 %copy-start.2 = (f32[16,64,128]{2,1,0:T(8,128)S(1)}, f32[16,64,128]{2,1,0:T(8,128)}, u32[]{:S(2)}) copy-start(f32[16,64,128]{2,1,0:T(8,128)} %slice.420.refs_0_) | copy-start | bytes 1572868
  58.7 0.8 copy-start.10
  59.3 0.8 copy-start.9
  60.2 0.8 copy-start.16
  60.2 6.2 %copy-start.13 = (f32[64,64,1]{1,0,2:T(8,128)S(1)}, f32[64,64,1]{1,0,2:T(8,128)}, u32[]{:S(2)}) copy-start(f32[64,64,1]{1,0,2:T(8,128)} %constant.26) | copy-start | bytes 49156
  60.2 18.7 %copy-start.30 = (f32[64,64,1,1,1]{1,0,4,3,2:T(8,128)S(1)}, f32[64,64,1,1,1]{1,0,4,3,2:T(8,128)}, u32[]{:S(2)}) copy-start(f32[64,64,1,1,1]{1,0,4,3,2:T(8,128)} %constant.27) | copy-start | bytes 49156
  60.8 19.7 %copy-start.18 = (f32[24,40]{1,0:T(8,128)S(1)}, f32[24,40]{1,0:T(8,128)}, u32[]{:S(2)}) copy-start(f32[24,40]{1,0:T(8,128)} %constant.72.clone) | copy-start | bytes 11524
  60.9 20.2 %copy-start.17 = (f32[24,40]{1,0:T(8,128)S(1)}, f32[24,40]{1,0:T(8,128)}, u32[]{:S(2)}) copy-start(f32[24,40]{1,0:T(8,128)} %constant.73.clone) | copy-start | bytes 11524
  67.4 0.7 copy-start.5
  81.9 5.3 %copy-start.8 = (f32[128,128,1,1]{1,0,3,2:T(8,128)S(1)}, f32[128,128,1,1]{1,0,3,2:T(8,128)}, u32[]{:S(2)}) copy-start(f32[128,128,1,1]{1,0,3,2:T(8,128)} %constant.28) | copy-start | bytes 196612
  86.5 1.4 %copy-start.14 = (f32[40,68]{1,0:T(8,128)S(1)}, f32[40,68]{1,0:T(8,128)}, u32[]{:S(2)}) copy-start(f32[40,68]{1,0:T(8,128)} %constant.74.clone) | copy-start | bytes 32644
  87.2 1.7 %copy-start.15 = (f32[40,68]{1,0:T(8,128)S(1)}, f32[40,68]{1,0:T(8,128)}, u32[]{:S(2)}) copy-start(f32[40,68]{1,0:T(8,128)} %constant.75.clone) | copy-start | bytes 32644
  90.0 2.2 %copy-start.1 = (f32[32,128,256]{2,1,0:T(8,128)S(1)}, f32[32,128,256]{2,1,0:T(8,128)}, u32[]{:S(2)}) copy-start(f32[32,128,256]{2,1,0:T(8,128)} %get-tuple-element.114) | copy-start | bytes 12582916
  90.4 2.0 %copy-start.21 = (f32[2,2,2,64,256]{4,3,2,1,0:T(8,128)S(1)}, f32[2,2,2,64,256]{4,3,2,1,0:T(8,128)}, u32[]{:S(2)}) copy-start(f32[2,2,2,64,256]{4,3,2,1,0:T(8,128)} %get-tuple-element.62) | copy-start | bytes 1572868
  90.4 2.1 %copy-start.22 = (f32[2,2,2,64,256]{4,3,2,1,0:T(8,128)S(1)}, f32[2,2,2,64,256]{4,3,2,1,0:T(8,128)}, u32[]{:S(2)}) copy-start(f32[2,2,2,64,256]{4,3,2,1,0:T(8,128)} %get-tuple-element.67) | copy-start | bytes 1572868
  90.4 2.1 %copy-start.23 = (f32[2,16,2,2,256]{4,3,2,1,0:T(2,128)S(1)}, f32[2,16,2,2,256]{4,3,2,1,0:T(2,128)}, u32[]{:S(2)}) copy-start(f32[2,16,2,2,256]{4,3,2,1,0:T(2,128)} %get-tuple-element.64) | copy-start | bytes 393220
  90.5 2.2 %copy-start.24 = (f32[2,16,2,2,256]{4,3,2,1,0:T(2,128)S(1)}, f32[2,16,2,2,256]{4,3,2,1,0:T(2,128)}, u32[]{:S(2)}) copy-start(f32[2,16,2,2,256]{4,3,2,1,0:T(2,128)} %get-tuple-element.65) | copy-start | bytes 393220
  90.5 2.2 %copy-start.25 = (f32[2,2,2,2,256]{4,3,2,1,0:T(2,128)S(1)}, f32[2,2,2,2,256]{4,3,2,1,0:T(2,128)}, u32[]{:S(2)}) copy-start(f32[2,2,2,2,256]{4,3,2,1,0:T(2,128)} %get-tuple-element.61) | copy-start | bytes 49156
  90.5 2.2 %copy-start.26 = (f32[2,2,2,2,256]{4,3,2,1,0:T(2,128)S(1)}, f32[2,2,2,2,256]{4,3,2,1,0:T(2,128)}, u32[]{:S(2)}) copy-start(f32[2,2,2,2,256]{4,3,2,1,0:T(2,128)} %get-tuple-element.63) | copy-start | bytes 49156
  90.5 2.2 %copy-start.27 = (f32[2,2,2,2,256]{4,3,2,1,0:T(2,128)S(1)}, f32[2,2,2,2,256]{4,3,2,1,0:T(2,128)}, u32[]{:S(2)}) copy-start(f32[2,2,2,2,256]{4,3,2,1,0:T(2,128)} %get-tuple-element.66) | copy-start | bytes 49156
  90.5 2.1 %copy-start.28 = (f32[2,2,2,2,256]{4,3,2,1,0:T(2,128)S(1)}, f32[2,2,2,2,256]{4,3,2,1,0:T(2,128)}, u32[]{:S(2)}) copy-start(f32[2,2,2,2,256]{4,3,2,1,0:T(2,128)} %get-tuple-element.68) | copy-start | bytes 49156
  90.5 2.3 %copy-start.29 = (f32[256,256,1,1,1]{1,0,4,3,2:T(8,128)S(1)}, f32[256,256,1,1,1]{1,0,4,3,2:T(8,128)}, u32[]{:S(2)}) copy-start(f32[256,256,1,1,1]{1,0,4,3,2:T(8,128)} %constant.29) | copy-start | bytes 786436
  92.8 2.9 %copy-start.11 = (f32[68,128]{1,0:T(8,128)S(1)}, f32[68,128]{1,0:T(8,128)}, u32[]{:S(2)}) copy-start(f32[68,128]{1,0:T(8,128)} %constant.77.clone) | copy-start | bytes 104452
  95.7 4.9 %copy-start.12 = (f32[68,128]{1,0:T(8,128)S(1)}, f32[68,128]{1,0:T(8,128)}, u32[]{:S(2)}) copy-start(f32[68,128]{1,0:T(8,128)} %constant.76.clone) | copy-start | bytes 104452

commit v11 on v9

--- a/solution.py
+++ b/solution.py
@@ -218,7 +218,12 @@
 
 def synthesis_ext(extended, trim=0):
     two, hx4, _, hy4, size_z = extended.shape
-    z_part = contract(extended, jnp.asarray(periodic_analysis(size_z)), ((4,), (1,)), ((), ()))
+    matrix_z = jnp.asarray(periodic_analysis(size_z))
+    if hy4 % 8 == 0:
+        flat = extended.reshape(4 * hx4 * hy4, size_z)
+        z_part = contract(flat, matrix_z, ((1,), (1,)), ((), ()))
+    else:
+        z_part = contract(extended, matrix_z, ((4,), (1,)), ((), ()))
     z_part = z_part.reshape(2 * hx4, 2, hy4, size_z)
     size_y = 2 * (hy4 - 4)
     matrix = split_synthesis(size_y)

time: 117 us -> 117 us (level)
  other arithmetic: 29 us -> 30.3 us
  matrix products: 27.3 us -> 26.1 us
    concatenate x3 -> x4, other arithmetic: 5.64 us -> 6.88 us  [assemble(): return jnp.concatenate([top, mid, bottom], axis=dx)]
    dot_general x15, matrix products: 27.3 us -> 26.1 us  [contract(): lax.dot_general(left, right, (dims, batch), precision=PREC, preferred_ele...]
where the time goes in v11:
time: 117 us; the launch traced here: 116 us
  Pallas kernels  46.7 us (40%)
  other arithmetic  30.3 us (26%)
  matrix products  26.1 us (22%)
  local copies, waits for them, and re-layouts  12.2 us (10%)
    pallas_call x3, Pallas kernels, halos(): pl.pallas_call(functools.partial(exchange_kernel, layouts, lax.axis_size(...  46.7 us
    dot_general x15, matrix products, contract(): lax.dot_general(left, right, (dims, batch), precision=PREC, preferred_ele...  26.1 us
    select_n x3, other arithmetic, shrink_field(): high_z = jnp.where(plane_ids + 1 == band_no, eight[band_no], high_z)  13.3 us
    concatenate x4, other arithmetic, assemble(): return jnp.concatenate([top, mid, bottom], axis=dx)  6.88 us
    another operation x3, local copies, waits for them, and re-layouts, synthesise_lead(): joined = jnp.stack([even, odd], axis=1)  5.42 us
    another operation x6, other arithmetic, synthesise_lead(): joined = jnp.stack([even, odd], axis=1)  5.38 us
    unnamed x62, local copies, waits for them, and re-layouts  3.67 us
    add x3, other arithmetic, analyse_lead(): low = low + filt_low[j] * taken  3.26 us

profile of v11, /device:TPU:8, one launch (start us, length us, event | category | flops | bytes accessed | tf_op | source)
XLA Modules:
  0.0 116.0 jit_solution(8903560511200875690)
XLA Ops:
  0.0 16.7 %shard_map.172 = (f32[3,128,256]{2,1,0:T(8,128)}, f32[3,128,256]{2,1,0:T(8,128)}, f32[32,3,256]{2,1,0:T(4,128)}, f32[32,3,256]{2,1,0:T(4,128)}, f32[3,3,256]{2,1...) custom-call(f32[32,128,256]{2,1,0:T(8,128)} %refs_0_.1), custom_call_target="tpu_custom_call" | custom-call | tf_op jit(solution)/shard_map/pallas_call | solution.py:122
  16.8 3.2 %maximum_maximum_fusion.1 = f32[38,134,256]{2,1,0:T(8,128)S(1)} fusion(f32[3,3,256]{2,1,0:T(4,128)} %get-tuple-element.56, f32[3,128,256]{2,1,0:T(8,128)} %get-tuple-element.55, f32[3,3,256]{2,1,0:T(4,128)} %get-tuple-element.54, f32[32,3,256]{2,1,0:T(4,128)} %get-tuple-element.53, f32[32,128,256]{2,1,0:T(8,128)} %refs_0_.1, ...), kind=kLoop, calls=%fused_computation.1 | loop fusion | flops 10428416 | bytes 10428416 | tf_op jit(solution)/shard_map/concatenate | solution.py:141
  20.0 0.7 copy-done
  20.6 0.0 copy-done.5
  20.7 0.5 pad_maximum_fusion
  21.2 0.0 copy-start.12
  21.2 2.5 %multiply_add_fusion.1 = (f32[16,134,256]{2,1,0:T(8,128)S(1)}, f32[16,134,256]{2,1,0:T(8,128)S(1)}) fusion(f32[38,134,256]{2,1,0:T(8,128)S(1)} %maximum_maximum_fusion.1, f32[32,134,256]{2,1,0:T(8,128)S(1)} %pad_maximum_fusion), kind=kLoop, calls=%fused_computation.15 | loop fusion | flops 16465920 | bytes 21954560 | tf_op jit(solution)/shard_map/add | solution.py:165
  23.7 0.0 copy-start.9
  23.8 3.8 %fusion = f32[32,128,256]{2,1,0:T(8,128)S(1)} fusion(f32[16,134,256]{2,1,0:T(8,128)S(1)} %get-tuple-element.85, f32[16,134,256]{2,1,0:T(8,128)S(1)} %get-tuple-element.84, f32[134,128]{1,0:T(8,128)S(1)} %copy-done.12), kind=kOutput, calls=%fused_computation.4 | convolution fusion | flops 844152832 | bytes 8653824 | tf_op jit(solution)/shard_map/dot_general | solution.py:149
  27.6 0.2 select_reduce_fusion
  27.8 0.7 fusion.68
  28.5 4.4 %select_select_fusion.3 = (f32[32,128]{1,0:T(8,128)S(1)}, f32[32,128]{1,0:T(8,128)S(1)}) fusion(f32[]{:T(128)} %bitcast.5, f32[]{:T(128)} %bitcast.4, f32[]{:T(128)} %bitcast.3, f32[]{:T(128)} %bitcast.2, s32[128]{0:T(128)S(1)} %broadcast_select_fusion, s32[32]{0:T(128)S(1)} %compare_select_fusion.4, f32[]{:T(128)} %bitcast.8, f32[]{:T(128)} %bitcast.7, ...), kind=kLoop, calls=%fused_computation.108 | loop fusion | flops 65536 | bytes 33436 | tf_op jit(solution)/shard_map/jit(_where)/select_n | solution.py:213
  32.9 4.4 %maximum_multiply_fusion = (f32[32,128,256]{2,1,0:T(8,128)}, f32[32,128,256]{2,1,0:T(8,128)S(1)}) fusion(f32[32,128]{1,0:T(8,128)S(1)} %get-tuple-element.104, f32[32,128]{1,0:T(8,128)S(1)} %get-tuple-element.103, pred[256]{0:T(512)(128)(4,1)S(1)} %iota_compare_fusion.3, f32[32,128,256]{2,1,0:T(8,128)S(1)} %fusion, f32[256,256,1]{1,0,2:T(8,128)S(1)} %copy-done.9), kind=kOutput, calls=%fused_computation.9 | convolution fusion | flops 1616904192 | bytes 12878080 | tf_op jit(solution)/shard_map/dot_general | solution.py:149
  37.2 0.8 slice.454.refs_0_
  38.1 19.2 %shard_map.173 = (f32[9,64,128]{2,1,0:T(8,128)}, f32[9,64,128]{2,1,0:T(8,128)}, f32[16,11,128]{2,1,0:T(8,128)}, f32[16,11,128]{2,1,0:T(8,128)}, f32[9,11,128]{2,...) custom-call(f32[16,64,128]{2,1,0:T(8,128)} %slice.454.refs_0_, ...), custom_call_target="tpu_custom_call" | custom-call | tf_op jit(solution)/shard_map/pallas_call | solution.py:122
  57.2 1.4 %maximum_maximum_fusion.2 = f32[34,86,128]{2,1,0:T(8,128)S(1)} fusion(f32[9,11,128]{2,1,0:T(8,128)} %get-tuple-element.72, f32[9,64,128]{2,1,0:T(8,128)} %get-tuple-element.71, f32[9,11,128]{2,1,0:T(8,128)} %get-tuple-element.70, f32[16,11,128]{2,1,0:T(8,128)} %get-tuple-element.69, f32[16,64,128]{2,1,0:T(8,128)S(1)} %copy-done.2, ...), kind=kLoop, calls=%fused_computation.28 | loop fusion | flops 2994176 | bytes 2994176 | tf_op jit(solution)/shard_map/concatenate | solution.py:141
  58.7 0.0 copy-start.15
  58.7 0.7 multiply_add_fusion.3
  59.3 0.0 copy-start.14
  59.3 0.1 copy-done.15
  59.4 0.7 fusion.15
  60.1 0.1 copy-done.14
  60.2 0.6 fusion.69
  60.8 0.0 copy-start.28
  60.9 0.1 multiply_add_fusion.5
  61.0 0.0 copy-start.27
  61.0 0.2 fusion.44
  61.2 0.7 fusion.66
  61.9 4.5 %select_select_fusion.5 = (f32[8,32]{1,0:T(8,128)S(1)}, f32[8,32]{1,0:T(8,128)S(1)}) fusion(f32[]{:T(128)} %bitcast.16, f32[]{:T(128)} %bitcast.15, f32[]{:T(128)} %bitcast.14, f32[]{:T(128)} %bitcast.13, s32[32]{0:T(128)S(1)} %compare_select_fusion.3, s32[8]{0:T(128)S(1)} %compare_select_fusion.2, f32[]{:T(128)} %bitcast.19, f32[]{:T(128)} %bitcast.18, ...), kind=kLoop, calls=%fused_computation.120 | loop fusion | flops 4096 | bytes 2236 | tf_op jit(solution)/shard_map/jit(_where)/select_n | solution.py:213
  66.4 0.2 maximum_multiply_fusion.1
  66.6 0.8 dynamic_update_slice.3
  67.4 0.6 copy-done.3
  68.1 10.8 %shard_map.174 = (f32[2,4,2,16,64]{4,3,2,1,0:T(8,128)}, f32[2,4,2,16,64]{4,3,2,1,0:T(8,128)}, f32[2,4,2,4,64]{4,3,2,1,0:T(4,128)}, f32[2,4,2,4,64]{4,3,2,1,0:T(4...) custom-call(f32[2,4,2,16,64]{4,3,2,1,0:T(8,128)} %bitcast.108), custom_call_target="tpu_custom_call" | custom-call | tf_op jit(solution)/shard_map/pallas_call | solution.py:122
  78.9 1.2 %maximum_maximum_fusion.3 = f32[2,12,2,24,64]{4,3,2,1,0:T(8,128)S(1)} fusion(f32[2,4,2,4,64]{4,3,2,1,0:T(4,128)} %get-tuple-element.80, f32[2,4,2,16,64]{4,3,2,1,0:T(8,128)} %get-tuple-element.79, f32[2,4,2,4,64]{4,3,2,1,0:T(4,128)} %get-tuple-element.78, f32[2,4,2,4,64]{4,3,2,1,0:T(4,128)} %get-tuple-element.77, f32[2,4,2,16,64]{4,3,2,1,0:T(8,128)} %bitcast.109, ...), kind=kLoop, calls=%fused_computation.44 | loop fusion | flops 589824 | bytes 589824 | tf_op jit(solution)/shard_map/concatenate | solution.py:141
  80.2 0.4 fusion.70
  80.6 0.6 fusion.33
  81.2 0.6 fusion.19
  81.8 0.2 fusion.43
  82.0 0.0 copy-start.13
  82.1 4.4 %select_select_fusion.1 = (f32[28,80]{1,0:T(8,128)S(1)}, f32[28,80]{1,0:T(8,128)S(1)}) fusion(f32[]{:T(128)} %bitcast.34, f32[]{:T(128)} %bitcast.33, f32[]{:T(128)} %bitcast.32, f32[]{:T(128)} %bitcast.31, s32[80]{0:T(128)S(1)} %compare_select_fusion, s32[28]{0:T(128)S(1)} %compare_select_fusion.1, f32[]{:T(128)} %bitcast.37, f32[]{:T(128)} %bitcast.36, ...), kind=kLoop, calls=%fused_computation.106 | loop fusion | flops 35840 | bytes 18380 | tf_op jit(solution)/shard_map/jit(_where)/select_n | solution.py:213
  86.6 0.0 copy-start.20
  86.6 0.7 multiply_select_fusion
  87.3 0.0 copy-start.21
  87.3 0.6 fusion.71
  88.0 1.0 fusion.23
  89.0 1.1 fusion.14
  90.1 0.4 fusion.32
  90.6 0.1 pad_maximum_fusion.2
  90.7 1.6 %copy-done.1 = f32[32,128,256]{2,1,0:T(8,128)S(1)} copy-done((f32[32,128,256]{2,1,0:T(8,128)S(1)}, f32[32,128,256]{2,1,0:T(8,128)}, u32[]{:S(2)}) %copy-start.1) | copy-done | bytes 4194328
  92.3 0.2 copy-done.6
  92.5 0.2 copy-done.7
  92.6 0.0 copy-done.10
  92.7 0.0 copy-done.11
  92.7 0.0 copy-start.8
  92.7 1.1 maximum_maximum_fusion
  93.8 0.1 constant_dynamic-update-slice_fusion
  93.9 0.0 copy-start.16
  93.9 2.6 %fusion.72 = f32[2,20,2,68,256]{4,3,2,1,0:T(8,128)S(1)} fusion(f32[2,20,2,68,256]{4,3,2,1,0:T(8,128)S(1)} %constant_dynamic-update-slice_fusion, f32[256,256,1,1,1]{1,0,4,3,2:T(8,128)S(1)} %copy-done.8), kind=kOutput, calls=%fused_computation.150 | convolution fusion | flops 2139095040 | bytes 11403264 | tf_op jit(solution)/shard_map/dot_general | solution.py:149
  96.5 0.0 copy-start.17
  96.5 4.7 %fusion.4 = f32[40,256,128]{2,1,0:T(8,128)S(1)} fusion(f32[40,2,68,256]{3,2,1,0:T(8,128)S(1)} %bitcast.103, f32[68,128]{1,0:T(8,128)S(1)} %copy-done.16), kind=kOutput, calls=%fused_computation.11 | convolution fusion | flops 534773760 | bytes 8228864 | tf_op jit(solution)/shard_map/dot_general | solution.py:149
  101.2 4.7 %add_bitcast_fusion = f32[40,128,256]{1,2,0:T(8,128)S(1)} fusion(f32[40,256,128]{2,1,0:T(8,128)S(1)} %fusion.4, f32[40,2,68,256]{3,2,1,0:T(8,128)S(1)} %bitcast.104, f32[68,128]{1,0:T(8,128)S(1)} %copy-done.17), kind=kOutput, calls=%fused_computation.2 | convolution fusion | flops 536084480 | bytes 13471744 | tf_op jit(solution)/shard_map/dot_general | solution.py:149
  105.9 2.3 %fusion.13 = (f32[16,1,128,256]{2,3,0,1:T(8,128)S(1)}, f32[16,1,128,256]{2,3,0,1:T(8,128)S(1)}) fusion(f32[40,128,256]{1,2,0:T(8,128)S(1)} %add_bitcast_fusion), kind=kLoop, calls=%fused_computation.26 | loop fusion | flops 15728640 | bytes 25165824 | tf_op jit(solution)/shard_map/stack | solution.py:184
  108.3 2.4 %pad_maximum_fusion.1 = f32[16,2,128,256]{2,3,0,1:T(8,128)} fusion(f32[16,1,128,256]{2,3,0,1:T(8,128)S(1)} %get-tuple-element.87, f32[16,1,128,256]{2,3,0,1:T(8,128)S(1)} %get-tuple-element.86), kind=kLoop, calls=%fused_computation.8 | loop fusion | flops 1048576 | bytes 8388608 | tf_op jit(solution)/shard_map/stack | solution.py:184
  110.7 5.3 %copy.32 = f32[16,2,128,256]{3,2,1,0:T(8,128)} copy(f32[16,2,128,256]{2,3,0,1:T(8,128)} %pad_maximum_fusion.1) | data formatting | bytes 8388608 | tf_op jit(solution)/shard_map/stack | solution.py:184
  (58 shorter events, 0.3 us)
Async XLA Ops:
  16.7 3.9 %copy-start = (f32[32,128,256]{2,1,0:T(8,128)S(1)}, f32[32,128,256]{2,1,0:T(8,128)}, u32[]{:S(2)}) copy-start(f32[32,128,256]{2,1,0:T(8,128)} %refs_0_.1) | copy-start | bytes 12582916
  16.7 3.9 %copy-start.4 = (f32[32,3,256]{2,1,0:T(4,128)S(1)}, f32[32,3,256]{2,1,0:T(4,128)}, u32[]{:S(2)}) copy-start(f32[32,3,256]{2,1,0:T(4,128)} %get-tuple-element.52) | copy-start | bytes 294916
  16.8 3.9 %copy-start.5 = (f32[32,3,256]{2,1,0:T(4,128)S(1)}, f32[32,3,256]{2,1,0:T(4,128)}, u32[]{:S(2)}) copy-start(f32[32,3,256]{2,1,0:T(4,128)} %get-tuple-element.53) | copy-start | bytes 294916
  21.2 2.5 %copy-start.12 = (f32[134,128]{1,0:T(8,128)S(1)}, f32[134,128]{1,0:T(8,128)}, u32[]{:S(2)}) copy-start(f32[134,128]{1,0:T(8,128)} %constant.75.clone) | copy-start | bytes 205828
  23.7 3.8 %copy-start.29 = (s32[3,7]{1,0:T(4,128)S(1)}, s32[3,7]{1,0:T(4,128)}, u32[]{:S(2)}) copy-start(s32[3,7]{1,0:T(4,128)} %param.22) | copy-start | bytes 256
  23.7 3.8 %copy-start.30 = (f32[16]{0:T(128)S(1)}, f32[16]{0:T(128)}, u32[]{:S(2)}) copy-start(f32[16]{0:T(128)} %param.21) | copy-start | bytes 196
  23.7 9.1 %copy-start.9 = (f32[256,256,1]{1,0,2:T(8,128)S(1)}, f32[256,256,1]{1,0,2:T(8,128)}, u32[]{:S(2)}) copy-start(f32[256,256,1]{1,0,2:T(8,128)} %constant.90) | copy-start | bytes 786436
  38.1 19.2 %copy-start.2 = (f32[16,64,128]{2,1,0:T(8,128)S(1)}, f32[16,64,128]{2,1,0:T(8,128)}, u32[]{:S(2)}) copy-start(f32[16,64,128]{2,1,0:T(8,128)} %slice.454.refs_0_) | copy-start | bytes 1572868
  58.7 0.8 copy-start.15
  59.3 0.8 copy-start.14
  60.2 0.8 copy-start.26
  60.2 6.2 %copy-start.19 = (f32[64,64,1]{1,0,2:T(8,128)S(1)}, f32[64,64,1]{1,0,2:T(8,128)}, u32[]{:S(2)}) copy-start(f32[64,64,1]{1,0,2:T(8,128)} %constant.92) | copy-start | bytes 49156
  60.8 19.3 %copy-start.18 = (f32[64,64,1,1]{1,0,3,2:T(8,128)S(1)}, f32[64,64,1,1]{1,0,3,2:T(8,128)}, u32[]{:S(2)}) copy-start(f32[64,64,1,1]{1,0,3,2:T(8,128)} %constant.93) | copy-start | bytes 49156
  60.8 19.7 %copy-start.28 = (f32[24,40]{1,0:T(8,128)S(1)}, f32[24,40]{1,0:T(8,128)}, u32[]{:S(2)}) copy-start(f32[24,40]{1,0:T(8,128)} %constant.81.clone) | copy-start | bytes 11524
  61.0 20.2 %copy-start.27 = (f32[24,40]{1,0:T(8,128)S(1)}, f32[24,40]{1,0:T(8,128)}, u32[]{:S(2)}) copy-start(f32[24,40]{1,0:T(8,128)} %constant.82.clone) | copy-start | bytes 11524
  67.4 0.7 copy-start.3
  82.0 5.3 %copy-start.13 = (f32[128,128,1,1]{1,0,3,2:T(8,128)S(1)}, f32[128,128,1,1]{1,0,3,2:T(8,128)}, u32[]{:S(2)}) copy-start(f32[128,128,1,1]{1,0,3,2:T(8,128)} %constant.94) | copy-start | bytes 196612
  86.6 1.4 %copy-start.20 = (f32[40,68]{1,0:T(8,128)S(1)}, f32[40,68]{1,0:T(8,128)}, u32[]{:S(2)}) copy-start(f32[40,68]{1,0:T(8,128)} %constant.83.clone) | copy-start | bytes 32644
  87.3 1.7 %copy-start.21 = (f32[40,68]{1,0:T(8,128)S(1)}, f32[40,68]{1,0:T(8,128)}, u32[]{:S(2)}) copy-start(f32[40,68]{1,0:T(8,128)} %constant.84.clone) | copy-start | bytes 32644
  90.1 2.2 %copy-start.1 = (f32[32,128,256]{2,1,0:T(8,128)S(1)}, f32[32,128,256]{2,1,0:T(8,128)}, u32[]{:S(2)}) copy-start(f32[32,128,256]{2,1,0:T(8,128)} %get-tuple-element.126) | copy-start | bytes 12582916
  90.5 2.0 %copy-start.6 = (f32[2,2,2,64,256]{4,3,2,1,0:T(8,128)S(1)}, f32[2,2,2,64,256]{4,3,2,1,0:T(8,128)}, u32[]{:S(2)}) copy-start(f32[2,2,2,64,256]{4,3,2,1,0:T(8,128)} %get-tuple-element.58) | copy-start | bytes 1572868
  90.5 2.1 %copy-start.7 = (f32[2,2,2,64,256]{4,3,2,1,0:T(8,128)S(1)}, f32[2,2,2,64,256]{4,3,2,1,0:T(8,128)}, u32[]{:S(2)}) copy-start(f32[2,2,2,64,256]{4,3,2,1,0:T(8,128)} %get-tuple-element.63) | copy-start | bytes 1572868
  90.5 2.1 %copy-start.10 = (f32[2,16,2,2,256]{4,3,2,1,0:T(2,128)S(1)}, f32[2,16,2,2,256]{4,3,2,1,0:T(2,128)}, u32[]{:S(2)}) copy-start(f32[2,16,2,2,256]{4,3,2,1,0:T(2,128)} %get-tuple-element.60) | copy-start | bytes 393220
  90.5 2.2 %copy-start.11 = (f32[2,16,2,2,256]{4,3,2,1,0:T(2,128)S(1)}, f32[2,16,2,2,256]{4,3,2,1,0:T(2,128)}, u32[]{:S(2)}) copy-start(f32[2,16,2,2,256]{4,3,2,1,0:T(2,128)} %get-tuple-element.61) | copy-start | bytes 393220
  90.5 2.2 %copy-start.22 = (f32[2,2,2,2,256]{4,3,2,1,0:T(2,128)S(1)}, f32[2,2,2,2,256]{4,3,2,1,0:T(2,128)}, u32[]{:S(2)}) copy-start(f32[2,2,2,2,256]{4,3,2,1,0:T(2,128)} %get-tuple-element.57) | copy-start | bytes 49156
  90.5 2.2 %copy-start.23 = (f32[2,2,2,2,256]{4,3,2,1,0:T(2,128)S(1)}, f32[2,2,2,2,256]{4,3,2,1,0:T(2,128)}, u32[]{:S(2)}) copy-start(f32[2,2,2,2,256]{4,3,2,1,0:T(2,128)} %get-tuple-element.59) | copy-start | bytes 49156
  90.5 2.2 %copy-start.24 = (f32[2,2,2,2,256]{4,3,2,1,0:T(2,128)S(1)}, f32[2,2,2,2,256]{4,3,2,1,0:T(2,128)}, u32[]{:S(2)}) copy-start(f32[2,2,2,2,256]{4,3,2,1,0:T(2,128)} %get-tuple-element.62) | copy-start | bytes 49156
  90.6 2.1 %copy-start.25 = (f32[2,2,2,2,256]{4,3,2,1,0:T(2,128)S(1)}, f32[2,2,2,2,256]{4,3,2,1,0:T(2,128)}, u32[]{:S(2)}) copy-start(f32[2,2,2,2,256]{4,3,2,1,0:T(2,128)} %get-tuple-element.64) | copy-start | bytes 49156
  92.7 1.2 %copy-start.8 = (f32[256,256,1,1,1]{1,0,4,3,2:T(8,128)S(1)}, f32[256,256,1,1,1]{1,0,4,3,2:T(8,128)}, u32[]{:S(2)}) copy-start(f32[256,256,1,1,1]{1,0,4,3,2:T(8,128)} %constant.95) | copy-start | bytes 786436
  93.9 2.6 %copy-start.16 = (f32[68,128]{1,0:T(8,128)S(1)}, f32[68,128]{1,0:T(8,128)}, u32[]{:S(2)}) copy-start(f32[68,128]{1,0:T(8,128)} %constant.86.clone) | copy-start | bytes 104452
  96.5 4.7 %copy-start.17 = (f32[68,128]{1,0:T(8,128)S(1)}, f32[68,128]{1,0:T(8,128)}, u32[]{:S(2)}) copy-start(f32[68,128]{1,0:T(8,128)} %constant.85.clone) | copy-start | bytes 104452

commit v12 on v11

--- a/solution.py
+++ b/solution.py
@@ -248,7 +248,7 @@
     EXCHANGE_IDS[0] = 0
     cube0 = analysis_ext(halo(velocity, 0, 3, 1, 3))
     shrunk0 = blocked(shrink_field(cube0, threshold_table, band_index[0]))
-    ext1, ext0 = halos([(low_corner(cube0), 0, 9, 1, 11), (shrunk0, 1, 2, 3, 2)])
+    ext1, ext0 = halos([(low_corner(cube0), 0, 9, 1, 11), (shrunk0, 1, 2, 3, 4)])
     cube1 = analysis_ext(ext1)
     approx2 = low_corner(cube1)
     cube2 = analysis_ext(approx2[:, 1 : approx2.shape[1] - 1])
@@ -264,9 +264,9 @@
         & (lax.broadcasted_iota(jnp.int32, size1, 1) < size1[1] // 2)
         & (lax.broadcasted_iota(jnp.int32, size1, 2) < size1[2] // 2)
     )
-    recon1 = synthesis_ext(blocked(jnp.where(in_band0, padded2, shrunk1)), trim=2)
+    recon1 = synthesis_ext(blocked(jnp.where(in_band0, padded2, shrunk1)))
     half_z = ext0.shape[4] // 2
-    return synthesis_ext(ext0.at[0, :, 0, :, :half_z].set(recon1))
+    return synthesis_ext(ext0.at[0, :, 0, :, :half_z].set(recon1), trim=4)
 
 
 def solution(mesh):

time: 117 us -> 117 us (level)
  no operation moved by 1% of the time
where the time goes in v12:
time: 117 us; the launch traced here: 116 us
  Pallas kernels  47.1 us (40%)
  other arithmetic  30.1 us (26%)
  matrix products  26.1 us (22%)
  local copies, waits for them, and re-layouts  12.3 us (11%)
    pallas_call x3, Pallas kernels, halos(): pl.pallas_call(functools.partial(exchange_kernel, layouts, lax.axis_size(...  47.1 us
    dot_general x15, matrix products, contract(): lax.dot_general(left, right, (dims, batch), precision=PREC, preferred_ele...  26.1 us
    select_n x3, other arithmetic, shrink_field(): high_z = jnp.where(plane_ids + 1 == band_no, eight[band_no], high_z)  13.1 us
    concatenate x4, other arithmetic, assemble(): return jnp.concatenate([top, mid, bottom], axis=dx)  6.94 us
    another operation x3, local copies, waits for them, and re-layouts, synthesise_lead(): joined = jnp.stack([even, odd], axis=1)  5.42 us
    another operation x6, other arithmetic, synthesise_lead(): joined = jnp.stack([even, odd], axis=1)  5.26 us
    unnamed x62, local copies, waits for them, and re-layouts  3.76 us
    add x3, other arithmetic, analyse_lead(): low = low + filt_low[j] * taken  3.26 us

profile of v12, /device:TPU:8, one launch (start us, length us, event | category | flops | bytes accessed | tf_op | source)
XLA Modules:
  0.0 116.2 jit_solution(10608928636288081484)
XLA Ops:
  0.0 16.7 %shard_map.172 = (f32[3,128,256]{2,1,0:T(8,128)}, f32[3,128,256]{2,1,0:T(8,128)}, f32[32,3,256]{2,1,0:T(4,128)}, f32[32,3,256]{2,1,0:T(4,128)}, f32[3,3,256]{2,1...) custom-call(f32[32,128,256]{2,1,0:T(8,128)} %refs_0_.1), custom_call_target="tpu_custom_call" | custom-call | tf_op jit(solution)/shard_map/pallas_call | solution.py:122
  16.8 3.2 %maximum_maximum_fusion.1 = f32[38,134,256]{2,1,0:T(8,128)S(1)} fusion(f32[3,3,256]{2,1,0:T(4,128)} %get-tuple-element.56, f32[3,128,256]{2,1,0:T(8,128)} %get-tuple-element.55, f32[3,3,256]{2,1,0:T(4,128)} %get-tuple-element.54, f32[32,3,256]{2,1,0:T(4,128)} %get-tuple-element.53, f32[32,128,256]{2,1,0:T(8,128)} %refs_0_.1, ...), kind=kLoop, calls=%fused_computation.1 | loop fusion | flops 10428416 | bytes 10428416 | tf_op jit(solution)/shard_map/concatenate | solution.py:141
  20.0 0.7 copy-done.1
  20.6 0.0 copy-done.5
  20.7 0.5 pad_maximum_fusion
  21.2 0.0 copy-start.12
  21.2 2.5 %multiply_add_fusion.1 = (f32[16,134,256]{2,1,0:T(8,128)S(1)}, f32[16,134,256]{2,1,0:T(8,128)S(1)}) fusion(f32[38,134,256]{2,1,0:T(8,128)S(1)} %maximum_maximum_fusion.1, f32[32,134,256]{2,1,0:T(8,128)S(1)} %pad_maximum_fusion), kind=kLoop, calls=%fused_computation.15 | loop fusion | flops 16465920 | bytes 21954560 | tf_op jit(solution)/shard_map/add | solution.py:165
  23.7 0.0 copy-start.11
  23.8 3.8 %fusion = f32[32,128,256]{2,1,0:T(8,128)S(1)} fusion(f32[16,134,256]{2,1,0:T(8,128)S(1)} %get-tuple-element.85, f32[16,134,256]{2,1,0:T(8,128)S(1)} %get-tuple-element.84, f32[134,128]{1,0:T(8,128)S(1)} %copy-done.12), kind=kOutput, calls=%fused_computation.4 | convolution fusion | flops 844152832 | bytes 8653824 | tf_op jit(solution)/shard_map/dot_general | solution.py:149
  27.6 0.2 select_reduce_fusion
  27.8 0.7 fusion.68
  28.5 4.4 %select_select_fusion.3 = (f32[32,128]{1,0:T(8,128)S(1)}, f32[32,128]{1,0:T(8,128)S(1)}) fusion(f32[]{:T(128)} %bitcast.5, f32[]{:T(128)} %bitcast.4, f32[]{:T(128)} %bitcast.3, f32[]{:T(128)} %bitcast.2, s32[128]{0:T(128)S(1)} %broadcast_select_fusion, s32[32]{0:T(128)S(1)} %compare_select_fusion.4, f32[]{:T(128)} %bitcast.8, f32[]{:T(128)} %bitcast.7, ...), kind=kLoop, calls=%fused_computation.108 | loop fusion | flops 65536 | bytes 33436 | tf_op jit(solution)/shard_map/jit(_where)/select_n | solution.py:213
  32.9 4.4 %maximum_multiply_fusion = (f32[32,128,256]{2,1,0:T(8,128)}, f32[32,128,256]{2,1,0:T(8,128)S(1)}) fusion(f32[32,128]{1,0:T(8,128)S(1)} %get-tuple-element.104, f32[32,128]{1,0:T(8,128)S(1)} %get-tuple-element.103, pred[256]{0:T(512)(128)(4,1)S(1)} %iota_compare_fusion.3, f32[32,128,256]{2,1,0:T(8,128)S(1)} %fusion, f32[256,256,1]{1,0,2:T(8,128)S(1)} %copy-done.11), kind=kOutput, calls=%fused_computation.9 | convolution fusion | flops 1616904192 | bytes 12878080 | tf_op jit(solution)/shard_map/dot_general | solution.py:149
  37.2 0.8 slice.454.refs_0_
  38.1 19.3 %shard_map.173 = (f32[9,64,128]{2,1,0:T(8,128)}, f32[9,64,128]{2,1,0:T(8,128)}, f32[16,11,128]{2,1,0:T(8,128)}, f32[16,11,128]{2,1,0:T(8,128)}, f32[9,11,128]{2,...) custom-call(f32[16,64,128]{2,1,0:T(8,128)} %slice.454.refs_0_, ...), custom_call_target="tpu_custom_call" | custom-call | tf_op jit(solution)/shard_map/pallas_call | solution.py:122
  57.4 1.4 %maximum_maximum_fusion.2 = f32[34,86,128]{2,1,0:T(8,128)S(1)} fusion(f32[9,11,128]{2,1,0:T(8,128)} %get-tuple-element.72, f32[9,64,128]{2,1,0:T(8,128)} %get-tuple-element.71, f32[9,11,128]{2,1,0:T(8,128)} %get-tuple-element.70, f32[16,11,128]{2,1,0:T(8,128)} %get-tuple-element.69, f32[16,64,128]{2,1,0:T(8,128)S(1)} %copy-done.2, ...), kind=kLoop, calls=%fused_computation.28 | loop fusion | flops 2994176 | bytes 2994176 | tf_op jit(solution)/shard_map/concatenate | solution.py:141
  58.8 0.0 copy-start.15
  58.8 0.7 multiply_add_fusion.3
  59.5 0.0 copy-start.14
  59.5 0.1 copy-done.15
  59.6 0.7 fusion.15
  60.3 0.1 copy-done.14
  60.4 0.6 fusion.69
  61.0 0.0 copy-start.22
  61.0 0.0 copy-start.28
  61.0 0.1 multiply_add_fusion.5
  61.1 0.0 copy-start.27
  61.2 0.2 fusion.44
  61.4 0.7 fusion.66
  62.1 4.4 %select_select_fusion.5 = (f32[8,32]{1,0:T(8,128)S(1)}, f32[8,32]{1,0:T(8,128)S(1)}) fusion(f32[]{:T(128)} %bitcast.16, f32[]{:T(128)} %bitcast.15, f32[]{:T(128)} %bitcast.14, f32[]{:T(128)} %bitcast.13, s32[32]{0:T(128)S(1)} %compare_select_fusion.3, s32[8]{0:T(128)S(1)} %compare_select_fusion.2, f32[]{:T(128)} %bitcast.19, f32[]{:T(128)} %bitcast.18, ...), kind=kLoop, calls=%fused_computation.120 | loop fusion | flops 4096 | bytes 2236 | tf_op jit(solution)/shard_map/jit(_where)/select_n | solution.py:213
  66.5 0.2 maximum_multiply_fusion.1
  66.8 0.8 dynamic_update_slice.3
  67.6 0.6 copy-done.3
  68.2 11.0 %shard_map.174 = (f32[2,4,2,16,64]{4,3,2,1,0:T(8,128)}, f32[2,4,2,16,64]{4,3,2,1,0:T(8,128)}, f32[2,4,2,4,64]{4,3,2,1,0:T(4,128)}, f32[2,4,2,4,64]{4,3,2,1,0:T(4...) custom-call(f32[2,4,2,16,64]{4,3,2,1,0:T(8,128)} %bitcast.103), custom_call_target="tpu_custom_call" | custom-call | tf_op jit(solution)/shard_map/pallas_call | solution.py:122
  79.2 1.2 %maximum_maximum_fusion.3 = f32[2,12,2,24,64]{4,3,2,1,0:T(8,128)S(1)} fusion(f32[2,4,2,4,64]{4,3,2,1,0:T(4,128)} %get-tuple-element.80, f32[2,4,2,16,64]{4,3,2,1,0:T(8,128)} %get-tuple-element.79, f32[2,4,2,4,64]{4,3,2,1,0:T(4,128)} %get-tuple-element.78, f32[2,4,2,4,64]{4,3,2,1,0:T(4,128)} %get-tuple-element.77, f32[2,4,2,16,64]{4,3,2,1,0:T(8,128)} %bitcast.104, ...), kind=kLoop, calls=%fused_computation.44 | loop fusion | flops 589824 | bytes 589824 | tf_op jit(solution)/shard_map/concatenate | solution.py:141
  80.5 0.4 fusion.70
  80.9 0.6 fusion.33
  81.5 0.6 fusion.19
  82.1 0.2 fusion.43
  82.3 0.0 copy-start.13
  82.4 4.3 %select_select_fusion.1 = (f32[28,80]{1,0:T(8,128)S(1)}, f32[28,80]{1,0:T(8,128)S(1)}) fusion(f32[]{:T(128)} %bitcast.34, f32[]{:T(128)} %bitcast.33, f32[]{:T(128)} %bitcast.32, f32[]{:T(128)} %bitcast.31, s32[80]{0:T(128)S(1)} %compare_select_fusion, s32[28]{0:T(128)S(1)} %compare_select_fusion.1, f32[]{:T(128)} %bitcast.37, f32[]{:T(128)} %bitcast.36, ...), kind=kLoop, calls=%fused_computation.106 | loop fusion | flops 35840 | bytes 18380 | tf_op jit(solution)/shard_map/jit(_where)/select_n | solution.py:213
  86.8 0.7 multiply_select_fusion
  87.5 0.0 copy-start.25
  87.5 0.6 fusion.71
  88.2 1.0 fusion.23
  89.3 1.1 fusion.14
  90.3 0.4 fusion.32
  90.8 0.1 pad_maximum_fusion.2
  90.9 1.6 %copy-done = f32[32,128,256]{2,1,0:T(8,128)S(1)} copy-done((f32[32,128,256]{2,1,0:T(8,128)S(1)}, f32[32,128,256]{2,1,0:T(8,128)}, u32[]{:S(2)}) %copy-start) | copy-done | bytes 4194328
  92.5 0.2 copy-done.6
  92.7 0.2 copy-done.7
  92.9 0.1 copy-done.9
  92.9 0.1 copy-done.10
  93.0 0.0 copy-start.8
  93.0 1.1 maximum_maximum_fusion
  94.2 0.1 constant_dynamic-update-slice_fusion
  94.3 0.0 copy-start.16
  94.3 2.5 %fusion.72 = f32[40,2,72,256]{3,2,1,0:T(8,128)S(1)} fusion(f32[40,2,72,256]{3,2,1,0:T(8,128)S(1)} %bitcast.99, f32[256,256,1,1]{1,0,3,2:T(8,128)S(1)} %copy-done.8), kind=kOutput, calls=%fused_computation.150 | convolution fusion | flops 2264924160 | bytes 12058624 | tf_op jit(solution)/shard_map/dot_general | solution.py:149
  96.8 0.0 copy-start.17
  96.8 4.7 %fusion.4 = f32[40,256,128]{2,1,0:T(8,128)S(1)} fusion(f32[40,2,72,256]{3,2,1,0:T(8,128)S(1)} %fusion.72, f32[72,128]{1,0:T(8,128)S(1)} %copy-done.16), kind=kOutput, calls=%fused_computation.11 | convolution fusion | flops 566231040 | bytes 8228864 | tf_op jit(solution)/shard_map/dot_general | solution.py:149
  101.5 4.7 %add_bitcast_fusion = f32[40,128,256]{1,2,0:T(8,128)S(1)} fusion(f32[40,256,128]{2,1,0:T(8,128)S(1)} %fusion.4, f32[40,2,72,256]{3,2,1,0:T(8,128)S(1)} %fusion.72, f32[72,128]{1,0:T(8,128)S(1)} %copy-done.17), kind=kOutput, calls=%fused_computation.2 | convolution fusion | flops 567541760 | bytes 13471744 | tf_op jit(solution)/shard_map/dot_general | solution.py:149
  106.2 2.3 %fusion.13 = (f32[16,1,128,256]{2,3,0,1:T(8,128)S(1)}, f32[16,1,128,256]{2,3,0,1:T(8,128)S(1)}) fusion(f32[40,128,256]{1,2,0:T(8,128)S(1)} %add_bitcast_fusion), kind=kLoop, calls=%fused_computation.26 | loop fusion | flops 15728640 | bytes 25165824 | tf_op jit(solution)/shard_map/stack | solution.py:184
  108.6 2.3 %pad_maximum_fusion.1 = f32[16,2,128,256]{2,3,0,1:T(8,128)} fusion(f32[16,1,128,256]{2,3,0,1:T(8,128)S(1)} %get-tuple-element.87, f32[16,1,128,256]{2,3,0,1:T(8,128)S(1)} %get-tuple-element.86), kind=kLoop, calls=%fused_computation.8 | loop fusion | flops 1048576 | bytes 8388608 | tf_op jit(solution)/shard_map/stack | solution.py:184
  110.8 5.3 %copy.26 = f32[16,2,128,256]{3,2,1,0:T(8,128)} copy(f32[16,2,128,256]{2,3,0,1:T(8,128)} %pad_maximum_fusion.1) | data formatting | bytes 8388608 | tf_op jit(solution)/shard_map/stack | solution.py:184
  (58 shorter events, 0.3 us)
Async XLA Ops:
  16.7 3.9 %copy-start.1 = (f32[32,128,256]{2,1,0:T(8,128)S(1)}, f32[32,128,256]{2,1,0:T(8,128)}, u32[]{:S(2)}) copy-start(f32[32,128,256]{2,1,0:T(8,128)} %refs_0_.1) | copy-start | bytes 12582916
  16.7 3.9 %copy-start.4 = (f32[32,3,256]{2,1,0:T(4,128)S(1)}, f32[32,3,256]{2,1,0:T(4,128)}, u32[]{:S(2)}) copy-start(f32[32,3,256]{2,1,0:T(4,128)} %get-tuple-element.52) | copy-start | bytes 294916
  16.8 3.9 %copy-start.5 = (f32[32,3,256]{2,1,0:T(4,128)S(1)}, f32[32,3,256]{2,1,0:T(4,128)}, u32[]{:S(2)}) copy-start(f32[32,3,256]{2,1,0:T(4,128)} %get-tuple-element.53) | copy-start | bytes 294916
  21.2 2.5 %copy-start.12 = (f32[134,128]{1,0:T(8,128)S(1)}, f32[134,128]{1,0:T(8,128)}, u32[]{:S(2)}) copy-start(f32[134,128]{1,0:T(8,128)} %constant.75.clone) | copy-start | bytes 205828
  23.7 3.8 %copy-start.29 = (s32[3,7]{1,0:T(4,128)S(1)}, s32[3,7]{1,0:T(4,128)}, u32[]{:S(2)}) copy-start(s32[3,7]{1,0:T(4,128)} %param.22) | copy-start | bytes 256
  23.7 3.8 %copy-start.30 = (f32[16]{0:T(128)S(1)}, f32[16]{0:T(128)}, u32[]{:S(2)}) copy-start(f32[16]{0:T(128)} %param.21) | copy-start | bytes 196
  23.7 9.1 %copy-start.11 = (f32[256,256,1]{1,0,2:T(8,128)S(1)}, f32[256,256,1]{1,0,2:T(8,128)}, u32[]{:S(2)}) copy-start(f32[256,256,1]{1,0,2:T(8,128)} %constant.90) | copy-start | bytes 786436
  38.1 19.4 %copy-start.2 = (f32[16,64,128]{2,1,0:T(8,128)S(1)}, f32[16,64,128]{2,1,0:T(8,128)}, u32[]{:S(2)}) copy-start(f32[16,64,128]{2,1,0:T(8,128)} %slice.454.refs_0_) | copy-start | bytes 1572868
  58.8 0.8 copy-start.15
  59.5 0.8 copy-start.14
  60.4 0.8 copy-start.26
  60.4 6.2 %copy-start.23 = (f32[64,64,1]{1,0,2:T(8,128)S(1)}, f32[64,64,1]{1,0,2:T(8,128)}, u32[]{:S(2)}) copy-start(f32[64,64,1]{1,0,2:T(8,128)} %constant.92) | copy-start | bytes 49156
  61.0 19.5 %copy-start.22 = (f32[64,64,1,1]{1,0,3,2:T(8,128)S(1)}, f32[64,64,1,1]{1,0,3,2:T(8,128)}, u32[]{:S(2)}) copy-start(f32[64,64,1,1]{1,0,3,2:T(8,128)} %constant.93) | copy-start | bytes 49156
  61.0 19.9 %copy-start.28 = (f32[24,40]{1,0:T(8,128)S(1)}, f32[24,40]{1,0:T(8,128)}, u32[]{:S(2)}) copy-start(f32[24,40]{1,0:T(8,128)} %constant.81.clone) | copy-start | bytes 11524
  61.1 20.4 %copy-start.27 = (f32[24,40]{1,0:T(8,128)S(1)}, f32[24,40]{1,0:T(8,128)}, u32[]{:S(2)}) copy-start(f32[24,40]{1,0:T(8,128)} %constant.82.clone) | copy-start | bytes 11524
  67.6 0.7 copy-start.3
  82.3 5.2 %copy-start.13 = (f32[128,128,1,1]{1,0,3,2:T(8,128)S(1)}, f32[128,128,1,1]{1,0,3,2:T(8,128)}, u32[]{:S(2)}) copy-start(f32[128,128,1,1]{1,0,3,2:T(8,128)} %constant.94) | copy-start | bytes 196612
  86.8 1.4 %copy-start.24 = (f32[40,72]{1,0:T(8,128)S(1)}, f32[40,72]{1,0:T(8,128)}, u32[]{:S(2)}) copy-start(f32[40,72]{1,0:T(8,128)} %constant.83.clone) | copy-start | bytes 34564
  87.5 1.7 %copy-start.25 = (f32[40,72]{1,0:T(8,128)S(1)}, f32[40,72]{1,0:T(8,128)}, u32[]{:S(2)}) copy-start(f32[40,72]{1,0:T(8,128)} %constant.84.clone) | copy-start | bytes 34564
  90.3 2.2 %copy-start = (f32[32,128,256]{2,1,0:T(8,128)S(1)}, f32[32,128,256]{2,1,0:T(8,128)}, u32[]{:S(2)}) copy-start(f32[32,128,256]{2,1,0:T(8,128)} %get-tuple-element.126) | copy-start | bytes 12582916
  90.7 2.0 %copy-start.6 = (f32[2,2,2,64,256]{4,3,2,1,0:T(8,128)S(1)}, f32[2,2,2,64,256]{4,3,2,1,0:T(8,128)}, u32[]{:S(2)}) copy-start(f32[2,2,2,64,256]{4,3,2,1,0:T(8,128)} %get-tuple-element.58) | copy-start | bytes 1572868
  90.7 2.1 %copy-start.7 = (f32[2,2,2,64,256]{4,3,2,1,0:T(8,128)S(1)}, f32[2,2,2,64,256]{4,3,2,1,0:T(8,128)}, u32[]{:S(2)}) copy-start(f32[2,2,2,64,256]{4,3,2,1,0:T(8,128)} %get-tuple-element.63) | copy-start | bytes 1572868
  90.7 2.2 %copy-start.9 = (f32[2,16,2,4,256]{4,3,2,1,0:T(4,128)S(1)}, f32[2,16,2,4,256]{4,3,2,1,0:T(4,128)}, u32[]{:S(2)}) copy-start(f32[2,16,2,4,256]{4,3,2,1,0:T(4,128)} %get-tuple-element.60) | copy-start | bytes 786436
  90.7 2.3 %copy-start.10 = (f32[2,16,2,4,256]{4,3,2,1,0:T(4,128)S(1)}, f32[2,16,2,4,256]{4,3,2,1,0:T(4,128)}, u32[]{:S(2)}) copy-start(f32[2,16,2,4,256]{4,3,2,1,0:T(4,128)} %get-tuple-element.61) | copy-start | bytes 786436
  90.8 2.3 %copy-start.18 = (f32[2,2,2,4,256]{4,3,2,1,0:T(4,128)S(1)}, f32[2,2,2,4,256]{4,3,2,1,0:T(4,128)}, u32[]{:S(2)}) copy-start(f32[2,2,2,4,256]{4,3,2,1,0:T(4,128)} %get-tuple-element.57) | copy-start | bytes 98308
  90.8 2.2 %copy-start.19 = (f32[2,2,2,4,256]{4,3,2,1,0:T(4,128)S(1)}, f32[2,2,2,4,256]{4,3,2,1,0:T(4,128)}, u32[]{:S(2)}) copy-start(f32[2,2,2,4,256]{4,3,2,1,0:T(4,128)} %get-tuple-element.59) | copy-start | bytes 98308
  90.8 2.2 %copy-start.20 = (f32[2,2,2,4,256]{4,3,2,1,0:T(4,128)S(1)}, f32[2,2,2,4,256]{4,3,2,1,0:T(4,128)}, u32[]{:S(2)}) copy-start(f32[2,2,2,4,256]{4,3,2,1,0:T(4,128)} %get-tuple-element.62) | copy-start | bytes 98308
  90.8 2.2 %copy-start.21 = (f32[2,2,2,4,256]{4,3,2,1,0:T(4,128)S(1)}, f32[2,2,2,4,256]{4,3,2,1,0:T(4,128)}, u32[]{:S(2)}) copy-start(f32[2,2,2,4,256]{4,3,2,1,0:T(4,128)} %get-tuple-element.64) | copy-start | bytes 98308
  93.0 1.2 %copy-start.8 = (f32[256,256,1,1]{1,0,3,2:T(8,128)S(1)}, f32[256,256,1,1]{1,0,3,2:T(8,128)}, u32[]{:S(2)}) copy-start(f32[256,256,1,1]{1,0,3,2:T(8,128)} %constant.95) | copy-start | bytes 786436
  94.3 2.5 %copy-start.16 = (f32[72,128]{1,0:T(8,128)S(1)}, f32[72,128]{1,0:T(8,128)}, u32[]{:S(2)}) copy-start(f32[72,128]{1,0:T(8,128)} %constant.86.clone) | copy-start | bytes 110596
  96.8 4.7 %copy-start.17 = (f32[72,128]{1,0:T(8,128)S(1)}, f32[72,128]{1,0:T(8,128)}, u32[]{:S(2)}) copy-start(f32[72,128]{1,0:T(8,128)} %constant.85.clone) | copy-start | bytes 110596
